TPU v7x, 32 devices: a whole 2x2x4 slice. The times are simulated.
32 devices in a mesh: seq: 4 (over x, core), fsdp: 8 (over z, y).
Axes of the slice: x: 2, y: 2, z: 4, core: 2. Of those that a mesh axis runs over, the one named last changes fastest.
Arguments:
- hidden_states: bfloat16 [16, 1024, 1536], P('fsdp', 'seq'), may hold values from -15 to 15
- text_states: bfloat16 [16, 64, 1536], P('fsdp'), may hold values from -6 to 6
- self_gain: bfloat16 [1536], P('fsdp'), may hold values from 0.5 to 1.5
- self_bias: bfloat16 [1536], P('fsdp'), may hold values from -3 to 3
- query_key_value: bfloat16 [1536, 4608], P('fsdp'), may hold values from -0.15625 to 0.15625
- self_output: bfloat16 [1536, 1536], P('fsdp'), may hold values from -2.5 to 2.5
- cross_gain: bfloat16 [1536], P('fsdp'), may hold values from 0.5 to 1.5
- cross_bias: bfloat16 [1536], P('fsdp'), may hold values from -3 to 3
- cross_query: bfloat16 [1536, 1536], P('fsdp'), may hold values from -0.15625 to 0.15625
- cross_memory: bfloat16 [1536, 3072], P('fsdp'), may hold values from -0.15625 to 0.15625
- cross_output: bfloat16 [1536, 1536], P('fsdp'), may hold values from -0.875 to 0.875
- final_gain: bfloat16 [1536], P('fsdp'), may hold values from 0.5 to 1.5
- final_bias: bfloat16 [1536], P('fsdp'), may hold values from -3 to 3
- expand_weight: bfloat16 [1536, 6144], P('fsdp'), may hold values from -0.15625 to 0.15625
- contract_weight: bfloat16 [6144, 1536], P('fsdp'), may hold values from -0.109375 to 0.109375
- output_cotangent: bfloat16 [16, 1024, 1536], P('fsdp', 'seq'), may hold values from -6 to 6
Outputs:
- block_output: bfloat16 [16, 1024, 1536], P('fsdp', 'seq')
- hidden_gradient: float32 [16, 1024, 1536], P('fsdp', 'seq')
- self_gain_gradient: float32 [1536], P('fsdp')
- self_bias_gradient: float32 [1536], P('fsdp')
- qkv_gradient: float32 [1536, 4608], P('fsdp')
- self_output_gradient: float32 [1536, 1536], P('fsdp')
- cross_gain_gradient: float32 [1536], P('fsdp')
- cross_bias_gradient: float32 [1536], P('fsdp')
- cross_query_gradient: float32 [1536, 1536], P('fsdp')
- cross_memory_gradient: float32 [1536, 3072], P('fsdp')
- cross_output_gradient: float32 [1536, 1536], P('fsdp')
- final_gain_gradient: float32 [1536], P('fsdp')
- final_bias_gradient: float32 [1536], P('fsdp')
- expand_gradient: float32 [1536, 6144], P('fsdp')
- contract_gradient: float32 [6144, 1536], P('fsdp')
- layer_rms: float32 [4], replicated
All inputs are finite; a program needn't handle non-finite values.
Results may differ from a plain program's by a relative error of at most 0.023.
Values may be sent and summed in bfloat16 or wider, within the bound.
A program may use at most 320 MiB of HBM per device.

v0:
```python
import jax
import jax.numpy as jnp
from jax import lax
from jax.sharding import PartitionSpec as P

H = 24
HD = 64
TEXT = 64


NEGATIVE = -1e30


def layer_norm(values, gain, offset):
    center = values - jnp.mean(values, axis=-1, keepdims=True)
    spread = jnp.mean(center * center, axis=-1, keepdims=True)
    return center * lax.rsqrt(spread + 1e-05) * gain + offset


def gelu_exact(values):
    return jax.nn.gelu(values, approximate=False)


def product(left, right):
    return jnp.dot(left, right, preferred_element_type=jnp.float32)


def product_left(left, right):
    return lax.dot_general(
        left, right, (((0,), (0,)), ((), ())), preferred_element_type=jnp.float32
    )


def product_right(left, right):
    return lax.dot_general(
        left, right, (((1,), (1,)), ((), ())), preferred_element_type=jnp.float32
    )


def causal_forward(queries, keys, values, rows_block, scale):
    clips, length, heads_local, head_width = queries.shape
    count = length // rows_block
    columns = jnp.arange(length, dtype=jnp.int32)

    def one_block(start):
        block = lax.dynamic_slice_in_dim(queries, start, rows_block, 1)
        scores = (
            jnp.einsum("cqhd,ckhd->chqk", block, keys, preferred_element_type=jnp.float32) * scale
        )
        positions = start + jnp.arange(rows_block, dtype=jnp.int32)
        allowed = columns[None, :] <= positions[:, None]
        scores = jnp.where(allowed, scores, NEGATIVE)
        highest = jnp.max(scores, axis=-1, keepdims=True)
        raised = jnp.exp(scores - highest)
        summed = jnp.sum(raised, axis=-1, keepdims=True)
        weights = (raised / summed).astype(jnp.bfloat16)
        result = jnp.einsum("chqk,ckhd->cqhd", weights, values, preferred_element_type=jnp.float32)
        return (result.astype(jnp.bfloat16), (highest + jnp.log(summed))[..., 0])

    starts = jnp.arange(count, dtype=jnp.int32) * rows_block
    results, logsum = lax.map(one_block, starts)
    results = jnp.moveaxis(results, 0, 1).reshape(clips, length, heads_local * head_width)
    return (results, logsum)


def causal_backward(queries, keys, values, logsum, grad_heads, rows_block, scale):
    clips, length, heads_local, head_width = queries.shape
    count = length // rows_block
    columns = jnp.arange(length, dtype=jnp.int32)
    starts = jnp.arange(count, dtype=jnp.int32) * rows_block

    def one_block(carry, inputs):
        grad_keys, grad_values = carry
        start, block_logsum = inputs
        block = lax.dynamic_slice_in_dim(queries, start, rows_block, 1)
        block_grad = lax.dynamic_slice_in_dim(grad_heads, start, rows_block, 1)
        scores = (
            jnp.einsum("cqhd,ckhd->chqk", block, keys, preferred_element_type=jnp.float32) * scale
        )
        positions = start + jnp.arange(rows_block, dtype=jnp.int32)
        allowed = columns[None, :] <= positions[:, None]
        scores = jnp.where(allowed, scores, NEGATIVE)
        weights = jnp.exp(scores - block_logsum[..., None])
        rounded = weights.astype(jnp.bfloat16)
        grad_weights = jnp.einsum(
            "cqhd,ckhd->chqk", block_grad, values, preferred_element_type=jnp.float32
        )
        inner = jnp.sum(weights * grad_weights, axis=-1, keepdims=True)
        grad_scores = (weights * (grad_weights - inner)).astype(jnp.bfloat16)
        grad_query = (
            jnp.einsum("chqk,ckhd->cqhd", grad_scores, keys, preferred_element_type=jnp.float32)
            * scale
        )
        grad_keys = (
            grad_keys
            + jnp.einsum("chqk,cqhd->ckhd", grad_scores, block, preferred_element_type=jnp.float32)
            * scale
        )
        grad_values = grad_values + jnp.einsum(
            "chqk,cqhd->ckhd", rounded, block_grad, preferred_element_type=jnp.float32
        )
        return ((grad_keys, grad_values), grad_query.astype(jnp.bfloat16))

    zeros = jnp.zeros(queries.shape, jnp.float32)
    (grad_keys, grad_values), grad_queries = lax.scan(one_block, (zeros, zeros), (starts, logsum))
    local_width = heads_local * head_width
    grad_queries = jnp.moveaxis(grad_queries, 0, 1).reshape(clips, length, local_width)
    grad_keys = grad_keys.astype(jnp.bfloat16).reshape(clips, length, local_width)
    grad_values = grad_values.astype(jnp.bfloat16).reshape(clips, length, local_width)
    return jnp.stack([grad_queries, grad_keys, grad_values], axis=2)


def on_device(
    hidden_states,
    text_states,
    self_gain,
    self_bias,
    query_key_value,
    self_output,
    cross_gain,
    cross_bias,
    cross_query,
    cross_memory,
    cross_output,
    final_gain,
    final_bias,
    expand_weight,
    contract_weight,
    output_cotangent,
):
    clips, frames, width = hidden_states.shape
    rows = clips * frames
    groups = lax.axis_size("seq")
    fsdp_count = lax.axis_size("fsdp")
    heads_local = H // groups
    length = frames * groups
    rows_block = min(512, length)
    scale = HD ** (-0.5)
    entries = rows * groups * fsdp_count * width
    self_set = (
        lax.all_gather(self_gain, "fsdp", axis=0, tiled=True),
        lax.all_gather(self_bias, "fsdp", axis=0, tiled=True),
        lax.all_gather(query_key_value, "fsdp", axis=0, tiled=True),
        lax.all_gather(self_output, "fsdp", axis=0, tiled=True),
    )
    hidden = hidden_states.reshape(rows, width).astype(jnp.float32)
    normed_one, norm_one_back = jax.vjp(
        layer_norm, hidden, self_set[0].astype(jnp.float32), self_set[1].astype(jnp.float32)
    )
    normed_one = normed_one.astype(jnp.bfloat16)
    projected = (
        product(normed_one, self_set[2]).astype(jnp.bfloat16).reshape(clips, frames, 3, width)
    )
    regrouped = lax.all_to_all(projected, "seq", split_axis=3, concat_axis=1, tiled=True)
    regrouped = regrouped.reshape(clips, length, 3, heads_local, HD)
    queries = regrouped[:, :, 0]
    keys = regrouped[:, :, 1]
    values = regrouped[:, :, 2]
    context_heads, logsum = causal_forward(queries, keys, values, rows_block, scale)
    context = lax.all_to_all(context_heads, "seq", split_axis=1, concat_axis=2, tiled=True).reshape(
        rows, width
    )
    attended = product(context, self_set[3])
    first = hidden + attended
    rest_set = (
        lax.all_gather(cross_gain, "fsdp", axis=0, tiled=True),
        lax.all_gather(cross_bias, "fsdp", axis=0, tiled=True),
        lax.all_gather(cross_query, "fsdp", axis=0, tiled=True),
        lax.all_gather(cross_memory, "fsdp", axis=0, tiled=True),
        lax.all_gather(cross_output, "fsdp", axis=0, tiled=True),
        lax.all_gather(final_gain, "fsdp", axis=0, tiled=True),
        lax.all_gather(final_bias, "fsdp", axis=0, tiled=True),
        lax.all_gather(expand_weight, "fsdp", axis=0, tiled=True),
        lax.all_gather(contract_weight, "fsdp", axis=0, tiled=True),
    )
    normed_two, norm_two_back = jax.vjp(
        layer_norm, first, rest_set[0].astype(jnp.float32), rest_set[1].astype(jnp.float32)
    )
    normed_two = normed_two.astype(jnp.bfloat16)
    cross_q = product(normed_two, rest_set[2]).astype(jnp.bfloat16).reshape(clips, frames, H, HD)
    text_rows = text_states.reshape(clips * TEXT, width)
    memory = product(text_rows, rest_set[3]).astype(jnp.bfloat16).reshape(clips, TEXT, 2, H, HD)
    cross_keys = memory[:, :, 0]
    cross_values = memory[:, :, 1]
    cross_scores = (
        jnp.einsum("cqhd,ckhd->chqk", cross_q, cross_keys, preferred_element_type=jnp.float32)
        * scale
    )
    highest = jnp.max(cross_scores, axis=-1, keepdims=True)
    raised = jnp.exp(cross_scores - highest)
    cross_weights = raised / jnp.sum(raised, axis=-1, keepdims=True)
    cross_rounded = cross_weights.astype(jnp.bfloat16)
    cross_context = jnp.einsum(
        "chqk,ckhd->cqhd", cross_rounded, cross_values, preferred_element_type=jnp.float32
    )
    cross_context = cross_context.astype(jnp.bfloat16).reshape(rows, width)
    crossed = product(cross_context, rest_set[4])
    second = first + crossed
    normed_three, norm_three_back = jax.vjp(
        layer_norm, second, rest_set[5].astype(jnp.float32), rest_set[6].astype(jnp.float32)
    )
    normed_three = normed_three.astype(jnp.bfloat16)
    preact = product(normed_three, rest_set[7])
    activated, gelu_back = jax.vjp(gelu_exact, preact)
    activated = activated.astype(jnp.bfloat16)
    mixed = product(activated, rest_set[8])
    output = second + mixed
    squares = jnp.stack(
        [
            jnp.sum(output * output),
            jnp.sum(attended * attended),
            jnp.sum(crossed * crossed),
            jnp.sum(mixed * mixed),
        ]
    )
    square_totals = lax.psum(squares, ("seq", "fsdp"))
    back_rest = (
        lax.all_gather(cross_gain, "fsdp", axis=0, tiled=True),
        lax.all_gather(cross_bias, "fsdp", axis=0, tiled=True),
        lax.all_gather(cross_query, "fsdp", axis=0, tiled=True),
        lax.all_gather(cross_memory, "fsdp", axis=0, tiled=True),
        lax.all_gather(cross_output, "fsdp", axis=0, tiled=True),
        lax.all_gather(final_gain, "fsdp", axis=0, tiled=True),
        lax.all_gather(final_bias, "fsdp", axis=0, tiled=True),
        lax.all_gather(expand_weight, "fsdp", axis=0, tiled=True),
        lax.all_gather(contract_weight, "fsdp", axis=0, tiled=True),
    )
    upstream = output_cotangent.reshape(rows, width).astype(jnp.float32)
    grad_mixed = upstream.astype(jnp.bfloat16)
    contract_term = product_left(activated, grad_mixed)
    grad_activated = product_right(grad_mixed, back_rest[8])
    grad_preact = gelu_back(grad_activated)[0].astype(jnp.bfloat16)
    expand_term = product_left(normed_three, grad_preact)
    grad_normed_three = product_right(grad_preact, back_rest[7])
    grad_second, final_gain_term, final_bias_term = norm_three_back(grad_normed_three)
    grad_second = upstream + grad_second
    grad_crossed = grad_second.astype(jnp.bfloat16)
    cross_output_term = product_left(cross_context, grad_crossed)
    grad_cross_context = (
        product_right(grad_crossed, back_rest[4]).astype(jnp.bfloat16).reshape(clips, frames, H, HD)
    )
    grad_cross_weights = jnp.einsum(
        "cqhd,ckhd->chqk", grad_cross_context, cross_values, preferred_element_type=jnp.float32
    )
    cross_inner = jnp.sum(cross_weights * grad_cross_weights, axis=-1, keepdims=True)
    grad_cross_scores = (cross_weights * (grad_cross_weights - cross_inner)).astype(jnp.bfloat16)
    grad_cross_q = (
        jnp.einsum(
            "chqk,ckhd->cqhd", grad_cross_scores, cross_keys, preferred_element_type=jnp.float32
        )
        * scale
    )
    grad_cross_q = grad_cross_q.astype(jnp.bfloat16).reshape(rows, width)
    grad_cross_keys = (
        jnp.einsum(
            "chqk,cqhd->ckhd", grad_cross_scores, cross_q, preferred_element_type=jnp.float32
        )
        * scale
    )
    grad_cross_values = jnp.einsum(
        "chqk,cqhd->ckhd", cross_rounded, grad_cross_context, preferred_element_type=jnp.float32
    )
    grad_memory = jnp.stack([grad_cross_keys, grad_cross_values], axis=2).reshape(
        clips * TEXT, 2 * width
    )
    memory_term = lax.dot_general(
        text_rows.astype(jnp.float32),
        grad_memory,
        (((0,), (0,)), ((), ())),
        precision=lax.Precision.HIGHEST,
        preferred_element_type=jnp.float32,
    )
    query_term = product_left(normed_two, grad_cross_q)
    grad_normed_two = product_right(grad_cross_q, back_rest[2])
    grad_first, cross_gain_term, cross_bias_term = norm_two_back(grad_normed_two)
    grad_first = grad_second + grad_first
    rest_sums = (
        lax.psum_scatter(
            cross_gain_term.astype(jnp.bfloat16), "fsdp", scatter_dimension=0, tiled=True
        ).astype(jnp.float32),
        lax.psum_scatter(
            cross_bias_term.astype(jnp.bfloat16), "fsdp", scatter_dimension=0, tiled=True
        ).astype(jnp.float32),
        lax.psum_scatter(
            query_term.astype(jnp.bfloat16), "fsdp", scatter_dimension=0, tiled=True
        ).astype(jnp.float32),
        lax.psum_scatter(
            memory_term.astype(jnp.bfloat16), "fsdp", scatter_dimension=0, tiled=True
        ).astype(jnp.float32),
        lax.psum_scatter(
            cross_output_term.astype(jnp.bfloat16), "fsdp", scatter_dimension=0, tiled=True
        ).astype(jnp.float32),
        lax.psum_scatter(
            final_gain_term.astype(jnp.bfloat16), "fsdp", scatter_dimension=0, tiled=True
        ).astype(jnp.float32),
        lax.psum_scatter(
            final_bias_term.astype(jnp.bfloat16), "fsdp", scatter_dimension=0, tiled=True
        ).astype(jnp.float32),
        lax.psum_scatter(
            expand_term.astype(jnp.bfloat16), "fsdp", scatter_dimension=0, tiled=True
        ).astype(jnp.float32),
        lax.psum_scatter(
            contract_term.astype(jnp.bfloat16), "fsdp", scatter_dimension=0, tiled=True
        ).astype(jnp.float32),
    )
    back_self = (
        lax.all_gather(self_gain, "fsdp", axis=0, tiled=True),
        lax.all_gather(self_bias, "fsdp", axis=0, tiled=True),
        lax.all_gather(query_key_value, "fsdp", axis=0, tiled=True),
        lax.all_gather(self_output, "fsdp", axis=0, tiled=True),
    )
    grad_attended = grad_first.astype(jnp.bfloat16)
    self_output_term = product_left(context, grad_attended)
    grad_context = (
        product_right(grad_attended, back_self[3])
        .astype(jnp.bfloat16)
        .reshape(clips, frames, width)
    )
    grad_heads = lax.all_to_all(grad_context, "seq", split_axis=2, concat_axis=1, tiled=True)
    grad_heads = grad_heads.reshape(clips, length, heads_local, HD)
    grad_regrouped = causal_backward(queries, keys, values, logsum, grad_heads, rows_block, scale)
    grad_projected = lax.all_to_all(
        grad_regrouped, "seq", split_axis=1, concat_axis=3, tiled=True
    ).reshape(rows, 3 * width)
    qkv_term = product_left(normed_one, grad_projected)
    grad_normed_one = product_right(grad_projected, back_self[2])
    grad_hidden, gain_one_term, bias_one_term = norm_one_back(grad_normed_one)
    grad_hidden = grad_first + grad_hidden
    self_sums = (
        lax.psum_scatter(
            gain_one_term.astype(jnp.bfloat16), "fsdp", scatter_dimension=0, tiled=True
        ).astype(jnp.float32),
        lax.psum_scatter(
            bias_one_term.astype(jnp.bfloat16), "fsdp", scatter_dimension=0, tiled=True
        ).astype(jnp.float32),
        lax.psum_scatter(
            qkv_term.astype(jnp.bfloat16), "fsdp", scatter_dimension=0, tiled=True
        ).astype(jnp.float32),
        lax.psum_scatter(
            self_output_term.astype(jnp.bfloat16), "fsdp", scatter_dimension=0, tiled=True
        ).astype(jnp.float32),
    )
    finals = (
        lax.psum(self_sums[0].astype(jnp.bfloat16), "seq").astype(jnp.float32),
        lax.psum(self_sums[1].astype(jnp.bfloat16), "seq").astype(jnp.float32),
        lax.psum(self_sums[2].astype(jnp.bfloat16), "seq").astype(jnp.float32),
        lax.psum(self_sums[3].astype(jnp.bfloat16), "seq").astype(jnp.float32),
        lax.psum(rest_sums[0].astype(jnp.bfloat16), "seq").astype(jnp.float32),
        lax.psum(rest_sums[1].astype(jnp.bfloat16), "seq").astype(jnp.float32),
        lax.psum(rest_sums[2].astype(jnp.bfloat16), "seq").astype(jnp.float32),
        lax.psum(rest_sums[3].astype(jnp.bfloat16), "seq").astype(jnp.float32),
        lax.psum(rest_sums[4].astype(jnp.bfloat16), "seq").astype(jnp.float32),
        lax.psum(rest_sums[5].astype(jnp.bfloat16), "seq").astype(jnp.float32),
        lax.psum(rest_sums[6].astype(jnp.bfloat16), "seq").astype(jnp.float32),
        lax.psum(rest_sums[7].astype(jnp.bfloat16), "seq").astype(jnp.float32),
        lax.psum(rest_sums[8].astype(jnp.bfloat16), "seq").astype(jnp.float32),
    )
    layer_rms = jnp.sqrt(square_totals / entries)
    return (
        output.astype(jnp.bfloat16).reshape(clips, frames, width),
        grad_hidden.reshape(clips, frames, width),
        finals[0],
        finals[1],
        finals[2],
        finals[3],
        finals[4],
        finals[5],
        finals[6],
        finals[7],
        finals[8],
        finals[9],
        finals[10],
        finals[11],
        finals[12],
        layer_rms,
    )


def solution(mesh):
    return jax.shard_map(
        on_device,
        mesh=mesh,
        in_specs=(
            P("fsdp", "seq", None),
            P("fsdp", None, None),
            P("fsdp"),
            P("fsdp"),
            P("fsdp", None),
            P("fsdp", None),
            P("fsdp"),
            P("fsdp"),
            P("fsdp", None),
            P("fsdp", None),
            P("fsdp", None),
            P("fsdp"),
            P("fsdp"),
            P("fsdp", None),
            P("fsdp", None),
            P("fsdp", "seq", None),
        ),
        out_specs=(
            P("fsdp", "seq", None),
            P("fsdp", "seq", None),
            P("fsdp"),
            P("fsdp"),
            P("fsdp", None),
            P("fsdp", None),
            P("fsdp"),
            P("fsdp"),
            P("fsdp", None),
            P("fsdp", None),
            P("fsdp", None),
            P("fsdp"),
            P("fsdp"),
            P("fsdp", None),
            P("fsdp", None),
            P(),
        ),
        check_vma=False,
    )
```

profile of v0, /device:TPU:0, one launch (start us, length us, event | category | flops | bytes accessed | tf_op | source)
XLA Modules:
  0.0 2984.4 jit_solution(15501810035124365257)
XLA Ops:
  14.8 40.7 %all-reduce.13 = (bf16[1536]{0:T(1024)(128)(2,1)S(1)}, bf16[1536]{0:T(1024)(128)(2,1)S(1)}, bf16[1536]{0:T(1024)(128)(2,1)}, bf16[1536]{0:T(1024)(128)(2,1)}, bf...) all-reduce(bf16[1536]{0:T(1024)(128)(2,1)S(1)} %dynamic-update-slice.1, ...), channel_id=1, replica_groups=mesh['seq'=4,'fsdp'=8] {'fsdp'}, use_global_device_ids=true, to_apply=%add.1 | all-reduce | flops 9216 | bytes 36864
  58.6 150.4 %all-gather.8.cloned.1.call-done = bf16[1536,4608]{1,0:T(8,128)(2,1)} async-done(((bf16[192,4608]{1,0:T(8,128)(2,1)}), bf16[1536,4608]{1,0:T(8,128)(2,1)}) %all-gather.8.cloned.1.call-update) | async-done | bytes 14155792 | tf_op jit(solution)/shard_map/all_gather | solution.py:143
  256.9 53.8 %all-to-all-done = bf16[2,256,3,1536]{1,0,2,3:T(2,128)(2,1)} async-done(((bf16[2,256,3,1536]{1,0,2,3:T(2,128)(2,1)}), bf16[2,256,3,1536]{1,0,2,3:T(2,128)(2,1)}, u32[]{:S(2)}, u32[]{:S(2)}) %all-to-all-start) | async-done | bytes 4718624 | tf_op jit(solution)/shard_map/all_to_all | solution.py:154
  333.8 78.0 %while.28 = (s32[]{:T(128)}, bf16[2,2,512,6,64]{2,4,3,1,0:T(8,128)(2,1)}, f32[2,2,6,512]{3,2,1,0:T(8,128)}, s32[2]{0:T(128)S(1)}, bf16[2,1024,6,64]{1,3,2,0:T(8,...) while((s32[]{:T(128)}, ...), condition=%wide.region_5.6_spmd.clone, body=%wide.region_2.5_spmd.clone.sunk | while | flops 1687022080 | bytes 189478112 | solution.py:61
  463.0 44.9 %all-gather.14.cloned.1.call-done = bf16[1536,1536]{1,0:T(8,128)(2,1)} async-done(((bf16[192,1536]{1,0:T(8,128)(2,1)}), bf16[1536,1536]{1,0:T(8,128)(2,1)}) %all-gather.14.cloned.1.call-update) | async-done | bytes 4718608 | tf_op jit(solution)/shard_map/all_gather | solution.py:168
  531.8 56.2 %all-gather.16.cloned.1.call-done = bf16[1536,1536]{1,0:T(8,128)(2,1)} async-done(((bf16[192,1536]{1,0:T(8,128)(2,1)}), bf16[1536,1536]{1,0:T(8,128)(2,1)}) %all-gather.16.cloned.1.call-update) | async-done | bytes 4718608 | tf_op jit(solution)/shard_map/all_gather | solution.py:170
  596.8 353.2 %all-gather.18.cloned.1.call-done = bf16[1536,6144]{1,0:T(8,128)(2,1)} async-done(((bf16[192,6144]{1,0:T(8,128)(2,1)}), bf16[1536,6144]{1,0:T(8,128)(2,1)}) %all-gather.18.cloned.1.call-update) | async-done | bytes 18874384 | tf_op jit(solution)/shard_map/all_gather | solution.py:173
  966.8 347.3 %all-gather.20.cloned.1.call-done = bf16[6144,1536]{1,0:T(8,128)(2,1)} async-done(((bf16[768,1536]{1,0:T(8,128)(2,1)}), bf16[6144,1536]{1,0:T(8,128)(2,1)}) %all-gather.20.cloned.1.call-update) | async-done | bytes 18874384 | tf_op jit(solution)/shard_map/all_gather | solution.py:174
  1314.0 41.1 %add_convert_fusion = (bf16[512,6144]{1,0:T(8,128)(2,1)}, f32[512,6144]{1,0:T(8,128)S(1)}) fusion(f32[512,6144]{1,0:T(8,128)} %fusion.80, bf16[512,1536]{1,0:T(8,128)(2,1)} %bitcast.224, bf16[6144,1536]{1,0:T(8,128)(2,1)} %all-gather.20.cloned.1.call-done), kind=kOutput, calls=%fused_computation.51 | convolution fusion | flops 9890168832 | bytes 51904512 | tf_op jit(solution)/shard_map/dot_general | solution.py:35
  1375.1 19.3 multiply_reduce_fusion.4
  1527.1 183.4 %while.29 = (s32[]{:T(128)}, f32[2,1024,6,64]{1,3,2,0:T(8,128)}, f32[2,1024,6,64]{1,3,2,0:T(8,128)}, bf16[2,2,512,6,64]{2,4,3,1,0:T(8,128)(2,1)}, s32[2]{0:T(128...) while((s32[]{:T(128)}, f32[2,1024,6,64]{1,3,2,0:T(8,128)}, ...), condition=%wide.region_19.20_spmd.clone, body=%wide.region_17.19_spmd.clone.sunk | while | flops 4126140928 | bytes 212251344 | solution.py:105
  1545.2 18.2 multiply_reduce_fusion.14
  1563.4 22.4 multiply_convert_fusion.6
  1635.8 18.3 multiply_reduce_fusion.14
  1654.1 21.9 multiply_convert_fusion.6
  1741.9 53.1 %all-to-all-done.3 = bf16[2,1024,3,384]{3,0,2,1:T(2,128)(2,1)} async-done(((bf16[2,1024,3,384]{3,0,2,1:T(2,128)(2,1)}), bf16[2,1024,3,384]{3,0,2,1:T(2,128)(2,1)}, u32[]{:S(2)}, u32[]{:S(2)}) %all-to-all-start.3) | async-done | bytes 4718624 | tf_op jit(solution)/shard_map/all_to_all | solution.py:322
  1823.9 17.7 convolution_convert_fusion
  1861.7 52.5 %reduce-scatter.12.cloned.1.call-done = bf16[192,1536]{1,0:T(8,128)(2,1)} async-done(((bf16[1536,1536]{1,0:T(8,128)(2,1)}), bf16[192,1536]{1,0:T(8,128)(2,1)}) %reduce-scatter.12.cloned.1.call-update) | async-done | bytes 589840 | tf_op jit(solution)/shard_map/reduce_scatter | solution.py:339
  1914.2 232.5 %reduce-scatter.10.cloned.1.call-done = bf16[192,4608]{1,0:T(8,128)(2,1)} async-done(((bf16[1536,4608]{1,0:T(8,128)(2,1)}), bf16[192,4608]{1,0:T(8,128)(2,1)}) %reduce-scatter.10.cloned.1.call-update) | async-done | bytes 1769488 | tf_op jit(solution)/shard_map/reduce_scatter | solution.py:336
  2146.7 316.4 %reduce-scatter.18.cloned.1.call-done = bf16[192,6144]{1,0:T(8,128)(2,1)} async-done(((bf16[1536,6144]{1,0:T(8,128)(2,1)}), bf16[192,6144]{1,0:T(8,128)(2,1)}) %reduce-scatter.18.cloned.1.call-update) | async-done | bytes 2359312 | tf_op jit(solution)/shard_map/reduce_scatter | solution.py:299
  2463.1 316.3 %reduce-scatter.20.cloned.1.call-done = bf16[768,1536]{1,0:T(8,128)(2,1)} async-done(((bf16[6144,1536]{1,0:T(8,128)(2,1)}), bf16[768,1536]{1,0:T(8,128)(2,1)}) %reduce-scatter.20.cloned.1.call-update) | async-done | bytes 2359312 | tf_op jit(solution)/shard_map/reduce_scatter | solution.py:302
  2782.8 40.6 %psum.111 = f32[4]{0:T(128)S(1)} all-reduce(f32[4]{0:T(128)S(1)} %pad_maximum_fusion.2), channel_id=1, replica_groups=mesh['seq'=4,'fsdp'=8] {'seq','fsdp'}, use_global_device_ids=true, to_apply=%region_58.59 | all-reduce | flops 4 | bytes 32 | tf_op jit(solution)/shard_map/psum | solution.py:216
  2839.3 36.9 %all-reduce.12 = (bf16[1536]{0:T(1024)(128)(2,1)S(1)}, bf16[1536]{0:T(1024)(128)(2,1)S(1)}, bf16[1536]{0:T(1024)(128)(2,1)S(1)}, bf16[1536]{0:T(1024)(128)(2,1)S...) all-reduce(bf16[1536]{0:T(1024)(128)(2,1)S(1)} %get-tuple-element.2, ...), channel_id=2, replica_groups=mesh['seq'=4,'fsdp'=8] {'fsdp'}, use_global_device_ids=true, to_apply=%region_23.24.clone | all-reduce | flops 9216 | bytes 36864
  2891.7 70.1 %all-reduce.18.cloned.1.call-done = (bf16[192,3072]{0,1:T(8,128)(2,1)}, bf16[192,4608]{1,0:T(8,128)(2,1)}, bf16[192,1536]{1,0:T(8,128)(2,1)}, bf16[192,1536]{1,0...) async-done(((bf16[192,3072]{0,1:T(8,128)(2,1)}, bf16[192,4608]{1,0:T(8,128)(2,1)}, bf16[192,1536]{1,0:T(8,128)(2,1)}, ...) | async-done | bytes 9437200 | tf_op jit(solution)/shard_map/psum | solution.py:351
  (410 shorter events, 635.4 us)
Async XLA Ops:
  7.2 423.8 %copy-start = (bf16[2,64,1536]{2,1,0:T(8,128)(2,1)S(1)}, bf16[2,64,1536]{2,1,0:T(8,128)(2,1)}, u32[]{:S(2)}) copy-start(bf16[2,64,1536]{2,1,0:T(8,128)(2,1)} %param.21) | copy-start | bytes 1179652
  7.2 201.9 %all-gather.8.cloned.1.call-start = ((), (), s32[]{:S(2)}) async-start(), calls=%async_computation.11 | async-start | bytes 15925248 | tf_op jit(solution)/shard_map/all_gather | solution.py:143
  7.9 423.1 %all-gather.12.cloned.1.call-start = ((), (), s32[]{:S(2)}) async-start(), calls=%async_computation.13 | async-start | bytes 10616832 | tf_op jit(solution)/shard_map/all_gather | solution.py:169
  8.8 446.3 %all-gather.10.cloned.1.call-start = ((), (), s32[]{:S(2)}) async-start(), calls=%async_computation.12 | async-start | bytes 5308416 | tf_op jit(solution)/shard_map/all_gather | solution.py:144
  9.5 498.4 %all-gather.14.cloned.1.call-start = ((), (), s32[]{:S(2)}) async-start(), calls=%async_computation.14 | async-start | bytes 5308416 | tf_op jit(solution)/shard_map/all_gather | solution.py:168
  10.1 577.9 %all-gather.16.cloned.1.call-start = ((), (), s32[]{:S(2)}) async-start(), calls=%async_computation.15 | async-start | bytes 5308416 | tf_op jit(solution)/shard_map/all_gather | solution.py:170
  10.7 939.3 %all-gather.18.cloned.1.call-start = ((), (), s32[]{:S(2)}) async-start(), calls=%async_computation.16 | async-start | bytes 21233664 | tf_op jit(solution)/shard_map/all_gather | solution.py:173
  11.2 1302.8 %all-gather.20.cloned.1.call-start = ((), (), s32[]{:S(2)}) async-start(), calls=%async_computation.17 | async-start | bytes 21233664 | tf_op jit(solution)/shard_map/all_gather | solution.py:174
  251.8 59.0 %all-to-all-start = ((bf16[2,256,3,1536]{1,0,2,3:T(2,128)(2,1)}), bf16[2,256,3,1536]{1,0,2,3:T(2,128)(2,1)}, u32[]{:S(2)}, u32[]{:S(2)}) async-start(bf16[2,256,3,1536]{1,0,2,3:T(2,128)(2,1)} %copy.87), calls=%async_computation | async-start | bytes 9437184 | tf_op jit(solution)/shard_map/all_to_all | solution.py:154
  426.0 23.7 all-to-all-start.1
  429.7 1429.5 %reduce-scatter.22.cloned.1.call-start = ((), (), s32[]{:S(2)}) async-start(), calls=%async_computation.24 | async-start | bytes 10616832
  430.4 519.6 %copy-start.48 = (f32[1536]{0:T(1024)}, f32[1536]{0:T(1024)S(1)}, u32[]{:S(2)}) copy-start(f32[1536]{0:T(1024)S(1)} %convert_element_type.245) | copy-start | bytes 18436
  595.5 371.2 %copy-start.11 = (f32[512,1536]{1,0:T(8,128)}, f32[512,1536]{1,0:T(8,128)S(1)}, u32[]{:S(2)}) copy-start(f32[512,1536]{1,0:T(8,128)S(1)} %get-tuple-element.318) | copy-start | bytes 9437188
  595.5 371.2 %copy-start.59 = (f32[512]{0:T(512)}, f32[512]{0:T(512)S(1)}, u32[]{:S(2)}) copy-start(f32[512]{0:T(512)S(1)} %broadcast_multiply_fusion) | copy-start | bytes 6148
  596.8 370.0 %copy-start.71 = (f32[512]{0:T(512)}, f32[512]{0:T(512)S(1)}, u32[]{:S(2)}) copy-start(f32[512]{0:T(512)S(1)} %fusion.74) | copy-start | bytes 6148
  1455.2 406.5 %reduce-scatter.14.cloned.1.call-start = ((), (), s32[]{:S(2)}) async-start(), calls=%async_computation.20 | async-start | bytes 5308416 | tf_op jit(solution)/shard_map/reduce_scatter | solution.py:284
  1466.0 395.7 %reduce-scatter.16.cloned.1.call-start = ((), (), s32[]{:S(2)}) async-start(), calls=%async_computation.21 | async-start | bytes 5308416 | tf_op jit(solution)/shard_map/reduce_scatter | solution.py:290
  1493.6 24.6 all-to-all-start.2
  1498.0 416.3 %reduce-scatter.12.cloned.1.call-start = ((), (), s32[]{:S(2)}) async-start(), calls=%async_computation.19 | async-start | bytes 5308416 | tf_op jit(solution)/shard_map/reduce_scatter | solution.py:339
  1736.1 59.0 %all-to-all-start.3 = ((bf16[2,1024,3,384]{3,0,2,1:T(2,128)(2,1)}), bf16[2,1024,3,384]{3,0,2,1:T(2,128)(2,1)}, u32[]{:S(2)}, u32[]{:S(2)}) async-start(bf16[2,1024,3,384]{3,0,2,1:T(2,128)(2,1)} %copy.106), calls=%async_computation.3 | async-start | bytes 9437184 | tf_op jit(solution)/shard_map/all_to_all | solution.py:322
  1741.2 405.5 %reduce-scatter.10.cloned.1.call-start = ((), (), s32[]{:S(2)}) async-start(), calls=%async_computation.18 | async-start | bytes 15925248 | tf_op jit(solution)/shard_map/reduce_scatter | solution.py:336
  1823.2 639.9 %reduce-scatter.18.cloned.1.call-start = ((), (), s32[]{:S(2)}) async-start(), calls=%async_computation.22 | async-start | bytes 21233664 | tf_op jit(solution)/shard_map/reduce_scatter | solution.py:299
  1841.6 937.8 %reduce-scatter.20.cloned.1.call-start = ((), (), s32[]{:S(2)}) async-start(), calls=%async_computation.23 | async-start | bytes 21233664 | tf_op jit(solution)/shard_map/reduce_scatter | solution.py:302
  1859.1 1102.6 %all-reduce.18.cloned.1.call-start = ((), (), s32[]{:S(2)}) async-start(), calls=%async_computation.25 | async-start | bytes 19660800 | tf_op jit(solution)/shard_map/psum | solution.py:351
  (95 other events, 975.9 us)
Sparse Core Ops, SparseCore 0:
  10.2 198.7 all-gather.7
  211.2 136.2 all-gather.11
  349.7 78.0 all-gather.9
  429.8 78.0 all-gather.13
  509.9 78.0 all-gather.15
  589.4 360.5 all-gather.17
  951.5 362.4 all-gather.19
  1455.4 163.4 reduce-scatter.21
  1622.5 94.5 reduce-scatter.13
  1720.5 94.9 reduce-scatter.15
  1819.2 95.0 reduce-scatter.11
  1917.7 228.9 reduce-scatter.9
  2150.6 312.5 reduce-scatter.17
  2466.9 312.5 reduce-scatter.19
  2783.1 178.5 all-reduce.17
where the time goes:
time: 2990 us; the launch traced here: 2980 us
  waiting for transfers between devices  2070 us (69%)
  matrix products  413 us (14%)
  local copies, waits for them, and re-layouts  201 us (7%)
  other arithmetic  128 us (4%)
  blocking collectives  124 us (4%)
    all_gather x1, waiting for transfers between devices, on_device(): lax.all_gather(expand_weight, 'fsdp', axis=0, tiled=True)  353 us
    all_gather x1, waiting for transfers between devices, on_device(): lax.all_gather(contract_weight, 'fsdp', axis=0, tiled=True)  347 us
    reduce_scatter x1, waiting for transfers between devices, on_device(): lax.psum_scatter(expand_term.astype(jnp.bfloat16), 'fsdp', scatter_dimens...  316 us
    reduce_scatter x1, waiting for transfers between devices, on_device(): lax.psum_scatter(contract_term.astype(jnp.bfloat16), 'fsdp', scatter_dime...  316 us
    reduce_scatter x1, waiting for transfers between devices, on_device(): lax.psum_scatter(qkv_term.astype(jnp.bfloat16), 'fsdp', scatter_dimension...  232 us
    all_gather x1, waiting for transfers between devices, on_device(): lax.all_gather(query_key_value, 'fsdp', axis=0, tiled=True)  150 us
    dot_general x6, matrix products, product_right(): lax.dot_general(left, right, (((1,), (1,)), ((), ())), preferred_element_...  86.7 us
    unnamed x2, blocking collectives  77.6 us
  transfers between devices with their start and end apart: 19, of which 14 were waited for; matrix products, arithmetic and copies ran while one was open for 19% of the time, Pallas kernels for 0%

commit v1 on v0

--- a/solution.py
+++ b/solution.py
@@ -1,14 +1,20 @@
+import functools
+
 import jax
 import jax.numpy as jnp
 from jax import lax
+from jax.experimental import pallas as pl
+from jax.experimental.pallas import tpu as pltpu
 from jax.sharding import PartitionSpec as P
 
 H = 24
 HD = 64
 TEXT = 64
 
-
 NEGATIVE = -1e30
+BF16 = jnp.bfloat16
+F32 = jnp.float32
+MESH = pl.DeviceIdType.MESH
 
 
 def layer_norm(values, gain, offset):
@@ -110,7 +116,7 @@
     return jnp.stack([grad_queries, grad_keys, grad_values], axis=2)
 
 
-def on_device(
+def on_any_mesh(
     hidden_states,
     text_states,
     self_gain,
@@ -376,9 +382,694 @@
     )
 
 
+CORE_PAIRS = [(0, 1), (1, 0), (2, 3), (3, 2)]
+X_PAIRS = [(0, 2), (2, 0), (1, 3), (3, 1)]
+Y_PAIRS = [(i, i ^ 1) for i in range(8)]
+Z_SHIFTS = [[(i, (i + 2 * k) % 8) for i in range(8)] for k in (1, 2, 3)]
+
+
+def gather_kernel(plan, has_vectors, *refs):
+    weights = len({entry[0] for entry in plan})
+    inputs = refs[:weights]
+    refs = refs[weights:]
+    if has_vectors:
+        vector_in, refs = refs[0], refs[1:]
+    outputs = refs[:weights]
+    refs = refs[weights:]
+    if has_vectors:
+        vector_out, refs = refs[0], refs[1:]
+    zs_sem, zr_sem, ys_sem, yr_sem, xs_sem, xr_sem, cs_sem, cr_sem, own_sem, vs_sem, vr_sem = refs
+    seq = lax.axis_index("seq")
+    fsdp = lax.axis_index("fsdp")
+    x, c = seq // 2, seq % 2
+    z, y = fsdp // 2, fsdp % 2
+    x_seq = 2 * (1 - x) + c
+    c_seq = 2 * x + 1 - c
+    y_fsdp = 2 * z + 1 - y
+
+    def at_z(k):
+        return 2 * ((z + k) % 4) + y
+
+    barrier = pltpu.get_barrier_semaphore()
+    partners = [(x_seq, fsdp), (c_seq, fsdp), (seq, y_fsdp)] + [(seq, at_z(k)) for k in (1, 2, 3)]
+    if has_vectors:
+        partners += [(seq, 2 * ((z + k) % 4) + 1 - y) for k in (1, 2, 3)]
+    for partner in partners:
+        pl.semaphore_signal(barrier, inc=1, device_id=partner, device_id_type=MESH)
+    pl.semaphore_wait(barrier, len(partners))
+
+    if has_vectors:
+        vector_sends = []
+        for k in range(1, 8):
+            copy = pltpu.make_async_remote_copy(
+                src_ref=vector_in,
+                dst_ref=vector_out.at[fsdp],
+                send_sem=vs_sem.at[k],
+                recv_sem=vr_sem.at[k],
+                device_id=(seq, (fsdp + k) % 8),
+                device_id_type=MESH,
+            )
+            copy.start()
+            vector_sends.append(copy)
+        own = pltpu.make_async_copy(vector_in, vector_out.at[fsdp], vs_sem.at[0])
+        own.start()
+
+    def part(entry):
+        weight, block, column, split = entry
+        first = 2 * c + x if split else 2 * c
+        count = 1 if split else 2
+        return weight, block, pl.ds(column, 1536), pl.ds(first, count)
+
+    def remote(region, send, recv, device):
+        return pltpu.make_async_remote_copy(
+            src_ref=region,
+            dst_ref=region,
+            send_sem=send,
+            recv_sem=recv,
+            device_id=device,
+            device_id_type=MESH,
+        )
+
+    sends = []
+
+    def send(copy):
+        copy.start()
+        sends.append(copy)
+
+    def start_z(i):
+        weight, block, columns, mine = part(plan[i])
+        source = inputs[weight].at[block, mine, :, columns]
+        target = outputs[weight].at[z, y, block, mine, :, columns]
+        for k in (1, 2, 3):
+            copy = pltpu.make_async_remote_copy(
+                src_ref=source,
+                dst_ref=target,
+                send_sem=zs_sem.at[i, k],
+                recv_sem=zr_sem.at[i, k],
+                device_id=(seq, at_z(k)),
+                device_id_type=MESH,
+            )
+            send(copy)
+        pltpu.make_async_copy(source, target, own_sem.at[i]).start()
+
+    def start_y(i):
+        weight, block, columns, mine = part(plan[i])
+        output = outputs[weight]
+        for k in (1, 2, 3):
+            region = output.at[(z + 4 - k) % 4, y, block, mine, :, columns]
+            remote(region, zs_sem.at[i, k], zr_sem.at[i, k], (seq, at_z(k))).wait_recv()
+        source = inputs[weight].at[block, mine, :, columns]
+        target = output.at[z, y, block, mine, :, columns]
+        pltpu.make_async_copy(source, target, own_sem.at[i]).wait()
+        region = output.at[:, y, block, mine, :, columns]
+        send(remote(region, ys_sem.at[i], yr_sem.at[i], (seq, y_fsdp)))
+
+    def start_x(i):
+        weight, block, columns, mine = part(plan[i])
+        output = outputs[weight]
+        region = output.at[:, 1 - y, block, mine, :, columns]
+        remote(region, ys_sem.at[i], yr_sem.at[i], (seq, y_fsdp)).wait_recv()
+        region = output.at[:, :, block, mine, :, columns]
+        if plan[i][3]:
+            send(remote(region, xs_sem.at[i], xr_sem.at[i], (x_seq, fsdp)))
+        send(remote(region, cs_sem.at[i, 0], cr_sem.at[i, 0], (c_seq, fsdp)))
+
+    def start_core(i):
+        if plan[i][3]:
+            weight, block, columns, _ = part(plan[i])
+            region = outputs[weight].at[:, :, block, pl.ds(2 * c + 1 - x, 1), :, columns]
+            remote(region, xs_sem.at[i], xr_sem.at[i], (x_seq, fsdp)).wait_recv()
+            send(remote(region, cs_sem.at[i, 1], cr_sem.at[i, 1], (c_seq, fsdp)))
+
+    def finish(i):
+        weight, block, columns, _ = part(plan[i])
+        other = 2 * (1 - c)
+        output = outputs[weight]
+        if plan[i][3]:
+            for j, quarter in ((0, other + x), (1, other + 1 - x)):
+                region = output.at[:, :, block, pl.ds(quarter, 1), :, columns]
+                remote(region, cs_sem.at[i, j], cr_sem.at[i, j], (c_seq, fsdp)).wait_recv()
+        else:
+            region = output.at[:, :, block, pl.ds(other, 2), :, columns]
+            remote(region, cs_sem.at[i, 0], cr_sem.at[i, 0], (c_seq, fsdp)).wait_recv()
+
+    chunks = len(plan)
+    ahead = 2
+    for i in range(min(ahead, chunks)):
+        start_z(i)
+    for t in range(chunks + 2):
+        if t + ahead < chunks:
+            start_z(t + ahead)
+        if t < chunks:
+            start_y(t)
+        if 0 <= t - 1 < chunks:
+            start_x(t - 1)
+        if 0 <= t - 2 < chunks:
+            start_core(t - 2)
+    for i in range(chunks):
+        finish(i)
+    for copy in sends:
+        copy.wait_send()
+    if has_vectors:
+        own.wait()
+        for k in range(1, 8):
+            vector_sends[k - 1].wait_send()
+            region = vector_out.at[(fsdp + 8 - k) % 8]
+            remote(region, vs_sem.at[k], vr_sem.at[k], (seq, (fsdp + k) % 8)).wait_recv()
+
+
+def gather_plan(shapes):
+    plan = []
+    for weight, (rows, columns) in enumerate(shapes):
+        for block in range(rows // 192):
+            for column in range(0, columns, 1536):
+                plan.append((weight, block, column, len(plan) % 3 != 2))
+    return tuple(plan)
+
+
+def gather_weights(shards, vectors, collective_id):
+    shapes = [shard.shape for shard in shards]
+    plan = gather_plan(shapes)
+    chunks = len(plan)
+    inputs = [shard.reshape(rows // 192, 4, 48, columns) for shard, (rows, columns) in zip(shards, shapes)]
+    out_shapes = [
+        jax.ShapeDtypeStruct((4, 2, rows // 192, 4, 48, columns), BF16) for rows, columns in shapes
+    ]
+    if vectors is not None:
+        inputs.append(vectors)
+        out_shapes.append(jax.ShapeDtypeStruct((8,) + vectors.shape, vectors.dtype))
+    anywhere = pl.BlockSpec(memory_space=pl.ANY)
+    dma = pltpu.SemaphoreType.DMA
+    results = pl.pallas_call(
+        functools.partial(gather_kernel, plan, vectors is not None),
+        out_shape=out_shapes,
+        in_specs=[anywhere] * len(inputs),
+        out_specs=[anywhere] * len(out_shapes),
+        scratch_shapes=[
+            dma((chunks, 4)),
+            dma((chunks, 4)),
+            dma((chunks,)),
+            dma((chunks,)),
+            dma((chunks,)),
+            dma((chunks,)),
+            dma((chunks, 2)),
+            dma((chunks, 2)),
+            dma((chunks,)),
+            dma((8,)),
+            dma((8,)),
+        ],
+        compiler_params=pltpu.CompilerParams(collective_id=collective_id, has_side_effects=True),
+        name="gather_weights",
+    )(*inputs)
+    whole = [result.reshape(8 * rows, columns) for result, (rows, columns) in zip(results, shapes)]
+    return whole, results[-1]
+
+
+def pack_vectors(vectors):
+    stacked = jnp.stack([vector.astype(F32) for vector in vectors])
+    return jnp.pad(stacked, ((0, 8 - stacked.shape[0]), (0, (-stacked.shape[1]) % 128)))
+
+
+def blocks_kernel(left, right, out):
+    out[0] = jnp.dot(left[...], right[...], preferred_element_type=F32).astype(BF16)
+
+
+def product_blocks(left, right, count):
+    rows, depth = left.shape
+    width = right.shape[1] // count
+    return pl.pallas_call(
+        blocks_kernel,
+        grid=(count,),
+        out_shape=jax.ShapeDtypeStruct((count, rows, width), BF16),
+        in_specs=[
+            pl.BlockSpec((rows, depth), lambda i: (0, 0)),
+            pl.BlockSpec((depth, width), lambda i: (0, i)),
+        ],
+        out_specs=pl.BlockSpec((1, rows, width), lambda i: (i, 0, 0)),
+        compiler_params=pltpu.CompilerParams(vmem_limit_bytes=48 << 20),
+        cost_estimate=pl.CostEstimate(
+            flops=2 * rows * depth * width * count,
+            bytes_accessed=2 * (rows * depth + depth * width * count + rows * width * count),
+            transcendentals=0,
+        ),
+        name="product_blocks",
+    )(left, right)
+
+
+QUERIES = 256
+
+
+def both_heads(value):
+    lane = lax.broadcasted_iota(jnp.int32, value.shape, 1)
+    zero = jnp.zeros_like(value)
+    return jnp.where(lane < HD, value, zero), jnp.where(lane < HD, zero, value)
+
+
+def across(left, right):
+    return lax.dot_general(left, right, (((1,), (1,)), ((), ())), preferred_element_type=F32)
+
+
+def down(left, right):
+    return lax.dot_general(left, right, (((0,), (0,)), ((), ())), preferred_element_type=F32)
+
+
+def join_heads(pair):
+    row = lax.broadcasted_iota(jnp.int32, pair[0].shape, 0)
+    return jnp.where(row < HD, pair[0], pair[1])
+
+
+def key_parts(block):
+    return ([(0, block * QUERIES, False)] if block else []) + [
+        (block * QUERIES, (block + 1) * QUERIES, True)
+    ]
+
+
+def masked_scores(keys, queries, diagonal):
+    scores = across(keys, queries)
+    if diagonal:
+        key = lax.broadcasted_iota(jnp.int32, scores.shape, 0)
+        query = lax.broadcasted_iota(jnp.int32, scores.shape, 1)
+        scores = jnp.where(key <= query, scores, NEGATIVE)
+    return scores
+
+
+def attention_kernel(scale, q_ref, k_ref, v_ref, out_ref, logsum_ref):
+    blocks = q_ref.shape[0] * q_ref.shape[2] // QUERIES
+    k = k_ref[:, 0].reshape(-1, 2 * HD)
+    v = v_ref[:, 0].reshape(-1, 2 * HD)
+    for block in range(blocks):
+        rows = slice(block * QUERIES, (block + 1) * QUERIES)
+        queries = both_heads((q_ref[block, 0].astype(F32) * scale).astype(BF16))
+        outs = []
+        for head in range(2):
+            parts = key_parts(block)
+            scores = [masked_scores(k[a:b], queries[head], diagonal) for a, b, diagonal in parts]
+            highest = functools.reduce(
+                jnp.maximum, [jnp.max(part, axis=0, keepdims=True) for part in scores]
+            )
+            raised = [jnp.exp(part - highest) for part in scores]
+            summed = sum(jnp.sum(part, axis=0, keepdims=True) for part in raised)
+            total = sum(
+                down(v[a:b], part.astype(BF16)) for (a, b, _), part in zip(parts, raised)
+            )
+            outs.append(total / summed)
+            logsum_ref[0, 0, head : head + 1, rows] = highest + jnp.log(summed)
+        out_ref[block, 0] = join_heads(outs).T.astype(BF16)
+
+
+def attention(qkv, scale):
+    blocks, clips, frames, width = qkv.shape
+    pairs = width // (3 * 2 * HD)
+    length = blocks * frames
+    spec = lambda offset: pl.BlockSpec(
+        (blocks, 1, frames, 2 * HD), lambda clip, pair: (0, clip, 0, offset + pair)
+    )
+    return pl.pallas_call(
+        functools.partial(attention_kernel, scale),
+        grid=(clips, pairs),
+        out_shape=(
+            jax.ShapeDtypeStruct((blocks, clips, frames, pairs * 2 * HD), BF16),
+            jax.ShapeDtypeStruct((clips, pairs, 2, length), F32),
+        ),
+        in_specs=[spec(0), spec(pairs), spec(2 * pairs)],
+        out_specs=(
+            spec(0),
+            pl.BlockSpec((1, 1, 2, length), lambda clip, pair: (clip, pair, 0, 0)),
+        ),
+        compiler_params=pltpu.CompilerParams(vmem_limit_bytes=48 << 20),
+        cost_estimate=pl.CostEstimate(
+            flops=clips * pairs * 2 * 4 * length * length * 2 * HD,
+            bytes_accessed=4 * clips * pairs * length * 2 * HD * 2,
+            transcendentals=clips * pairs * 2 * length * length,
+        ),
+        name="attention",
+    )(qkv, qkv, qkv)
+
+
+def attention_back_kernel(
+    scale, q_ref, k_ref, v_ref, grad_ref, logsum_ref, out_ref, grad_keys, grad_values
+):
+    blocks = q_ref.shape[0] * q_ref.shape[2] // QUERIES
+    frames = q_ref.shape[2]
+    pair = pl.program_id(1)
+    group = pl.num_programs(1) * 2 * HD
+    k = k_ref[:, 0].reshape(-1, 2 * HD)
+    v = v_ref[:, 0].reshape(-1, 2 * HD)
+
+    def columns(kind):
+        return pl.ds(pl.multiple_of(kind * group + pair * 2 * HD, 2 * HD), 2 * HD)
+
+    for block in range(blocks):
+        rows = slice(block * QUERIES, (block + 1) * QUERIES)
+        queries = both_heads((q_ref[block, 0].astype(F32) * scale).astype(BF16))
+        grads = both_heads(grad_ref[block, 0])
+        parts = key_parts(block)
+        query_grads = []
+        held = [[], []]
+        for head in range(2):
+            logsum = logsum_ref[0, 0, head : head + 1, rows]
+            weights, weighted = [], []
+            for a, b, diagonal in parts:
+                weight = jnp.exp(masked_scores(k[a:b], queries[head], diagonal) - logsum)
+                weights.append(weight)
+                weighted.append(weight * across(v[a:b], grads[head]))
+            inner = sum(jnp.sum(part, axis=0, keepdims=True) for part in weighted)
+            changes = [
+                (term - weight * inner).astype(BF16) for term, weight in zip(weighted, weights)
+            ]
+            query_grads.append(sum(down(k[a:b], part) for (a, b, _), part in zip(parts, changes)))
+            held[head] = [(weight.astype(BF16), change) for weight, change in zip(weights, changes)]
+        out_ref[block, 0, :, columns(0)] = (join_heads(query_grads).T * scale).astype(BF16)
+        for j, (a, b, diagonal) in enumerate(parts):
+            value_term = sum(
+                jnp.dot(held[head][j][0], grads[head], preferred_element_type=F32)
+                for head in range(2)
+            )
+            key_term = sum(
+                jnp.dot(held[head][j][1], queries[head], preferred_element_type=F32)
+                for head in range(2)
+            )
+            if diagonal:
+                grad_values[a:b] = value_term
+                grad_keys[a:b] = key_term
+            else:
+                grad_values[a:b] += value_term
+                grad_keys[a:b] += key_term
+    out_ref[:, 0, :, columns(1)] = grad_keys[...].reshape(-1, frames, 2 * HD).astype(BF16)
+    out_ref[:, 0, :, columns(2)] = grad_values[...].reshape(-1, frames, 2 * HD).astype(BF16)
+
+
+def attention_back(qkv, grad, logsum, scale):
+    blocks, clips, frames, width = qkv.shape
+    pairs = width // (3 * 2 * HD)
+    length = blocks * frames
+    spec = lambda offset: pl.BlockSpec(
+        (blocks, 1, frames, 2 * HD), lambda clip, pair: (0, clip, 0, offset + pair)
+    )
+    return pl.pallas_call(
+        functools.partial(attention_back_kernel, scale),
+        grid=(clips, pairs),
+        out_shape=jax.ShapeDtypeStruct(qkv.shape, BF16),
+        in_specs=[
+            spec(0),
+            spec(pairs),
+            spec(2 * pairs),
+            spec(0),
+            pl.BlockSpec((1, 1, 2, length), lambda clip, pair: (clip, pair, 0, 0)),
+        ],
+        out_specs=pl.BlockSpec((blocks, 1, frames, width), lambda clip, pair: (0, clip, 0, 0)),
+        scratch_shapes=[pltpu.VMEM((length, 2 * HD), F32), pltpu.VMEM((length, 2 * HD), F32)],
+        compiler_params=pltpu.CompilerParams(vmem_limit_bytes=48 << 20),
+        cost_estimate=pl.CostEstimate(
+            flops=clips * pairs * 2 * 10 * length * length * 2 * HD,
+            bytes_accessed=7 * clips * pairs * length * 2 * HD * 2,
+            transcendentals=clips * pairs * 2 * length * length,
+        ),
+        name="attention_back",
+    )(qkv, qkv, qkv, grad, logsum)
+
+
+def spread(left, right, x_first):
+    seq = lax.axis_index("seq")
+    fsdp = lax.axis_index("fsdp")
+    x, c = seq // 2, seq % 2
+    z, y = fsdp // 2, fsdp % 2
+    height, width = left.shape[1], right.shape[1]
+    half, quarter = width // 2, width // 4
+    rows = height // 8
+
+    def add(a, b):
+        return (a.astype(F32) + b.astype(F32)).astype(BF16)
+
+    def columns(value, index, size):
+        return lax.dynamic_slice_in_dim(value, index * size, size, value.ndim - 1)
+
+    def of_y(value, index):
+        return lax.dynamic_index_in_dim(value, index, 1, keepdims=False)
+
+    def by_x(here, there):
+        sent = add(columns(here, 1 - x, quarter), columns(there, 1 - x, quarter))
+        kept = add(columns(here, x, quarter), columns(there, x, quarter))
+        return lax.ppermute(sent, "seq", X_PAIRS), kept
+
+    def by_y(here, there):
+        sent = add(of_y(here, 1 - y), of_y(there, 1 - y))
+        kept = add(of_y(here, y), of_y(there, y))
+        return lax.ppermute(sent, "fsdp", Y_PAIRS), kept
+
+    sent = product_left(left, columns(right, 1 - c, half)).astype(BF16)
+    there = lax.ppermute(sent, "seq", CORE_PAIRS).reshape(4, 2, rows, half)
+    here = product_left(left, columns(right, c, half)).astype(BF16).reshape(4, 2, rows, half)
+    there, here = yield there, here
+    for step in (by_x, by_y) if x_first else (by_y, by_x):
+        there, here = yield step(here, there)
+
+    def of_z(index):
+        return lax.dynamic_index_in_dim(here, index, 0, keepdims=False).astype(
+            F32
+        ) + lax.dynamic_index_in_dim(there, index, 0, keepdims=False).astype(F32)
+
+    parts = [
+        lax.ppermute(of_z((z + k) % 4).astype(BF16), "fsdp", Z_SHIFTS[k - 1]) for k in (1, 2, 3)
+    ]
+    *parts, total = yield *parts, of_z(z)
+    for piece in parts:
+        total = total + piece.astype(F32)
+    total = total.astype(BF16)
+    total, other = yield total, lax.ppermute(total, "seq", X_PAIRS)
+    pair = jnp.where(
+        x == 0, jnp.concatenate([total, other], 1), jnp.concatenate([other, total], 1)
+    )
+    pair, other = yield pair, lax.ppermute(pair, "seq", CORE_PAIRS)
+    result = jnp.where(
+        c == 0, jnp.concatenate([pair, other], 1), jnp.concatenate([other, pair], 1)
+    ).astype(F32)
+    yield (result,)
+
+
+class Sums:
+    def __init__(self):
+        self.steps = {}
+        self.waiting = {}
+
+    def add(self, name, left, right, x_first):
+        self.steps[name] = spread(left, right, x_first)
+        self.waiting[name] = next(self.steps[name])
+
+    def advance(self, names, *anchors):
+        names = [name for name in names if len(self.waiting[name]) > 1]
+        values = [self.waiting[name] for name in names]
+        anchors, values = lax.optimization_barrier((anchors, values))
+        for name, value in zip(names, values):
+            self.waiting[name] = self.steps[name].send(tuple(value))
+        return anchors if len(anchors) > 1 else anchors[0]
+
+    def finish(self):
+        for name in self.steps:
+            while len(self.waiting[name]) > 1:
+                self.waiting[name] = self.steps[name].send(self.waiting[name])
+        return {name: value[0] for name, value in self.waiting.items()}
+
+
+def on_blocks(
+    hidden_states,
+    text_states,
+    self_gain,
+    self_bias,
+    query_key_value,
+    self_output,
+    cross_gain,
+    cross_bias,
+    cross_query,
+    cross_memory,
+    cross_output,
+    final_gain,
+    final_bias,
+    expand_weight,
+    contract_weight,
+    output_cotangent,
+):
+    clips, frames, width = hidden_states.shape
+    rows = clips * frames
+    groups = lax.axis_size("seq")
+    fsdp_count = lax.axis_size("fsdp")
+    scale = HD ** (-0.5)
+    entries = rows * groups * fsdp_count * width
+    group_width = width // groups
+
+    def by_group(value):
+        return value.reshape(-1, 3, groups, group_width).transpose(0, 2, 1, 3).reshape(value.shape)
+
+    def by_kind(value):
+        return value.reshape(-1, groups, 3, group_width).transpose(0, 2, 1, 3).reshape(value.shape)
+
+    gains = (self_gain, self_bias, cross_gain, cross_bias, final_gain, final_bias)
+    early = (by_group(query_key_value), self_output)
+    (qkv_whole, self_output_whole), vectors = gather_weights(early, pack_vectors(gains), 1)
+    qkv_whole, expand_weight = lax.optimization_barrier((qkv_whole, expand_weight))
+    part = expand_weight.shape[0] // groups
+    expand_whole = lax.all_gather(
+        lax.dynamic_slice_in_dim(expand_weight, lax.axis_index("seq") * part, part, 0),
+        ("fsdp", "seq"),
+        axis=0,
+        tiled=True,
+    )
+    vectors = vectors[:, :6, : width // fsdp_count]
+    gains = [vectors[:, i].reshape(width) for i in range(6)]
+
+    hidden = hidden_states.reshape(rows, width).astype(F32)
+    normed_one, norm_one_back = jax.vjp(layer_norm, hidden, gains[0], gains[1])
+    normed_one = normed_one.astype(BF16)
+    projected = product_blocks(normed_one, qkv_whole, groups)
+    regrouped = lax.all_to_all(projected, "seq", split_axis=0, concat_axis=0, tiled=True)
+    regrouped = regrouped.reshape(groups, clips, frames, 3 * group_width)
+    context_heads, logsum = attention(regrouped, scale)
+    context_heads = context_heads.reshape(groups, rows, group_width)
+    context = lax.all_to_all(context_heads, "seq", split_axis=0, concat_axis=0, tiled=True)
+    late = (cross_query, cross_memory, cross_output, contract_weight)
+    context, late = lax.optimization_barrier((context, late))
+    late, _ = gather_weights(late, None, 2)
+    cross_query_whole, cross_memory_whole, cross_output_whole, contract_whole = late
+    context = context.transpose(1, 0, 2).reshape(rows, width)
+    attended = product(context, self_output_whole)
+    first = hidden + attended
+    normed_two, norm_two_back = jax.vjp(layer_norm, first, gains[2], gains[3])
+    normed_two = normed_two.astype(BF16)
+    cross_q = product(normed_two, cross_query_whole).astype(BF16).reshape(clips, frames, H, HD)
+    text_rows = text_states.reshape(clips * TEXT, width)
+    memory = product(text_rows, cross_memory_whole).astype(BF16).reshape(clips, TEXT, 2, H, HD)
+    cross_keys = memory[:, :, 0]
+    cross_values = memory[:, :, 1]
+    cross_scores = (
+        jnp.einsum("cqhd,ckhd->chqk", cross_q, cross_keys, preferred_element_type=F32) * scale
+    )
+    highest = jnp.max(cross_scores, axis=-1, keepdims=True)
+    raised = jnp.exp(cross_scores - highest)
+    cross_weights = raised / jnp.sum(raised, axis=-1, keepdims=True)
+    cross_rounded = cross_weights.astype(BF16)
+    cross_context = jnp.einsum(
+        "chqk,ckhd->cqhd", cross_rounded, cross_values, preferred_element_type=F32
+    )
+    cross_context = cross_context.astype(BF16).reshape(rows, width)
+    crossed = product(cross_context, cross_output_whole)
+    second = first + crossed
+    normed_three, norm_three_back = jax.vjp(layer_norm, second, gains[4], gains[5])
+    normed_three = normed_three.astype(BF16)
+    preact = product(normed_three, expand_whole)
+    activated, gelu_back = jax.vjp(gelu_exact, preact)
+    activated = activated.astype(BF16)
+    upstream = output_cotangent.reshape(rows, width).astype(F32)
+    grad_mixed = output_cotangent.reshape(rows, width)
+    sums = Sums()
+    sums.add("contract", activated, grad_mixed, False)
+    grad_activated = product_right(grad_mixed, contract_whole)
+    grad_preact = gelu_back(grad_activated)[0].astype(BF16)
+    sums.add("expand", normed_three, grad_preact, True)
+    grad_preact, activated = sums.advance(["contract"], grad_preact, activated)
+    mixed = product(activated, contract_whole)
+    output = second + mixed
+    squares = jnp.stack(
+        [
+            jnp.sum(output * output),
+            jnp.sum(attended * attended),
+            jnp.sum(crossed * crossed),
+            jnp.sum(mixed * mixed),
+        ]
+    )
+    output = output.astype(BF16)
+    grad_preact, output, squares = sums.advance(["expand"], grad_preact, output, squares)
+    grad_normed_three = product_right(grad_preact, expand_whole)
+    grad_second, final_gain_term, final_bias_term = norm_three_back(grad_normed_three)
+    grad_second = upstream + grad_second
+    grad_crossed = grad_second.astype(BF16)
+    sums.add("cross_output", cross_context, grad_crossed, False)
+    grad_cross_context = (
+        product_right(grad_crossed, cross_output_whole).astype(BF16).reshape(clips, frames, H, HD)
+    )
+    grad_cross_weights = jnp.einsum(
+        "cqhd,ckhd->chqk", grad_cross_context, cross_values, preferred_element_type=F32
+    )
+    cross_inner = jnp.sum(cross_weights * grad_cross_weights, axis=-1, keepdims=True)
+    grad_cross_scores = (cross_weights * (grad_cross_weights - cross_inner)).astype(BF16)
+    grad_cross_q = (
+        jnp.einsum("chqk,ckhd->cqhd", grad_cross_scores, cross_keys, preferred_element_type=F32)
+        * scale
+    )
+    grad_cross_q = grad_cross_q.astype(BF16).reshape(rows, width)
+    grad_cross_keys = (
+        jnp.einsum("chqk,cqhd->ckhd", grad_cross_scores, cross_q, preferred_element_type=F32)
+        * scale
+    )
+    grad_cross_values = jnp.einsum(
+        "chqk,cqhd->ckhd", cross_rounded, grad_cross_context, preferred_element_type=F32
+    )
+    grad_memory = jnp.stack([grad_cross_keys, grad_cross_values], axis=2).reshape(
+        clips * TEXT, 2 * width
+    )
+    sums.add("cross_query", normed_two, grad_cross_q, True)
+    sums.add("cross_memory", text_rows, grad_memory.astype(BF16), False)
+    grad_normed_two = product_right(grad_cross_q, cross_query_whole)
+    grad_first, cross_gain_term, cross_bias_term = norm_two_back(grad_normed_two)
+    grad_first = grad_second + grad_first
+    grad_attended = grad_first.astype(BF16)
+    sums.add("self_output", context, grad_attended, False)
+    cross_sums = ["cross_output", "cross_query", "cross_memory", "self_output"]
+    grad_context = product_right(grad_attended, self_output_whole).astype(BF16)
+    grad_context = sums.advance(["contract", "expand"] + cross_sums, grad_context)
+    grad_context = grad_context.reshape(rows, groups, group_width).transpose(1, 0, 2)
+    grad_heads = lax.all_to_all(grad_context, "seq", split_axis=0, concat_axis=0, tiled=True)
+    grad_heads = grad_heads.reshape(groups, clips, frames, group_width)
+    grad_regrouped = attention_back(regrouped, grad_heads, logsum, scale)
+    grad_regrouped = sums.advance(["contract", "expand"] + cross_sums, grad_regrouped)
+    grad_regrouped = grad_regrouped.reshape(groups, rows, 3 * group_width)
+    grad_projected = lax.all_to_all(grad_regrouped, "seq", split_axis=0, concat_axis=0, tiled=True)
+    grad_projected = sums.advance(["contract", "expand"] + cross_sums, grad_projected)
+    grad_projected = grad_projected.transpose(1, 0, 2).reshape(rows, 3 * width)
+    sums.add("qkv", normed_one, grad_projected, True)
+    grad_normed_one = product_right(grad_projected, qkv_whole)
+    grad_hidden, gain_one_term, bias_one_term = norm_one_back(grad_normed_one)
+    grad_hidden = grad_first + grad_hidden
+    terms = (
+        gain_one_term,
+        bias_one_term,
+        cross_gain_term,
+        cross_bias_term,
+        final_gain_term,
+        final_bias_term,
+    )
+    totals = lax.psum(jnp.concatenate(terms + (squares,)), ("seq", "fsdp"))
+    square_totals = totals[6 * width :]
+    shard = width // fsdp_count
+    vector_gradients = lax.dynamic_slice_in_dim(
+        totals[: 6 * width].reshape(6, width), lax.axis_index("fsdp") * shard, shard, 1
+    )
+    layer_rms = jnp.sqrt(square_totals / entries)
+    gradients = sums.finish()
+    return (
+        output.reshape(clips, frames, width),
+        grad_hidden.reshape(clips, frames, width),
+        vector_gradients[0],
+        vector_gradients[1],
+        by_kind(gradients["qkv"]),
+        gradients["self_output"],
+        vector_gradients[2],
+        vector_gradients[3],
+        gradients["cross_query"],
+        gradients["cross_memory"],
+        gradients["cross_output"],
+        vector_gradients[4],
+        vector_gradients[5],
+        gradients["expand"],
+        gradients["contract"],
+        layer_rms,
+    )
+
+
 def solution(mesh):
+    shape = dict(mesh.shape)
+    blocks = shape["seq"] == 4 and shape["fsdp"] == 8
     return jax.shard_map(
-        on_device,
+        on_blocks if blocks else on_any_mesh,
         mesh=mesh,
         in_specs=(
             P("fsdp", "seq", None),

time: 2990 us -> 1530 us (0.51)
  waiting for transfers between devices: 2070 us -> 320 us
  Pallas kernels: 0 us -> 412 us
  matrix products: 413 us -> 234 us
  local copies, waits for them, and re-layouts: 201 us -> 100 us
  starting transfers between devices: 19.1 us -> 101 us
  blocking collectives: 124 us -> 181 us
    all_gather x7 -> x1, waiting for transfers between devices: 952 us -> 0.02 us  [on_blocks(): lax.all_gather(lax.dynamic_slice_in_dim(expand_weight, lax.axis_index('se...]
    reduce_scatter x6 -> x0, waiting for transfers between devices: 918 us -> none  [the longest x1 316 us: on_device(): lax.psum_scatter(expand_term.astype(jnp.bfloat16), 'fsdp', scatter_dimens...]
    pallas_call x0 -> x5, Pallas kernels: none -> 412 us  [the longest x2 346 us: gather_weights(): pl.pallas_call(functools.partial(gather_kernel, plan, vectors is not None...]
    ppermute x0 -> x56, waiting for transfers between devices: none -> 300 us  [the longest x7 149 us: by_y(): return (lax.ppermute(sent, 'fsdp', Y_PAIRS), kept)]
    dot_general x21 -> x6, matrix products: 188 us -> 6.15 us  [the longest x1 3.27 us: on_blocks(): jnp.einsum('cqhd,ckhd->chqk', grad_cross_context, cross_values, preferred...]
    all_to_all x4 -> x3, waiting for transfers between devices: 130 us -> 19.7 us  [the longest x1 19.7 us: on_blocks(): lax.all_to_all(context_heads, 'seq', split_axis=0, concat_axis=0, tiled=T...]
    ppermute x0 -> x56, starting transfers between devices: none -> 87.8 us  [the longest x21 59 us: spread(): lax.ppermute(of_z((z + k) % 4).astype(BF16), 'fsdp', Z_SHIFTS[k - 1])]
    all_to_all x0 -> x1, blocking collectives: none -> 82 us  [on_blocks(): lax.all_to_all(projected, 'seq', split_axis=0, concat_axis=0, tiled=True)]
  transfers between devices with their start and end apart: 19 -> 60, of which waited for: 14 -> 17; matrix products, arithmetic and copies ran while one was open for 19% -> 21% of each run, Pallas kernels for 0% -> 19%
where the time goes in v1:
time: 1530 us; the launch traced here: 1520 us
  Pallas kernels  412 us (27%)
  waiting for transfers between devices  320 us (21%)
  matrix products  234 us (15%)
  blocking collectives  181 us (12%)
  other arithmetic  153 us (10%)
  starting transfers between devices  101 us (7%)
  local copies, waits for them, and re-layouts  100 us (7%)
  between operations  15.9 us (1%)
    pallas_call x2, Pallas kernels, gather_weights(): pl.pallas_call(functools.partial(gather_kernel, plan, vectors is not None...  346 us
    ppermute x7, waiting for transfers between devices, by_y(): return (lax.ppermute(sent, 'fsdp', Y_PAIRS), kept)  149 us
    ppermute x21, waiting for transfers between devices, spread(): lax.ppermute(of_z((z + k) % 4).astype(BF16), 'fsdp', Z_SHIFTS[k - 1])  113 us
    psum x1, blocking collectives, on_blocks(): totals = lax.psum(jnp.concatenate(terms + (squares,)), ('seq', 'fsdp'))  98.8 us
    all_to_all x1, blocking collectives, on_blocks(): lax.all_to_all(projected, 'seq', split_axis=0, concat_axis=0, tiled=True)  82 us
    dot_general x6, matrix products, product(): return jnp.dot(left, right, preferred_element_type=jnp.float32)  81.6 us
    dot_general x14, matrix products, product_left(): lax.dot_general(left, right, (((0,), (0,)), ((), ())), preferred_element_...  78.2 us
    convert_element_type x15, other arithmetic, add(): return (a.astype(F32) + b.astype(F32)).astype(BF16)  75.9 us
  transfers between devices with their start and end apart: 60, of which 17 were waited for; matrix products, arithmetic and copies ran while one was open for 21% of the time, Pallas kernels for 19%

profile of v1, /device:TPU:0, one launch (start us, length us, event | category | flops | bytes accessed | tf_op | source)
XLA Modules:
  0.0 1517.3 jit_solution(1847707062931074631)
XLA Ops:
  21.4 128.6 %gather_weights.2 = (bf16[4,2,1,4,48,4608]{5,4,3,2,1,0:T(8,128)(2,1)}, bf16[4,2,1,4,48,1536]{5,4,3,2,1,0:T(8,128)(2,1)}, f32[8,8,256]{2,1,0:T(8,128)}) custom-call(bf16[1,4,48,4608]{3,2,1,0:T(8,128)(2,1)} %reshape_reshape.3.refs_0_, bf16[1,4,48,1536]{3,2,1,0:T(8,128)(2,1)} %bitcast.384, f32[8,256]{1,0:T(8,128)} %pad_convert_fusion.refs_2_), custom_call_target="tpu_custom_call" | custom-call | tf_op jit(solution)/shard_map/gather_weights/pallas_call | solution.py:563
  155.9 12.9 product_blocks.1
  168.8 82.0 %all_to_all.20 = bf16[4,512,1152]{2,1,0:T(8,128)(2,1)} all-to-all(bf16[4,512,1152]{2,1,0:T(8,128)(2,1)} %product_blocks.1), channel_id=1, replica_groups=mesh['seq'=4,'fsdp'=8] {'seq'}, dimensions={0} | all-to-all | bytes 9437184 | tf_op jit(solution)/shard_map/all_to_all | solution.py:924
  250.8 19.5 %attention.1 = (bf16[4,2,256,384]{3,2,1,0:T(8,128)(2,1)S(1)}, f32[2,3,2,1024]{3,2,1,0:T(2,128)S(1)}) custom-call(bf16[4,2,256,1152]{3,2,1,0:T(8,128)(2,1)} %bitcast.359, bf16[4,2,256,1152]{3,2,1,0:T(8,128)(2,1)} %bitcast.360, bf16[4,2,256,1152]{3,2,1,0:T(8,128)(2,1)} %bitcast.361), custom_call_target="tpu_custom_call" | custom-call | flops 6442450944 | bytes 6291456 | tf_op jit(solution)/shard_map/attention/pallas_call | solution.py:687
  276.3 19.7 %all-to-all-done.1 = bf16[4,512,384]{1,2,0:T(8,128)(2,1)S(1)} async-done(((bf16[4,512,384]{1,2,0:T(8,128)(2,1)}), bf16[4,512,384]{1,2,0:T(8,128)(2,1)S(1)}, u32[]{:S(2)}, u32[]{:S(2)}) %all-to-all-start.1) | async-done | bytes 1572896 | tf_op jit(solution)/shard_map/all_to_all | solution.py:928
  296.0 217.6 %gather_weights.3 = (bf16[4,2,1,4,48,1536]{5,4,3,2,1,0:T(8,128)(2,1)}, bf16[4,2,1,4,48,3072]{5,4,3,2,1,0:T(8,128)(2,1)}, bf16[4,2,1,4,48,1536]{5,4,3,2,1,0:T(8,128)(2,1)}, bf16[4,2,4,4,48,1536]{5,4,3,2,1,0:T(8,128)(2,1)}) custom-call(bf16[1,4,48,1536]{3,2,1,0:T(8,128)(2,1)} %bitcast.382, bf16[1,4,48,3072]{3,2,1,0:T(8,128)(2,1)} %bitcast.381, ...), custom_call_target="tpu_custom_call" | custom-call | tf_op jit(solution)/shard_map/gather_weights/pallas_call | solution.py:563
  568.5 43.1 %multiply_convert_fusion = (bf16[512,6144]{1,0:T(8,128)(2,1)S(1)}, f32[512,6144]{1,0:T(8,128)}, f32[512,6144]{1,0:T(8,128)}) fusion(bf16[1536,6144]{1,0:T(8,128)(2,1)} %all-gather.2.cloned.1.call-done, f32[512,1536]{1,0:T(8,128)} %copy-done.16, f32[1536]{0:T(1024)S(1)} %add.646, f32[1536]{0:T(1024)S(1)} %mul.333, f32[512]{0:T(512)S(1)} %fusion.131, ...), kind=kOutput, calls=%fused_computation.12 | convolution fusion | flops 9872080896 | bytes 53493760 | tf_op jit(solution)/shard_map/dot_general | solution.py:31
  620.0 24.0 %fusion.7 = bf16[512,6144]{1,0:T(8,128)(2,1)} fusion(f32[512,6144]{1,0:T(8,128)} %get-tuple-element.175, f32[512,6144]{1,0:T(8,128)} %get-tuple-element.244, bf16[6144,1536]{1,0:T(8,128)(2,1)} %bitcast.397, bf16[512,1536]{1,0:T(8,128)(2,1)S(1)} %bitcast.341), kind=kOutput, calls=%fused_computation.10 | convolution fusion | flops 9707716608 | bytes 51904512 | tf_op jit(solution)/shard_map/dot_general | solution.py:41
  675.6 15.6 %multiply_reduce_fusion.8 = (f32[]{:T(128)}, f32[]{:T(128)}, bf16[512,1536]{1,0:T(8,128)(2,1)}) fusion(f32[512,1536]{1,0:T(8,128)S(1)} %copy-done.17, bf16[512,6144]{1,0:T(8,128)(2,1)S(1)} %bitcast.412, bf16[6144,1536]{1,0:T(8,128)(2,1)} %bitcast.398), kind=kOutput, calls=%fused_computation.93 | convolution fusion | flops 9668395008 | bytes 29884424 | tf_op jit(solution)/shard_map/dot_general | solution.py:31
  694.3 18.6 %multiply_reduce_fusion = (f32[1536]{0:T(1024)}, f32[512]{0:T(512)S(1)}, f32[1536]{0:T(1024)}, f32[512,1536]{1,0:T(8,128)}) fusion(f32[512,1536]{1,0:T(8,128)} %copy-done.16, f32[512]{0:T(512)S(1)} %fusion.131, f32[512]{0:T(512)S(1)} %broadcast_multiply_fusion, f32[1536]{0:T(1024)S(1)} %mul.333, bf16[512,6144]{1,0:T(8,128)(2,1)} %fusion.7, ...), kind=kOutput, calls=%fused_computation.78 | convolution fusion | flops 9669963776 | bytes 31481856 | tf_op jit(solution)/shard_map/dot_general | solution.py:41
  765.6 12.6 add_convert_fusion
  821.0 40.1 %collective-permute-done.2 = bf16[4,768,768]{2,1,0:T(8,128)(2,1)} collective-permute-done((bf16[4,768,768]{2,1,0:T(8,128)(2,1)}, bf16[4,768,768]{2,1,0:T(8,128)(2,1)}, u32[]{:S(2)}, u32[]{:S(2)}) %collective-permute-start.2) | collective-permute-done | bytes 4718624 | tf_op jit(solution)/shard_map/ppermute | solution.py:818
  861.1 21.5 %collective-permute-done.3 = bf16[4,2,192,1536]{3,2,0,1:T(8,128)(2,1)} collective-permute-done((bf16[4,2,192,1536]{3,2,0,1:T(8,128)(2,1)}, bf16[4,2,192,1536]{3,2,0,1:T(8,128)(2,1)}, u32[]{:S(2)}, u32[]{:S(2)}) %collective-permute-start.3) | collective-permute-done | bytes 4718624 | tf_op jit(solution)/shard_map/ppermute | solution.py:813
  923.1 60.6 %collective-permute-done.10 = bf16[4,192,768]{2,1,0:T(8,128)(2,1)S(1)} collective-permute-done((bf16[4,192,768]{2,1,0:T(8,128)(2,1)S(1)}, bf16[4,192,768]{2,1,0:T(8,128)(2,1)S(1)}, u32[]{:S(2)}, u32[]{:S(2)}) %collective-permute-start.10) | collective-permute-done | bytes 1179680 | tf_op jit(solution)/shard_map/ppermute | solution.py:818
  986.9 33.2 %attention_back.1 = bf16[4,2,256,1152]{3,2,1,0:T(8,128)(2,1)} custom-call(bf16[4,2,256,1152]{3,2,1,0:T(8,128)(2,1)} %bitcast.362, bf16[4,2,256,1152]{3,2,1,0:T(8,128)(2,1)} %bitcast.363, bf16[4,2,256,1152]{3,2,1,0:T(8,128)(2,1)} %bitcast.364, bf16[4,2,256,384]{3,2,1,0:T(8,128)(2,1)S(1)} %bitcast.330, f32[2,3,2,1024]{3,2,1,0:T(2,128)S(1)} %get-tuple-element.108.logsum_ref), custom_call_target="tpu_custom_call" | custom-call | flops 16106127360 | bytes 11010048 | tf_op jit(solution)/shard_map/attention_back/pallas_call | solution.py:769
  1020.1 38.8 %collective-permute-done.13 = bf16[4,192,768]{2,1,0:T(8,128)(2,1)} collective-permute-done((bf16[4,192,768]{2,1,0:T(8,128)(2,1)}, bf16[4,192,768]{2,1,0:T(8,128)(2,1)}, u32[]{:S(2)}, u32[]{:S(2)}) %collective-permute-start.13) | collective-permute-done | bytes 1179680 | tf_op jit(solution)/shard_map/ppermute | solution.py:818
  1109.0 18.1 %collective-permute-done.15 = bf16[768,384]{1,0:T(8,128)(2,1)S(1)} collective-permute-done((bf16[768,384]{1,0:T(8,128)(2,1)}, bf16[768,384]{1,0:T(8,128)(2,1)S(1)}, u32[]{:S(2)}, u32[]{:S(2)}) %collective-permute-start.15) | collective-permute-done | bytes 589856 | tf_op jit(solution)/shard_map/ppermute | solution.py:833
  1140.3 37.2 %collective-permute-done.18 = bf16[192,1536]{1,0:T(8,128)(2,1)S(1)} collective-permute-done((bf16[192,1536]{1,0:T(8,128)(2,1)S(1)}, bf16[192,1536]{1,0:T(8,128)(2,1)S(1)}, u32[]{:S(2)}, u32[]{:S(2)}) %collective-permute-start.18) | collective-permute-done | bytes 589856 | tf_op jit(solution)/shard_map/ppermute | solution.py:833
  1180.0 13.9 collective-permute-done.23
  1218.9 13.0 fusion.137
  1264.2 98.8 %psum.7 = f32[9220]{0:T(1024)} all-reduce(f32[9220]{0:T(1024)S(1)} %constant_dynamic-update-slice_fusion), channel_id=1, replica_groups=mesh['seq'=4,'fsdp'=8] {'seq','fsdp'}, use_global_device_ids=true, to_apply=%region_25.26 | all-reduce | flops 9220 | bytes 73760 | tf_op jit(solution)/shard_map/psum | solution.py:1040
  1377.7 12.2 collective-permute-start.47
  1418.4 12.8 collective-permute-done.43
  1460.5 22.2 %collective-permute-done.28 = bf16[192,1152]{1,0:T(8,128)(2,1)S(1)} collective-permute-done((bf16[192,1152]{1,0:T(8,128)(2,1)S(1)}, bf16[192,1152]{1,0:T(8,128)(2,1)S(1)}, u32[]{:S(2)}, u32[]{:S(2)}) %collective-permute-start.28) | collective-permute-done | bytes 442400 | tf_op jit(solution)/shard_map/ppermute | solution.py:833
  (521 shorter events, 484.7 us)
Async XLA Ops:
  7.2 561.3 %all-gather.2.cloned.1.call-start = ((), (), s32[]{:S(2)}) async-start(), calls=%async_computation.4 | async-start | bytes 19464192 | tf_op jit(solution)/shard_map/all_gather | solution.py:911
  619.6 55.9 %collective-permute-start = (bf16[6144,768]{1,0:T(8,128)(2,1)}, bf16[6144,768]{1,0:T(8,128)(2,1)}, u32[]{:S(2)}, u32[]{:S(2)}) collective-permute-start(bf16[6144,768]{1,0:T(8,128)(2,1)} %convolution_convert_fusion.5), channel_id=1, source_target_pairs={{0,8},{8,0},{16,24},{24,16},{1,9},{9,1},{17,25},{25,17},{2,10},{10... | collective-permute-start | bytes 28311560 | tf_op jit(solution)/shard_map/ppermute | solution.py:821
  756.6 104.5 %collective-permute-start.2 = (bf16[4,768,768]{2,1,0:T(8,128)(2,1)}, bf16[4,768,768]{2,1,0:T(8,128)(2,1)}, u32[]{:S(2)}, u32[]{:S(2)}) collective-permute-start(bf16[4,768,768]{2,1,0:T(8,128)(2,1)} %get-tuple-element.183), channel_id=1, source_target_pairs={{0,1},{1,0},{2,3},{3,2},{4,5},{5,4},{6,7},{7,6},{8,9},{9,8},{10,11... | collective-permute-start | bytes 14155784 | tf_op jit(solution)/shard_map/ppermute | solution.py:818
  778.3 104.3 %collective-permute-start.3 = (bf16[4,2,192,1536]{3,2,0,1:T(8,128)(2,1)}, bf16[4,2,192,1536]{3,2,0,1:T(8,128)(2,1)}, u32[]{:S(2)}, u32[]{:S(2)}) collective-permute-start(bf16[4,2,192,1536]{3,2,0,1:T(8,128)(2,1)} %get-tuple-element.181), channel_id=1, source_target_pairs={{0,16},{16,0},{8,24},{24,8},{1,17},{17,1},{9,25},{25,9},{2,18},{18... | collective-permute-start | bytes 14155784 | tf_op jit(solution)/shard_map/ppermute | solution.py:813
  884.0 102.9 %all-to-all-start.2 = ((bf16[4,512,384]{2,1,0:T(8,128)(2,1)}), bf16[4,512,384]{2,1,0:T(8,128)(2,1)S(1)}, u32[]{:S(2)}, u32[]{:S(2)}) async-start(bf16[4,512,384]{2,1,0:T(8,128)(2,1)} %bitcast.356), calls=%async_computation.2 | async-start | bytes 3145728 | tf_op jit(solution)/shard_map/all_to_all | solution.py:1020
  894.8 164.1 %collective-permute-start.8 = (bf16[4,768,384]{2,1,0:T(8,128)(2,1)}, bf16[4,768,384]{2,1,0:T(8,128)(2,1)}, u32[]{:S(2)}, u32[]{:S(2)}) collective-permute-start(bf16[4,768,384]{2,1,0:T(8,128)(2,1)} %get-tuple-element.189), channel_id=1, source_target_pairs={{0,16},{16,0},{8,24},{24,8},{1,17},{17,1},{9,25},{25,9},{2,18},{18... | collective-permute-start | bytes 7077896 | tf_op jit(solution)/shard_map/ppermute | solution.py:813
  904.2 154.7 %collective-permute-start.9 = (bf16[4,192,1536]{2,1,0:T(8,128)(2,1)}, bf16[4,192,1536]{2,1,0:T(8,128)(2,1)}, u32[]{:S(2)}, u32[]{:S(2)}) collective-permute-start(bf16[4,192,1536]{2,1,0:T(8,128)(2,1)} %get-tuple-element.187), channel_id=1, source_target_pairs={{0,1},{1,0},{2,3},{3,2},{4,5},{5,4},{6,7},{7,6},{8,9},{9,8},{10,11... | collective-permute-start | bytes 7077896 | tf_op jit(solution)/shard_map/ppermute | solution.py:818
  909.4 74.4 %collective-permute-start.10 = (bf16[4,192,768]{2,1,0:T(8,128)(2,1)S(1)}, bf16[4,192,768]{2,1,0:T(8,128)(2,1)S(1)}, u32[]{:S(2)}, u32[]{:S(2)}) collective-permute-start(bf16[4,192,768]{2,1,0:T(8,128)(2,1)S(1)} %get-tuple-element.208), channel_id=1, source_target_pairs={{0,1},{1,0},{2,3},{3,2},{4,5},{5,4},{6,7},{7,6},{8,9},{9,8},{10,11... | collective-permute-start | bytes 3538952 | tf_op jit(solution)/shard_map/ppermute | solution.py:818
  911.6 147.3 %collective-permute-start.12 = (bf16[4,192,1536]{2,1,0:T(8,128)(2,1)}, bf16[4,192,1536]{2,1,0:T(8,128)(2,1)}, u32[]{:S(2)}, u32[]{:S(2)}) collective-permute-start(bf16[4,192,1536]{2,1,0:T(8,128)(2,1)} %fusion.36), channel_id=1, source_target_pairs={{0,1},{1,0},{2,3},{3,2},{4,5},{5,4},{6,7},{7,6},{8,9},{9,8},{10,11... | collective-permute-start | bytes 7077896 | tf_op jit(solution)/shard_map/ppermute | solution.py:818
  917.2 102.8 %collective-permute-start.11 = (bf16[4,2,192,384]{3,2,0,1:T(8,128)(2,1)}, bf16[4,2,192,384]{3,2,0,1:T(8,128)(2,1)S(1)}, u32[]{:S(2)}, u32[]{:S(2)}) collective-permute-start(bf16[4,2,192,384]{3,2,0,1:T(8,128)(2,1)} %get-tuple-element.206), channel_id=1, source_target_pairs={{0,16},{16,0},{8,24},{24,8},{1,17},{17,1},{9,25},{25,9},{2,18},{18... | collective-permute-start | bytes 3538952 | tf_op jit(solution)/shard_map/ppermute | solution.py:813
  984.9 74.0 %collective-permute-start.13 = (bf16[4,192,768]{2,1,0:T(8,128)(2,1)}, bf16[4,192,768]{2,1,0:T(8,128)(2,1)}, u32[]{:S(2)}, u32[]{:S(2)}) collective-permute-start(bf16[4,192,768]{2,1,0:T(8,128)(2,1)} %get-tuple-element.204), channel_id=1, source_target_pairs={{0,1},{1,0},{2,3},{3,2},{4,5},{5,4},{6,7},{7,6},{8,9},{9,8},{10,11... | collective-permute-start | bytes 3538952 | tf_op jit(solution)/shard_map/ppermute | solution.py:818
  1065.5 128.4 %all-to-all-start.3 = ((bf16[4,512,1152]{1,2,0:T(8,128)(2,1)}), bf16[4,512,1152]{1,2,0:T(8,128)(2,1)}, u32[]{:S(2)}, u32[]{:S(2)}) async-start(bf16[4,512,1152]{1,2,0:T(8,128)(2,1)} %copy.156), calls=%async_computation.3 | async-start | bytes 9437184 | tf_op jit(solution)/shard_map/all_to_all | solution.py:1025
  1081.8 45.3 %collective-permute-start.15 = (bf16[768,384]{1,0:T(8,128)(2,1)}, bf16[768,384]{1,0:T(8,128)(2,1)S(1)}, u32[]{:S(2)}, u32[]{:S(2)}) collective-permute-start(bf16[768,384]{1,0:T(8,128)(2,1)} %get-tuple-element.201), channel_id=1, source_target_pairs={{0,4},{1,5},{2,6},{3,7},{4,0},{5,1},{6,2},{7,3},{8,12},{9,13},{10,... | collective-permute-start | bytes 1769480 | tf_op jit(solution)/shard_map/ppermute | solution.py:833
  1087.9 48.6 %collective-permute-start.16 = (bf16[768,384]{1,0:T(8,128)(2,1)}, bf16[768,384]{1,0:T(8,128)(2,1)S(1)}, u32[]{:S(2)}, u32[]{:S(2)}) collective-permute-start(bf16[768,384]{1,0:T(8,128)(2,1)} %get-tuple-element.200), channel_id=1, source_target_pairs={{0,6},{1,7},{2,0},{3,1},{4,2},{5,3},{6,4},{7,5},{8,14},{9,15},{10,... | collective-permute-start | bytes 1769480 | tf_op jit(solution)/shard_map/ppermute | solution.py:833
  1091.5 48.4 %collective-permute-start.17 = (bf16[192,1536]{1,0:T(8,128)(2,1)S(1)}, bf16[192,1536]{1,0:T(8,128)(2,1)S(1)}, u32[]{:S(2)}, u32[]{:S(2)}) collective-permute-start(bf16[192,1536]{1,0:T(8,128)(2,1)S(1)} %get-tuple-element.198), channel_id=1, source_target_pairs={{0,2},{1,3},{2,4},{3,5},{4,6},{5,7},{6,0},{7,1},{8,10},{9,11},{10,... | collective-permute-start | bytes 1769480 | tf_op jit(solution)/shard_map/ppermute | solution.py:833
  1093.4 84.0 %collective-permute-start.18 = (bf16[192,1536]{1,0:T(8,128)(2,1)S(1)}, bf16[192,1536]{1,0:T(8,128)(2,1)S(1)}, u32[]{:S(2)}, u32[]{:S(2)}) collective-permute-start(bf16[192,1536]{1,0:T(8,128)(2,1)S(1)} %get-tuple-element.197), channel_id=1, source_target_pairs={{0,4},{1,5},{2,6},{3,7},{4,0},{5,1},{6,2},{7,3},{8,12},{9,13},{10,... | collective-permute-start | bytes 1769480 | tf_op jit(solution)/shard_map/ppermute | solution.py:833
  1102.0 91.9 %collective-permute-start.22 = (bf16[4,192,768]{2,1,0:T(8,128)(2,1)}, bf16[4,192,768]{2,1,0:T(8,128)(2,1)}, u32[]{:S(2)}, u32[]{:S(2)}) collective-permute-start(bf16[4,192,768]{2,1,0:T(8,128)(2,1)} %get-tuple-element.194), channel_id=1, source_target_pairs={{0,16},{16,0},{8,24},{24,8},{1,17},{17,1},{9,25},{25,9},{2,18},{18... | collective-permute-start | bytes 3538952 | tf_op jit(solution)/shard_map/ppermute | solution.py:813
  1127.1 52.9 %collective-permute-start.19 = (bf16[192,1536]{1,0:T(8,128)(2,1)}, bf16[192,1536]{1,0:T(8,128)(2,1)}, u32[]{:S(2)}, u32[]{:S(2)}) collective-permute-start(bf16[192,1536]{1,0:T(8,128)(2,1)} %get-tuple-element.196), channel_id=1, source_target_pairs={{0,6},{1,7},{2,0},{3,1},{4,2},{5,3},{6,4},{7,5},{8,14},{9,15},{10,... | collective-permute-start | bytes 1769480 | tf_op jit(solution)/shard_map/ppermute | solution.py:833
  1203.6 161.6 %collective-permute-start.34 = (bf16[192,384]{1,0:T(8,128)(2,1)}, bf16[192,384]{1,0:T(8,128)(2,1)}, u32[]{:S(2)}, u32[]{:S(2)}) collective-permute-start(bf16[192,384]{1,0:T(8,128)(2,1)} %get-tuple-element.232), channel_id=1, source_target_pairs={{0,6},{1,7},{2,0},{3,1},{4,2},{5,3},{6,4},{7,5},{8,14},{9,15},{10,... | collective-permute-start | bytes 442376 | tf_op jit(solution)/shard_map/ppermute | solution.py:833
  1212.9 153.1 %collective-permute-start.33 = (bf16[192,384]{1,0:T(8,128)(2,1)}, bf16[192,384]{1,0:T(8,128)(2,1)}, u32[]{:S(2)}, u32[]{:S(2)}) collective-permute-start(bf16[192,384]{1,0:T(8,128)(2,1)} %get-tuple-element.233), channel_id=1, source_target_pairs={{0,4},{1,5},{2,6},{3,7},{4,0},{5,1},{6,2},{7,3},{8,12},{9,13},{10,... | collective-permute-start | bytes 442376 | tf_op jit(solution)/shard_map/ppermute | solution.py:833
  1212.9 155.1 %collective-permute-start.32 = (bf16[192,384]{1,0:T(8,128)(2,1)}, bf16[192,384]{1,0:T(8,128)(2,1)}, u32[]{:S(2)}, u32[]{:S(2)}) collective-permute-start(bf16[192,384]{1,0:T(8,128)(2,1)} %get-tuple-element.231), channel_id=1, source_target_pairs={{0,2},{1,3},{2,4},{3,5},{4,6},{5,7},{6,0},{7,1},{8,10},{9,11},{10,... | collective-permute-start | bytes 442376 | tf_op jit(solution)/shard_map/ppermute | solution.py:833
  1215.6 156.3 %collective-permute-start.39 = (bf16[192,384]{1,0:T(8,128)(2,1)}, bf16[192,384]{1,0:T(8,128)(2,1)}, u32[]{:S(2)}, u32[]{:S(2)}) collective-permute-start(bf16[192,384]{1,0:T(8,128)(2,1)} %get-tuple-element.229), channel_id=1, source_target_pairs={{0,6},{1,7},{2,0},{3,1},{4,2},{5,3},{6,4},{7,5},{8,14},{9,15},{10,... | collective-permute-start | bytes 442376 | tf_op jit(solution)/shard_map/ppermute | solution.py:833
  1251.5 148.7 %collective-permute-start.25 = (bf16[4,2,192,1152]{3,2,1,0:T(8,128)(2,1)}, bf16[4,2,192,1152]{3,2,1,0:T(8,128)(2,1)}, u32[]{:S(2)}, u32[]{:S(2)}) collective-permute-start(bf16[4,2,192,1152]{3,2,1,0:T(8,128)(2,1)} %get-tuple-element.185), channel_id=1, source_target_pairs={{0,16},{16,0},{8,24},{24,8},{1,17},{17,1},{9,25},{25,9},{2,18},{18... | collective-permute-start | bytes 10616840 | tf_op jit(solution)/shard_map/ppermute | solution.py:813
  1368.0 48.6 %collective-permute-start.44 = (bf16[192,768]{1,0:T(8,128)(2,1)}, bf16[192,768]{1,0:T(8,128)(2,1)}, u32[]{:S(2)}, u32[]{:S(2)}) collective-permute-start(bf16[192,768]{1,0:T(8,128)(2,1)} %get-tuple-element.215), channel_id=1, source_target_pairs={{0,6},{1,7},{2,0},{3,1},{4,2},{5,3},{6,4},{7,5},{8,14},{9,15},{10,... | collective-permute-start | bytes 884744 | tf_op jit(solution)/shard_map/ppermute | solution.py:833
  (161 other events, 3599.8 us)
Sparse Core Ops, SparseCore 0:
  151.0 151.4 all-gather.1

commit v2 on v1

--- a/solution.py
+++ b/solution.py
@@ -388,6 +388,9 @@
 Z_SHIFTS = [[(i, (i + 2 * k) % 8) for i in range(8)] for k in (1, 2, 3)]
 
 
+CHUNK = 768
+
+
 def gather_kernel(plan, has_vectors, *refs):
     weights = len({entry[0] for entry in plan})
     inputs = refs[:weights]
@@ -438,7 +441,7 @@
         weight, block, column, split = entry
         first = 2 * c + x if split else 2 * c
         count = 1 if split else 2
-        return weight, block, pl.ds(column, 1536), pl.ds(first, count)
+        return weight, block, pl.ds(column, CHUNK), pl.ds(first, count)
 
     def remote(region, send, recv, device):
         return pltpu.make_async_remote_copy(
@@ -514,7 +517,7 @@
             remote(region, cs_sem.at[i, 0], cr_sem.at[i, 0], (c_seq, fsdp)).wait_recv()
 
     chunks = len(plan)
-    ahead = 2
+    ahead = 3
     for i in range(min(ahead, chunks)):
         start_z(i)
     for t in range(chunks + 2):
@@ -539,12 +542,13 @@
 
 
 def gather_plan(shapes):
-    plan = []
-    for weight, (rows, columns) in enumerate(shapes):
-        for block in range(rows // 192):
-            for column in range(0, columns, 1536):
-                plan.append((weight, block, column, len(plan) % 3 != 2))
-    return tuple(plan)
+    places = [
+        (weight, block, column)
+        for weight, (rows, columns) in enumerate(shapes)
+        for block in range(rows // 192)
+        for column in range(0, columns, CHUNK)
+    ]
+    return tuple(place + ((len(places) - 1 - i) % 3 != 0,) for i, place in enumerate(places))
 
 
 def gather_weights(shards, vectors, collective_id):
@@ -789,86 +793,440 @@
     )(qkv, qkv, qkv, grad, logsum)
 
 
-def spread(left, right, x_first):
+PIECE = (192, 384)
+LAGS = (0, 1, 3, 4, 5, 6, 7)
+
+
+def sum_kernel(plan, weights, *refs):
+    chunks = len(plan)
+    tall = sum(entry[1] for entry in plan)
+    lefts, rights = refs[:weights], refs[weights : 2 * weights]
+    vector_in = refs[2 * weights]
+    outputs = refs[2 * weights + 1 : 3 * weights + 1]
+    vector_out = refs[3 * weights + 1]
+    (
+        mine,
+        c_out,
+        c_in,
+        x_in,
+        y_in,
+        second_in,
+        z_in,
+        total,
+        fx_in,
+        fc_in,
+        wide_stage,
+        tall_stage,
+        left_buf,
+        right_buf,
+        tall_buf,
+        vector,
+        vector_got,
+        vector_z,
+        c_sem,
+        first_sem,
+        second_sem,
+        z_sem,
+        fx_sem,
+        fc_sem,
+        stage_sem,
+        load_sem,
+        vector_sem,
+    ) = refs[3 * weights + 2 :]
     seq = lax.axis_index("seq")
     fsdp = lax.axis_index("fsdp")
     x, c = seq // 2, seq % 2
     z, y = fsdp // 2, fsdp % 2
-    height, width = left.shape[1], right.shape[1]
-    half, quarter = width // 2, width // 4
-    rows = height // 8
-
-    def add(a, b):
-        return (a.astype(F32) + b.astype(F32)).astype(BF16)
-
-    def columns(value, index, size):
-        return lax.dynamic_slice_in_dim(value, index * size, size, value.ndim - 1)
-
-    def of_y(value, index):
-        return lax.dynamic_index_in_dim(value, index, 1, keepdims=False)
-
-    def by_x(here, there):
-        sent = add(columns(here, 1 - x, quarter), columns(there, 1 - x, quarter))
-        kept = add(columns(here, x, quarter), columns(there, x, quarter))
-        return lax.ppermute(sent, "seq", X_PAIRS), kept
-
-    def by_y(here, there):
-        sent = add(of_y(here, 1 - y), of_y(there, 1 - y))
-        kept = add(of_y(here, y), of_y(there, y))
-        return lax.ppermute(sent, "fsdp", Y_PAIRS), kept
-
-    sent = product_left(left, columns(right, 1 - c, half)).astype(BF16)
-    there = lax.ppermute(sent, "seq", CORE_PAIRS).reshape(4, 2, rows, half)
-    here = product_left(left, columns(right, c, half)).astype(BF16).reshape(4, 2, rows, half)
-    there, here = yield there, here
-    for step in (by_x, by_y) if x_first else (by_y, by_x):
-        there, here = yield step(here, there)
-
-    def of_z(index):
-        return lax.dynamic_index_in_dim(here, index, 0, keepdims=False).astype(
-            F32
-        ) + lax.dynamic_index_in_dim(there, index, 0, keepdims=False).astype(F32)
-
-    parts = [
-        lax.ppermute(of_z((z + k) % 4).astype(BF16), "fsdp", Z_SHIFTS[k - 1]) for k in (1, 2, 3)
+    x_device = (2 * (1 - x) + c, fsdp)
+    c_device = (2 * x + 1 - c, fsdp)
+    y_device = (seq, 2 * z + 1 - y)
+
+    def z_device(k):
+        return (seq, 2 * ((z + k) % 4) + y)
+
+    barrier = pltpu.get_barrier_semaphore()
+    partners = [x_device, c_device, y_device] + [z_device(k) for k in (1, 2, 3)]
+    for partner in partners:
+        pl.semaphore_signal(barrier, inc=1, device_id=partner, device_id_type=MESH)
+    pl.semaphore_wait(barrier, len(partners))
+
+    def remote(source, target, sems, device):
+        return pltpu.make_async_remote_copy(
+            src_ref=source,
+            dst_ref=target,
+            send_sem=sems.at[0],
+            recv_sem=sems.at[1],
+            device_id=device,
+            device_id_type=MESH,
+        )
+
+    def x_first(i):
+        return i % 2 == 0
+
+    def loads(j):
+        weight, is_tall, column = plan[j]
+        slot = j % 2
+        if is_tall:
+            copies = [
+                pltpu.make_async_copy(
+                    rights[weight].at[:, pl.ds(column, 384)],
+                    right_buf.at[slot, :, pl.ds(0, 384)],
+                    load_sem.at[1, slot],
+                )
+            ]
+            if j == 0:
+                copies.append(pltpu.make_async_copy(lefts[weight], tall_buf, load_sem.at[2, 0]))
+            return copies
+        return [
+            pltpu.make_async_copy(lefts[weight], left_buf.at[slot], load_sem.at[0, slot]),
+            pltpu.make_async_copy(
+                rights[weight].at[:, pl.ds(column, 1536)], right_buf.at[slot], load_sem.at[1, slot]
+            ),
+        ]
+
+    def start_loads(i):
+        for j in range(chunks):
+
+            @pl.when(i == j)
+            def _():
+                for copy in loads(j):
+                    copy.start()
+
+    def wait_loads(i):
+        for j in range(chunks):
+
+            @pl.when(i == j)
+            def _():
+                for copy in loads(j):
+                    copy.wait()
+
+    def columns(block):
+        return pl.ds(pl.multiple_of(block * 384, 128), 384)
+
+    def multiply(i, half, target, slot):
+        buffer = i % 2
+
+        @pl.when(i >= tall)
+        def _():
+            right = right_buf.at[buffer, :, pl.ds(pl.multiple_of(half * 768, 128), 768)]
+
+            @pl.loop(0, 4)
+            def _(zz):
+                out = down(left_buf[buffer, :, columns(zz)], right[...]).astype(BF16)
+                for q in range(2):
+                    for yy in range(2):
+                        target[slot, q, zz, yy] = out[192 * yy : 192 * yy + 192, 384 * q : 384 * q + 384]
+
+        @pl.when(i < tall)
+        def _():
+            right = right_buf.at[buffer, :, pl.ds(0, 384)]
+
+            @pl.loop(0, 4)
+            def _(zz):
+                for yy in range(2):
+                    left = tall_buf[:, columns((2 * zz + yy) * 2 + half)]
+                    out = down(left, right[...]).astype(BF16)
+                    for q in range(2):
+                        target[slot, q, zz, yy] = out[192 * q : 192 * q + 192]
+
+    def add_to(slot, q, zz, yy, other):
+        here = mine[slot, q, zz, yy].astype(F32)
+        mine[slot, q, zz, yy] = (here + other.astype(F32)).astype(BF16)
+
+    def c_copy(i):
+        return remote(c_out.at[i % 2], c_in.at[i % 2], c_sem.at[:, i % 2], c_device)
+
+    def x_copy(i):
+        slot = i // 2 % 2
+        return remote(mine.at[i % 5, 1 - x], x_in.at[slot], first_sem.at[:, i % 4], x_device)
+
+    def y_copy(i):
+        slot = i // 2 % 2
+        return remote(mine.at[i % 5, :, :, 1 - y], y_in.at[slot], first_sem.at[:, i % 4], y_device)
+
+    def second_y_copy(i):
+        slot = i % 4
+        return remote(mine.at[i % 5, x, :, 1 - y], second_in.at[slot], second_sem.at[:, slot], y_device)
+
+    def second_x_copy(i):
+        slot = i % 4
+        return remote(mine.at[i % 5, 1 - x, :, y], second_in.at[slot], second_sem.at[:, slot], x_device)
+
+    def z_copy(i, k):
+        slot = i % 4
+        return remote(
+            mine.at[i % 5, x, (z + k) % 4, y],
+            z_in.at[slot, k - 1],
+            z_sem.at[:, slot, k - 1],
+            z_device(k),
+        )
+
+    def fx_copy(i):
+        slot = i % 4
+        return remote(total.at[slot], fx_in.at[slot], fx_sem.at[:, slot], x_device)
+
+    def fc_copy(i, which):
+        slot = i % 4
+        source = fx_in.at[slot] if which else total.at[slot]
+        return remote(source, fc_in.at[slot, which], fc_sem.at[:, slot, which], c_device)
+
+    def begin(i):
+        wait_loads(i)
+
+        @pl.when(i >= 2)
+        def _():
+            c_copy(i - 2).wait_send()
+
+        multiply(i, 1 - c, c_out, i % 2)
+        c_copy(i).start()
+        multiply(i, c, mine, i % 5)
+
+    def first(i):
+        slot = i % 5
+        got = i % 2
+        c_copy(i).wait_recv()
+
+        @pl.when(x_first(i))
+        def _():
+            for q, last in ((1 - x, False), (x, True)):
+
+                @pl.loop(0, 4)
+                def _(zz):
+                    for yy in range(2):
+                        add_to(slot, q, zz, yy, c_in[got, q, zz, yy])
+
+                if not last:
+                    x_copy(i).start()
+
+        @pl.when(jnp.logical_not(x_first(i)))
+        def _():
+            for yy, last in ((1 - y, False), (y, True)):
+
+                @pl.loop(0, 4)
+                def _(zz):
+                    for q in range(2):
+                        add_to(slot, q, zz, yy, c_in[got, q, zz, yy])
+
+                if not last:
+                    y_copy(i).start()
+
+    def second(i):
+        slot = i % 5
+        got = i // 2 % 2
+
+        @pl.when(x_first(i))
+        def _():
+            x_copy(i).wait()
+            for yy, last in ((1 - y, False), (y, True)):
+
+                @pl.loop(0, 4)
+                def _(zz):
+                    add_to(slot, x, zz, yy, x_in[got, zz, yy])
+
+                if not last:
+                    second_y_copy(i).start()
+
+        @pl.when(jnp.logical_not(x_first(i)))
+        def _():
+            y_copy(i).wait()
+            for q, last in ((1 - x, False), (x, True)):
+
+                @pl.loop(0, 4)
+                def _(zz):
+                    add_to(slot, q, zz, y, y_in[got, q, zz])
+
+                if not last:
+                    second_x_copy(i).start()
+
+    def third(i):
+        slot = i % 4
+
+        @pl.when(x_first(i))
+        def _():
+            second_y_copy(i).wait()
+
+        @pl.when(jnp.logical_not(x_first(i)))
+        def _():
+            second_x_copy(i).wait()
+
+        for k in (1, 2, 3):
+            zz = (z + k) % 4
+            add_to(i % 5, x, zz, y, second_in[slot, zz])
+            z_copy(i, k).start()
+
+    def put(i, quarter, value):
+        slot = i % 2
+
+        @pl.when(i >= tall)
+        def _():
+            wide_stage[slot, :, columns(quarter)] = value
+
+        @pl.when(i < tall)
+        def _():
+            tall_stage[slot, pl.ds(pl.multiple_of(quarter * 192, 64), 192)] = value
+
+    def fourth(i):
+        slot = i % 4
+        result = mine[i % 5, x, z, y].astype(F32) + second_in[slot, z].astype(F32)
+        for k in (1, 2, 3):
+            z_copy(i, k).wait()
+            result = result + z_in[slot, k - 1].astype(F32)
+        total[slot] = result.astype(BF16)
+        fx_copy(i).start()
+        fc_copy(i, 0).start()
+
+    def fifth(i):
+        fx_copy(i).wait()
+        fc_copy(i, 1).start()
+
+    def store(j):
+        weight, is_tall, column = plan[j]
+        slot = j % 2
+        if is_tall:
+            return pltpu.make_async_copy(
+                tall_stage.at[slot], outputs[weight].at[:, pl.ds(column, 384)], stage_sem.at[0, slot]
+            )
+        return pltpu.make_async_copy(
+            wide_stage.at[slot], outputs[weight].at[:, pl.ds(column, 1536)], stage_sem.at[1, slot]
+        )
+
+    def sixth(i):
+        slot = i % 4
+        for j in range(2, chunks):
+
+            @pl.when(i == j)
+            def _():
+                store(j - 2).wait()
+
+        fc_copy(i, 0).wait()
+        fc_copy(i, 1).wait()
+        put(i, 2 * c + x, total[slot])
+        put(i, 2 * c + 1 - x, fx_in[slot])
+        put(i, 2 * (1 - c) + x, fc_in[slot, 0])
+        put(i, 2 * (1 - c) + 1 - x, fc_in[slot, 1])
+        for j in range(chunks):
+
+            @pl.when(i == j)
+            def _():
+                store(j).start()
+
+    def vector_copy(leg):
+        device = (c_device, x_device, y_device)[leg]
+        return remote(vector.at[leg], vector_got.at[leg], vector_sem.at[:, leg], device)
+
+    def vector_z_copy(k):
+        return remote(vector_z.at[z], vector_z.at[z], vector_sem.at[:, 2 + k], z_device(k))
+
+    def vector_arrival(k):
+        source = (z + 4 - k) % 4
+        return remote(vector_z.at[source], vector_z.at[source], vector_sem.at[:, 2 + k], z_device(k))
+
+    def vector_step(t):
+        @pl.when(t == 0)
+        def _():
+            pltpu.sync_copy(vector_in, vector.at[0])
+            vector_copy(0).start()
+
+        for leg in range(3):
+
+            @pl.when(t == leg + 1)
+            def _():
+                vector_copy(leg).wait()
+                both = vector[leg] + vector_got[leg]
+                if leg < 2:
+                    vector[leg + 1] = both
+                    vector_copy(leg + 1).start()
+                else:
+                    vector_z[z] = both
+                    for k in (1, 2, 3):
+                        vector_z_copy(k).start()
+
+        @pl.when(t == 4)
+        def _():
+            for k in (1, 2, 3):
+                vector_z_copy(k).wait_send()
+                vector_arrival(k).wait_recv()
+            vector[0] = vector_z[0] + vector_z[1] + vector_z[2] + vector_z[3]
+            pltpu.sync_copy(vector.at[0], vector_out)
+
+    start_loads(0)
+
+    @pl.loop(0, chunks + LAGS[-1])
+    def _(t):
+        @pl.when(t + 1 < chunks)
+        def _():
+            start_loads(t + 1)
+
+        stages = (begin, first, second, third, fourth, fifth, sixth)
+        for lag, run in zip(LAGS[::-1], stages[::-1]):
+            i = t - lag
+
+            @pl.when(jnp.logical_and(i >= 0, i < chunks))
+            def _():
+                run(i)
+
+        vector_step(t)
+
+    for j in (chunks - 2, chunks - 1):
+        c_copy(j).wait_send()
+        store(j).wait()
+
+
+def sum_products(products, vectors):
+    lefts = [left for left, _ in products]
+    rights = [right for _, right in products]
+    height, width = lefts[0].shape[1], rights[0].shape[1]
+    plan = [(0, True, column) for column in range(0, width, 384)]
+    for weight in range(1, len(products)):
+        plan += [(weight, False, column) for column in range(0, rights[weight].shape[1], 1536)]
+    out_shapes = [
+        jax.ShapeDtypeStruct((left.shape[1] // 8, right.shape[1]), BF16) for left, right in products
     ]
-    *parts, total = yield *parts, of_z(z)
-    for piece in parts:
-        total = total + piece.astype(F32)
-    total = total.astype(BF16)
-    total, other = yield total, lax.ppermute(total, "seq", X_PAIRS)
-    pair = jnp.where(
-        x == 0, jnp.concatenate([total, other], 1), jnp.concatenate([other, total], 1)
-    )
-    pair, other = yield pair, lax.ppermute(pair, "seq", CORE_PAIRS)
-    result = jnp.where(
-        c == 0, jnp.concatenate([pair, other], 1), jnp.concatenate([other, pair], 1)
-    ).astype(F32)
-    yield (result,)
-
-
-class Sums:
-    def __init__(self):
-        self.steps = {}
-        self.waiting = {}
-
-    def add(self, name, left, right, x_first):
-        self.steps[name] = spread(left, right, x_first)
-        self.waiting[name] = next(self.steps[name])
-
-    def advance(self, names, *anchors):
-        names = [name for name in names if len(self.waiting[name]) > 1]
-        values = [self.waiting[name] for name in names]
-        anchors, values = lax.optimization_barrier((anchors, values))
-        for name, value in zip(names, values):
-            self.waiting[name] = self.steps[name].send(tuple(value))
-        return anchors if len(anchors) > 1 else anchors[0]
-
-    def finish(self):
-        for name in self.steps:
-            while len(self.waiting[name]) > 1:
-                self.waiting[name] = self.steps[name].send(self.waiting[name])
-        return {name: value[0] for name, value in self.waiting.items()}
+    out_shapes.append(jax.ShapeDtypeStruct(vectors.shape, F32))
+    depth = lefts[0].shape[0]
+    anywhere = pl.BlockSpec(memory_space=pl.ANY)
+    dma = pltpu.SemaphoreType.DMA
+    block = lambda *lead: pltpu.VMEM(lead + PIECE, BF16)
+    *sums, total = pl.pallas_call(
+        functools.partial(sum_kernel, tuple(plan), len(products)),
+        out_shape=out_shapes,
+        in_specs=[anywhere] * (2 * len(products) + 1),
+        out_specs=[anywhere] * len(out_shapes),
+        scratch_shapes=[
+            block(5, 2, 4, 2),
+            block(2, 2, 4, 2),
+            block(2, 2, 4, 2),
+            block(2, 4, 2),
+            block(2, 2, 4),
+            block(4, 4),
+            block(4, 3),
+            block(4),
+            block(4),
+            block(4, 2),
+            pltpu.VMEM((2, 192, 1536), BF16),
+            pltpu.VMEM((2, 768, 384), BF16),
+            pltpu.VMEM((2, depth, 1536), BF16),
+            pltpu.VMEM((2, depth, 1536), BF16),
+            pltpu.VMEM((depth, height), BF16),
+            pltpu.VMEM((3,) + vectors.shape, F32),
+            pltpu.VMEM((3,) + vectors.shape, F32),
+            pltpu.VMEM((4,) + vectors.shape, F32),
+            dma((2, 2)),
+            dma((2, 4)),
+            dma((2, 4)),
+            dma((2, 4, 3)),
+            dma((2, 4)),
+            dma((2, 4, 2)),
+            dma((2, 2)),
+            dma((3, 2)),
+            dma((2, 6)),
+        ],
+        compiler_params=pltpu.CompilerParams(
+            collective_id=3, has_side_effects=True, vmem_limit_bytes=60 << 20
+        ),
+        name="sum_products",
+    )(*lefts, *rights, vectors)
+    return sums, total
 
 
 def on_blocks(
@@ -960,12 +1318,47 @@
     activated = activated.astype(BF16)
     upstream = output_cotangent.reshape(rows, width).astype(F32)
     grad_mixed = output_cotangent.reshape(rows, width)
-    sums = Sums()
-    sums.add("contract", activated, grad_mixed, False)
     grad_activated = product_right(grad_mixed, contract_whole)
     grad_preact = gelu_back(grad_activated)[0].astype(BF16)
-    sums.add("expand", normed_three, grad_preact, True)
-    grad_preact, activated = sums.advance(["contract"], grad_preact, activated)
+    grad_normed_three = product_right(grad_preact, expand_whole)
+    grad_second, final_gain_term, final_bias_term = norm_three_back(grad_normed_three)
+    grad_second = upstream + grad_second
+    grad_crossed = grad_second.astype(BF16)
+    grad_cross_context = (
+        product_right(grad_crossed, cross_output_whole).astype(BF16).reshape(clips, frames, H, HD)
+    )
+    grad_cross_weights = jnp.einsum(
+        "cqhd,ckhd->chqk", grad_cross_context, cross_values, preferred_element_type=F32
+    )
+    cross_inner = jnp.sum(cross_weights * grad_cross_weights, axis=-1, keepdims=True)
+    grad_cross_scores = (cross_weights * (grad_cross_weights - cross_inner)).astype(BF16)
+    grad_cross_q = (
+        jnp.einsum("chqk,ckhd->cqhd", grad_cross_scores, cross_keys, preferred_element_type=F32)
+        * scale
+    )
+    grad_cross_q = grad_cross_q.astype(BF16).reshape(rows, width)
+    grad_cross_keys = (
+        jnp.einsum("chqk,cqhd->ckhd", grad_cross_scores, cross_q, preferred_element_type=F32)
+        * scale
+    )
+    grad_cross_values = jnp.einsum(
+        "chqk,cqhd->ckhd", cross_rounded, grad_cross_context, preferred_element_type=F32
+    )
+    grad_memory = jnp.stack([grad_cross_keys, grad_cross_values], axis=2).reshape(
+        clips * TEXT, 2 * width
+    )
+    grad_normed_two = product_right(grad_cross_q, cross_query_whole)
+    grad_first, cross_gain_term, cross_bias_term = norm_two_back(grad_normed_two)
+    grad_first = grad_second + grad_first
+    grad_attended = grad_first.astype(BF16)
+    grad_context = product_right(grad_attended, self_output_whole).astype(BF16)
+    grad_context = grad_context.reshape(rows, groups, group_width).transpose(1, 0, 2)
+    grad_heads = lax.all_to_all(grad_context, "seq", split_axis=0, concat_axis=0, tiled=True)
+    grad_heads = grad_heads.reshape(groups, clips, frames, group_width)
+    grad_regrouped = attention_back(regrouped, grad_heads, logsum, scale)
+    grad_regrouped, activated = lax.optimization_barrier((grad_regrouped, activated))
+    grad_regrouped = grad_regrouped.reshape(groups, rows, 3 * group_width)
+    grad_projected = lax.all_to_all(grad_regrouped, "seq", split_axis=0, concat_axis=0, tiled=True)
     mixed = product(activated, contract_whole)
     output = second + mixed
     squares = jnp.stack(
@@ -977,90 +1370,58 @@
         ]
     )
     output = output.astype(BF16)
-    grad_preact, output, squares = sums.advance(["expand"], grad_preact, output, squares)
-    grad_normed_three = product_right(grad_preact, expand_whole)
-    grad_second, final_gain_term, final_bias_term = norm_three_back(grad_normed_three)
-    grad_second = upstream + grad_second
-    grad_crossed = grad_second.astype(BF16)
-    sums.add("cross_output", cross_context, grad_crossed, False)
-    grad_cross_context = (
-        product_right(grad_crossed, cross_output_whole).astype(BF16).reshape(clips, frames, H, HD)
-    )
-    grad_cross_weights = jnp.einsum(
-        "cqhd,ckhd->chqk", grad_cross_context, cross_values, preferred_element_type=F32
-    )
-    cross_inner = jnp.sum(cross_weights * grad_cross_weights, axis=-1, keepdims=True)
-    grad_cross_scores = (cross_weights * (grad_cross_weights - cross_inner)).astype(BF16)
-    grad_cross_q = (
-        jnp.einsum("chqk,ckhd->cqhd", grad_cross_scores, cross_keys, preferred_element_type=F32)
-        * scale
-    )
-    grad_cross_q = grad_cross_q.astype(BF16).reshape(rows, width)
-    grad_cross_keys = (
-        jnp.einsum("chqk,cqhd->ckhd", grad_cross_scores, cross_q, preferred_element_type=F32)
-        * scale
-    )
-    grad_cross_values = jnp.einsum(
-        "chqk,cqhd->ckhd", cross_rounded, grad_cross_context, preferred_element_type=F32
-    )
-    grad_memory = jnp.stack([grad_cross_keys, grad_cross_values], axis=2).reshape(
-        clips * TEXT, 2 * width
-    )
-    sums.add("cross_query", normed_two, grad_cross_q, True)
-    sums.add("cross_memory", text_rows, grad_memory.astype(BF16), False)
-    grad_normed_two = product_right(grad_cross_q, cross_query_whole)
-    grad_first, cross_gain_term, cross_bias_term = norm_two_back(grad_normed_two)
-    grad_first = grad_second + grad_first
-    grad_attended = grad_first.astype(BF16)
-    sums.add("self_output", context, grad_attended, False)
-    cross_sums = ["cross_output", "cross_query", "cross_memory", "self_output"]
-    grad_context = product_right(grad_attended, self_output_whole).astype(BF16)
-    grad_context = sums.advance(["contract", "expand"] + cross_sums, grad_context)
-    grad_context = grad_context.reshape(rows, groups, group_width).transpose(1, 0, 2)
-    grad_heads = lax.all_to_all(grad_context, "seq", split_axis=0, concat_axis=0, tiled=True)
-    grad_heads = grad_heads.reshape(groups, clips, frames, group_width)
-    grad_regrouped = attention_back(regrouped, grad_heads, logsum, scale)
-    grad_regrouped = sums.advance(["contract", "expand"] + cross_sums, grad_regrouped)
-    grad_regrouped = grad_regrouped.reshape(groups, rows, 3 * group_width)
-    grad_projected = lax.all_to_all(grad_regrouped, "seq", split_axis=0, concat_axis=0, tiled=True)
-    grad_projected = sums.advance(["contract", "expand"] + cross_sums, grad_projected)
+    grad_projected, output, squares = lax.optimization_barrier((grad_projected, output, squares))
     grad_projected = grad_projected.transpose(1, 0, 2).reshape(rows, 3 * width)
-    sums.add("qkv", normed_one, grad_projected, True)
     grad_normed_one = product_right(grad_projected, qkv_whole)
     grad_hidden, gain_one_term, bias_one_term = norm_one_back(grad_normed_one)
     grad_hidden = grad_first + grad_hidden
-    terms = (
-        gain_one_term,
-        bias_one_term,
-        cross_gain_term,
-        cross_bias_term,
-        final_gain_term,
-        final_bias_term,
-    )
-    totals = lax.psum(jnp.concatenate(terms + (squares,)), ("seq", "fsdp"))
-    square_totals = totals[6 * width :]
+    terms = jnp.stack(
+        [
+            gain_one_term,
+            bias_one_term,
+            cross_gain_term,
+            cross_bias_term,
+            final_gain_term,
+            final_bias_term,
+            jnp.pad(squares, (0, width - 4)),
+            jnp.zeros_like(gain_one_term),
+        ]
+    )
+    deep = lambda value: jnp.pad(value, ((0, rows - value.shape[0]), (0, 0)))
+    gradients, totals = sum_products(
+        [
+            (activated, grad_mixed),
+            (normed_three, grad_preact),
+            (cross_context, grad_crossed),
+            (normed_two, grad_cross_q),
+            (deep(text_rows), deep(grad_memory.astype(BF16))),
+            (context, grad_attended),
+            (normed_one, grad_projected),
+        ],
+        terms,
+    )
+    gradients = [gradient.astype(F32) for gradient in gradients]
+    layer_rms = jnp.sqrt(totals[6, :4] / entries)
     shard = width // fsdp_count
     vector_gradients = lax.dynamic_slice_in_dim(
-        totals[: 6 * width].reshape(6, width), lax.axis_index("fsdp") * shard, shard, 1
-    )
-    layer_rms = jnp.sqrt(square_totals / entries)
-    gradients = sums.finish()
+        totals, lax.axis_index("fsdp") * shard, shard, 1
+    )
     return (
         output.reshape(clips, frames, width),
         grad_hidden.reshape(clips, frames, width),
         vector_gradients[0],
         vector_gradients[1],
-        by_kind(gradients["qkv"]),
-        gradients["self_output"],
+        by_kind(gradients[6]),
+        gradients[5],
         vector_gradients[2],
         vector_gradients[3],
-        gradients["cross_query"],
-        gradients["cross_memory"],
-        gradients["cross_output"],
+        gradients[3],
+        gradients[4],
+        gradients[2],
         vector_gradients[4],
         vector_gradients[5],
-        gradients["expand"],
-        gradients["contract"],
+        gradients[1],
+        gradients[0],
         layer_rms,
     )
 

time: 1530 us -> 1230 us (0.80)
  Pallas kernels: 412 us -> 759 us
  waiting for transfers between devices: 320 us -> 56.6 us
  other arithmetic: 153 us -> 41.5 us
  blocking collectives: 181 us -> 79.9 us
  starting transfers between devices: 101 us -> 12.8 us
  matrix products: 234 us -> 153 us
    pallas_call x0 -> x1, Pallas kernels: none -> 401 us  [sum_products(): pl.pallas_call(functools.partial(sum_kernel, tuple(plan), len(products)),...]
    ppermute x56 -> x0, waiting for transfers between devices: 300 us -> none  [the longest x7 149 us: by_y(): return (lax.ppermute(sent, 'fsdp', Y_PAIRS), kept)]
    psum x1 -> x0, blocking collectives: 98.8 us -> none  [on_blocks(): totals = lax.psum(jnp.concatenate(terms + (squares,)), ('seq', 'fsdp'))]
    convert_element_type x33 -> x7, other arithmetic: 109 us -> 14.4 us  [the longest x6 12.7 us: on_blocks(): gradients = [gradient.astype(F32) for gradient in gradients]]
    ppermute x56 -> x0, starting transfers between devices: 87.8 us -> none  [the longest x21 59 us: spread(): lax.ppermute(of_z((z + k) % 4).astype(BF16), 'fsdp', Z_SHIFTS[k - 1])]
    dot_general x14 -> x0, matrix products: 78.2 us -> none  [product_left(): lax.dot_general(left, right, (((0,), (0,)), ((), ())), preferred_element_...]
    pallas_call x2, Pallas kernels: 346 us -> 292 us  [gather_weights(): pl.pallas_call(functools.partial(gather_kernel, plan, vectors is not None...]
    all_to_all x1, waiting for transfers between devices: 0.01 us -> 33.5 us  [on_blocks(): lax.all_to_all(grad_regrouped, 'seq', split_axis=0, concat_axis=0, tiled=...]
  transfers between devices with their start and end apart: 60 -> 4, of which waited for: 17 -> 2; matrix products, arithmetic and copies ran while one was open for 21% -> 8% of each run, Pallas kernels for 19% -> 18%
where the time goes in v2:
time: 1230 us; the launch traced here: 1220 us
  Pallas kernels  759 us (62%)
  matrix products  153 us (12%)
  local copies, waits for them, and re-layouts  98.5 us (8%)
  blocking collectives  79.9 us (6%)
  waiting for transfers between devices  56.6 us (5%)
  other arithmetic  41.5 us (3%)
  between operations  15.7 us (1%)
  starting transfers between devices  12.8 us (1%)
    pallas_call x1, Pallas kernels, sum_products(): pl.pallas_call(functools.partial(sum_kernel, tuple(plan), len(products)),...  401 us
    pallas_call x2, Pallas kernels, gather_weights(): pl.pallas_call(functools.partial(gather_kernel, plan, vectors is not None...  292 us
    all_to_all x1, blocking collectives, on_blocks(): lax.all_to_all(projected, 'seq', split_axis=0, concat_axis=0, tiled=True)  79.9 us
    dot_general x6, matrix products, product(): return jnp.dot(left, right, preferred_element_type=jnp.float32)  78.7 us
    dot_general x6, matrix products, product_right(): lax.dot_general(left, right, (((1,), (1,)), ((), ())), preferred_element_...  64.3 us
    all_to_all x1, waiting for transfers between devices, on_blocks(): lax.all_to_all(grad_regrouped, 'seq', split_axis=0, concat_axis=0, tiled=...  33.5 us
    pallas_call x1, Pallas kernels, attention_back(): pl.pallas_call(functools.partial(attention_back_kernel, scale), grid=(cli...  33.2 us
  transfers between devices with their start and end apart: 4, of which 2 were waited for; matrix products, arithmetic and copies ran while one was open for 8% of the time, Pallas kernels for 18%

profile of v2, /device:TPU:0, one launch (start us, length us, event | category | flops | bytes accessed | tf_op | source)
XLA Modules:
  0.0 1217.0 jit_solution(326810776955318128)
XLA Ops:
  15.2 5.4 reshape_reshape.3.refs_0_
  21.4 107.4 %gather_weights.2 = (bf16[4,2,1,4,48,4608]{5,4,3,2,1,0:T(8,128)(2,1)}, bf16[4,2,1,4,48,1536]{5,4,3,2,1,0:T(8,128)(2,1)}, f32[8,8,256]{2,1,0:T(8,128)}) custom-call(bf16[1,4,48,4608]{3,2,1,0:T(8,128)(2,1)} %reshape_reshape.3.refs_0_, bf16[1,4,48,1536]{3,2,1,0:T(8,128)(2,1)} %bitcast.210, f32[8,256]{1,0:T(8,128)} %pad_convert_fusion.refs_2_), custom_call_target="tpu_custom_call" | custom-call | tf_op jit(solution)/shard_map/gather_weights/pallas_call | solution.py:567
  134.7 12.8 %product_blocks.1 = bf16[4,512,1152]{2,1,0:T(8,128)(2,1)} custom-call(bf16[512,1536]{1,0:T(8,128)(2,1)S(1)} %fusion.21.left.refs_6_, bf16[1536,4608]{1,0:T(8,128)(2,1)} %bitcast.227), custom_call_target="tpu_custom_call" | custom-call | flops 7247757312 | bytes 20447232 | tf_op jit(solution)/shard_map/product_blocks/pallas_call | solution.py:604
  147.5 79.9 %all_to_all.20 = bf16[4,512,1152]{2,1,0:T(8,128)(2,1)} all-to-all(bf16[4,512,1152]{2,1,0:T(8,128)(2,1)} %product_blocks.1), channel_id=1, replica_groups=mesh['seq'=4,'fsdp'=8] {'seq'}, dimensions={0} | all-to-all | bytes 9437184 | tf_op jit(solution)/shard_map/all_to_all | solution.py:1282
  227.4 20.1 %attention.1 = (bf16[4,2,256,384]{3,2,1,0:T(8,128)(2,1)}, f32[2,3,2,1024]{3,2,1,0:T(2,128)S(1)}) custom-call(bf16[4,2,256,1152]{3,2,1,0:T(8,128)(2,1)} %bitcast.197, bf16[4,2,256,1152]{3,2,1,0:T(8,128)(2,1)} %bitcast.198, bf16[4,2,256,1152]{3,2,1,0:T(8,128)(2,1)} %bitcast.199), custom_call_target="tpu_custom_call" | custom-call | flops 6442450944 | bytes 6291456 | tf_op jit(solution)/shard_map/attention/pallas_call | solution.py:691
  251.6 23.0 %all-to-all-done.1 = bf16[4,512,384]{2,1,0:T(8,128)(2,1)S(1)} async-done(((bf16[4,512,384]{2,1,0:T(8,128)(2,1)}), bf16[4,512,384]{2,1,0:T(8,128)(2,1)S(1)}, u32[]{:S(2)}, u32[]{:S(2)}) %all-to-all-start.1) | async-done | bytes 1572896 | tf_op jit(solution)/shard_map/all_to_all | solution.py:1286
  275.9 184.6 %gather_weights.3 = (bf16[4,2,1,4,48,1536]{5,4,3,2,1,0:T(8,128)(2,1)}, bf16[4,2,1,4,48,3072]{5,4,3,2,1,0:T(8,128)(2,1)}, bf16[4,2,1,4,48,1536]{5,4,3,2,1,0:T(8,128)(2,1)}, bf16[4,2,4,4,48,1536]{5,4,3,2,1,0:T(8,128)(2,1)}) custom-call(bf16[1,4,48,1536]{3,2,1,0:T(8,128)(2,1)} %bitcast.208, bf16[1,4,48,3072]{3,2,1,0:T(8,128)(2,1)} %bitcast.207, ...), custom_call_target="tpu_custom_call" | custom-call | tf_op jit(solution)/shard_map/gather_weights/pallas_call | solution.py:567
  460.6 5.8 fusion.52
  474.1 5.1 reshape.308
  482.7 6.9 fusion.14
  498.7 5.0 fusion.55
  515.8 40.8 %multiply_convert_fusion = (bf16[512,6144]{1,0:T(8,128)(2,1)}, f32[512,6144]{1,0:T(8,128)}, f32[512,6144]{1,0:T(8,128)}) fusion(bf16[512,1536]{1,0:T(8,128)(2,1)} %add_convert_fusion.refs_1_, bf16[1536,6144]{1,0:T(8,128)(2,1)} %all-gather.2.cloned.1.call-done), kind=kOutput, calls=%fused_computation.12 | convolution fusion | flops 9868148736 | bytes 51904512 | tf_op jit(solution)/shard_map/dot_general | solution.py:31
  556.6 24.3 %fusion.7.refs_8_ = bf16[512,6144]{1,0:T(8,128)(2,1)} fusion(f32[512,6144]{1,0:T(8,128)} %get-tuple-element.93, f32[512,6144]{1,0:T(8,128)} %get-tuple-element.117, bf16[6144,1536]{1,0:T(8,128)(2,1)} %bitcast.225, bf16[512,1536]{1,0:T(8,128)(2,1)S(1)} %bitcast.178), kind=kOutput, calls=%fused_computation.10 | convolution fusion | flops 9707716608 | bytes 51904512 | tf_op jit(solution)/shard_map/dot_general | solution.py:41
  581.0 17.7 %multiply_reduce_fusion = (f32[1536]{0:T(1024)S(1)}, f32[512]{0:T(512)S(1)}, f32[1536]{0:T(1024)S(1)}, f32[512,1536]{1,0:T(8,128)}) fusion(f32[512,1536]{1,0:T(8,128)} %copy-done.6, f32[512]{0:T(512)S(1)} %fusion.42, f32[512]{0:T(512)S(1)} %broadcast_multiply_fusion, f32[1536]{0:T(1024)S(1)} %mul.259, bf16[512,6144]{1,0:T(8,128)(2,1)} %fusion.7.refs_8_, ...), kind=kOutput, calls=%fused_computation.46 | convolution fusion | flops 9669963776 | bytes 31481856 | tf_op jit(solution)/shard_map/dot_general | solution.py:41
  610.8 5.0 reshape.309
  662.4 33.2 %attention_back.1 = bf16[4,2,256,1152]{3,2,1,0:T(8,128)(2,1)} custom-call(bf16[4,2,256,1152]{3,2,1,0:T(8,128)(2,1)} %bitcast.200, bf16[4,2,256,1152]{3,2,1,0:T(8,128)(2,1)} %bitcast.201, bf16[4,2,256,1152]{3,2,1,0:T(8,128)(2,1)} %bitcast.202, bf16[4,2,256,384]{3,2,1,0:T(8,128)(2,1)S(1)} %bitcast.176, f32[2,3,2,1024]{3,2,1,0:T(2,128)S(1)} %get-tuple-element.60.logsum_ref), custom_call_target="tpu_custom_call" | custom-call | flops 16106127360 | bytes 11010048 | tf_op jit(solution)/shard_map/attention_back/pallas_call | solution.py:773
  695.6 5.2 all-to-all-start.3
  700.9 17.6 %multiply_reduce_fusion.5 = (f32[]{:T(128)}, f32[]{:T(128)}, bf16[512,1536]{1,0:T(8,128)(2,1)}) fusion(f32[512,1536]{1,0:T(8,128)} %copy-done.6, bf16[512,6144]{1,0:T(8,128)(2,1)} %get-tuple-element.62.refs_0_, bf16[6144,1536]{1,0:T(8,128)(2,1)} %bitcast.226), kind=kOutput, calls=%fused_computation.52 | convolution fusion | flops 9668395008 | bytes 29884424 | tf_op jit(solution)/shard_map/dot_general | solution.py:31
  721.2 33.5 %all-to-all-done.3 = bf16[4,512,1152]{2,1,0:T(8,128)(2,1)} async-done(((bf16[4,512,1152]{2,1,0:T(8,128)(2,1)}), bf16[4,512,1152]{2,1,0:T(8,128)(2,1)}, u32[]{:S(2)}, u32[]{:S(2)}) %all-to-all-start.3) | async-done | bytes 4718624 | tf_op jit(solution)/shard_map/all_to_all | solution.py:1361
  757.6 12.3 %fusion.47 = (f32[1536]{0:T(1024)S(1)}, f32[512]{0:T(512)S(1)}, f32[512,1536]{1,0:T(8,128)S(1)}) fusion(f32[1536]{0:T(1024)S(1)} %copy-done.47, f32[512]{0:T(512)S(1)} %bitcast.214, bf16[2,256,1536]{2,1,0:T(8,128)(2,1)S(1)} %copy-done.13, bf16[512,4608]{1,0:T(8,128)(2,1)S(1)} %bitcast.181, bf16[1536,4608]{1,0:T(8,128)(2,1)} %bitcast.228), kind=kOutput, calls=%fused_computation.120 | convolution fusion | flops 7252473856 | bytes 23609344 | tf_op jit(solution)/shard_map/dot_general | solution.py:41
  772.3 401.2 %sum_products.1 = (bf16[768,1536]{1,0:T(8,128)(2,1)}, bf16[192,6144]{1,0:T(8,128)(2,1)}, bf16[192,1536]{1,0:T(8,128)(2,1)}, bf16[192,1536]{1,0:T(8,128)(2,1)}, b...) custom-call(bf16[512,6144]{1,0:T(8,128)(2,1)} %get-tuple-element.62.refs_0_, ...), custom_call_target="tpu_custom_call" | custom-call | tf_op jit(solution)/shard_map/sum_products/pallas_call | solution.py:1190
  1173.6 6.8 reshape.307
  1180.4 5.0 copy.110
  1185.4 5.4 reshape.304
  (259 shorter events, 137.1 us)
Async XLA Ops:
  7.2 121.6 %copy-start = (bf16[192,6144]{1,0:T(8,128)(2,1)S(1)}, bf16[192,6144]{1,0:T(8,128)(2,1)}, u32[]{:S(2)}) copy-start(bf16[192,6144]{1,0:T(8,128)(2,1)} %param.29) | copy-start | bytes 7077892
  7.2 508.6 %all-gather.2.cloned.1.call-start = ((), (), s32[]{:S(2)}) async-start(), calls=%async_computation.4 | async-start | bytes 19464192 | tf_op jit(solution)/shard_map/all_gather | solution.py:1269
  11.1 9.6 copy-start.65
  11.1 9.6 copy-start.66
  11.1 9.6 copy-start.67
  11.1 9.6 copy-start.68
  11.1 9.6 copy-start.69
  11.1 9.6 copy-start.70
  134.1 13.5 %copy-start.50 = (f32[512]{0:T(512)}, f32[512]{0:T(512)S(1)}, u32[]{:S(2)}) copy-start(f32[512]{0:T(512)S(1)} %rsqrt.30) | copy-start | bytes 6148
  134.1 13.4 %copy-start.52 = (f32[1,2,2,128]{3,1,2,0:T(2,128)}, f32[1,2,2,128]{3,1,2,0:T(2,128)S(1)}, u32[]{:S(2)}) copy-start(f32[1,2,2,128]{3,1,2,0:T(2,128)S(1)} %copy.123) | copy-start | bytes 6148
  134.7 12.8 %copy-start.2 = (bf16[512,1536]{1,0:T(8,128)(2,1)}, bf16[512,1536]{1,0:T(8,128)(2,1)S(1)}, u32[]{:S(2)}) copy-start(bf16[512,1536]{1,0:T(8,128)(2,1)S(1)} %fusion.21.left.refs_6_) | copy-start | bytes 4718596
  247.5 27.1 %all-to-all-start.1 = ((bf16[4,512,384]{2,1,0:T(8,128)(2,1)}), bf16[4,512,384]{2,1,0:T(8,128)(2,1)S(1)}, u32[]{:S(2)}, u32[]{:S(2)}) async-start(bf16[4,512,384]{2,1,0:T(8,128)(2,1)} %bitcast.6), calls=%async_computation.1 | async-start | bytes 3145728 | tf_op jit(solution)/shard_map/all_to_all | solution.py:1286
  251.3 215.5 %copy-start.48 = (f32[1536]{0:T(1024)}, f32[1536]{0:T(1024)S(1)}, u32[]{:S(2)}) copy-start(f32[1536]{0:T(1024)S(1)} %mul.251) | copy-start | bytes 18436
  275.9 184.6 %copy-start.12 = (bf16[2,256,1536]{2,1,0:T(8,128)(2,1)S(1)}, bf16[2,256,1536]{2,1,0:T(8,128)(2,1)}, u32[]{:S(2)}) copy-start(bf16[2,256,1536]{2,1,0:T(8,128)(2,1)} %param.16) | copy-start | bytes 4718596
  482.6 15.5 %copy-start.21 = (bf16[2,256,24,64]{1,3,2,0:T(8,128)(2,1)}, bf16[2,256,24,64]{1,3,2,0:T(8,128)(2,1)S(1)}, u32[]{:S(2)}) copy-start(bf16[2,256,24,64]{1,3,2,0:T(8,128)(2,1)S(1)} %copy.95) | copy-start | bytes 4718596
  512.9 43.8 %copy-start.60 = (f32[512]{0:T(512)}, f32[512]{0:T(512)S(1)}, u32[]{:S(2)}) copy-start(f32[512]{0:T(512)S(1)} %multiply_reduce_fusion.9) | copy-start | bytes 6148
  515.8 40.8 %copy-start.17 = (bf16[2,256,1536]{2,1,0:T(8,128)(2,1)S(1)}, bf16[2,256,1536]{2,1,0:T(8,128)(2,1)}, u32[]{:S(2)}) copy-start(bf16[2,256,1536]{2,1,0:T(8,128)(2,1)} %param.31) | copy-start | bytes 4718596
  581.0 17.7 %copy-start.61 = (f32[512]{0:T(512)S(1)}, f32[512]{0:T(512)}, u32[]{:S(2)}) copy-start(f32[512]{0:T(512)} %copy-done.60) | copy-start | bytes 6148
  638.3 24.1 %all-to-all-start.2 = ((bf16[4,512,384]{2,1,0:T(8,128)(2,1)}), bf16[4,512,384]{2,1,0:T(8,128)(2,1)S(1)}, u32[]{:S(2)}, u32[]{:S(2)}) async-start(bf16[4,512,384]{2,1,0:T(8,128)(2,1)} %bitcast.191), calls=%async_computation.2 | async-start | bytes 3145728 | tf_op jit(solution)/shard_map/all_to_all | solution.py:1356
  695.6 59.1 %all-to-all-start.3 = ((bf16[4,512,1152]{2,1,0:T(8,128)(2,1)}), bf16[4,512,1152]{2,1,0:T(8,128)(2,1)}, u32[]{:S(2)}, u32[]{:S(2)}) async-start(bf16[4,512,1152]{2,1,0:T(8,128)(2,1)} %bitcast.203), calls=%async_computation.3 | async-start | bytes 9437184 | tf_op jit(solution)/shard_map/all_to_all | solution.py:1361
  757.6 12.4 %copy-start.20 = (bf16[4,64,8,1152]{3,2,0,1:T(8,128)(2,1)}, bf16[4,64,8,1152]{3,2,0,1:T(8,128)(2,1)S(1)}, u32[]{:S(2)}) copy-start(bf16[4,64,8,1152]{3,2,0,1:T(8,128)(2,1)S(1)} %copy.122) | copy-start | bytes 14155780
  757.6 12.3 %copy-start.63 = (f32[1,2,2,128]{3,1,2,0:T(2,128)S(1)}, f32[1,2,2,128]{3,1,2,0:T(2,128)}, u32[]{:S(2)}) copy-start(f32[1,2,2,128]{3,1,2,0:T(2,128)} %copy-done.62) | copy-start | bytes 6148
  757.6 12.3 %copy-start.51 = (f32[512]{0:T(512)S(1)}, f32[512]{0:T(512)}, u32[]{:S(2)}) copy-start(f32[512]{0:T(512)} %copy-done.50) | copy-start | bytes 6148
  1195.4 9.5 copy-start.18
  (57 other events, 208.3 us)
Sparse Core Ops, SparseCore 0:
  129.8 155.0 all-gather.1

commit v3 on v2

--- a/solution.py
+++ b/solution.py
@@ -589,35 +589,44 @@
     return whole, results[-1]
 
 
+def gather_quarters(shard):
+    part = shard.shape[0] // lax.axis_size("seq")
+    mine = lax.dynamic_slice_in_dim(shard, lax.axis_index("seq") * part, part, 0)
+    return lax.all_gather(mine, ("fsdp", "seq"), axis=0, tiled=True)
+
+
 def pack_vectors(vectors):
     stacked = jnp.stack([vector.astype(F32) for vector in vectors])
     return jnp.pad(stacked, ((0, 8 - stacked.shape[0]), (0, (-stacked.shape[1]) % 128)))
 
 
-def blocks_kernel(left, right, out):
-    out[0] = jnp.dot(left[...], right[...], preferred_element_type=F32).astype(BF16)
-
-
-def product_blocks(left, right, count):
+def blocks_kernel(left, *refs):
+    *rights, out = refs
+    width = rights[0].shape[1]
+    for kind, right in enumerate(rights):
+        out[0, :, kind * width : (kind + 1) * width] = jnp.dot(
+            left[...], right[...], preferred_element_type=F32
+        ).astype(BF16)
+
+
+def product_blocks(left, right, kinds, groups):
     rows, depth = left.shape
-    width = right.shape[1] // count
+    width = right.shape[1] // (kinds * groups)
+    spec = lambda kind: pl.BlockSpec((depth, width), lambda i: (0, kind * groups + i))
     return pl.pallas_call(
         blocks_kernel,
-        grid=(count,),
-        out_shape=jax.ShapeDtypeStruct((count, rows, width), BF16),
-        in_specs=[
-            pl.BlockSpec((rows, depth), lambda i: (0, 0)),
-            pl.BlockSpec((depth, width), lambda i: (0, i)),
-        ],
-        out_specs=pl.BlockSpec((1, rows, width), lambda i: (i, 0, 0)),
+        grid=(groups,),
+        out_shape=jax.ShapeDtypeStruct((groups, rows, kinds * width), BF16),
+        in_specs=[pl.BlockSpec((rows, depth), lambda i: (0, 0))] + [spec(k) for k in range(kinds)],
+        out_specs=pl.BlockSpec((1, rows, kinds * width), lambda i: (i, 0, 0)),
         compiler_params=pltpu.CompilerParams(vmem_limit_bytes=48 << 20),
         cost_estimate=pl.CostEstimate(
-            flops=2 * rows * depth * width * count,
-            bytes_accessed=2 * (rows * depth + depth * width * count + rows * width * count),
+            flops=2 * rows * right.size,
+            bytes_accessed=2 * (rows * depth + right.size + rows * right.shape[1]),
             transcendentals=0,
         ),
         name="product_blocks",
-    )(left, right)
+    )(left, *[right] * kinds)
 
 
 QUERIES = 256
@@ -793,13 +802,79 @@
     )(qkv, qkv, qkv, grad, logsum)
 
 
+def text_weights(scale, queries, keys):
+    scores = across(keys, queries)
+    raised = jnp.exp(scores - jnp.max(scores, axis=0, keepdims=True))
+    return raised / jnp.sum(raised, axis=0, keepdims=True)
+
+
+def pair_columns(pair):
+    return slice(pair * 2 * HD, (pair + 1) * 2 * HD)
+
+
+def text_attention_kernel(scale, q_ref, memory_ref, out_ref):
+    pairs = q_ref.shape[1] // (2 * HD)
+    for pair in range(pairs):
+        queries = both_heads((q_ref[:, pair_columns(pair)].astype(F32) * scale).astype(BF16))
+        k = memory_ref[:, pair_columns(pair)]
+        v = memory_ref[:, pair_columns(pairs + pair)]
+        outs = [down(v, text_weights(scale, part, k).astype(BF16)) for part in queries]
+        out_ref[:, pair_columns(pair)] = join_heads(outs).T.astype(BF16)
+
+
+def text_attention_back_kernel(scale, q_ref, memory_ref, grad_ref, q_out, memory_out):
+    pairs = q_ref.shape[1] // (2 * HD)
+    for pair in range(pairs):
+        queries = both_heads((q_ref[:, pair_columns(pair)].astype(F32) * scale).astype(BF16))
+        grads = both_heads(grad_ref[:, pair_columns(pair)])
+        k = memory_ref[:, pair_columns(pair)]
+        v = memory_ref[:, pair_columns(pairs + pair)]
+        query_grads = []
+        key_grad = value_grad = 0.0
+        for head in range(2):
+            weights = text_weights(scale, queries[head], k)
+            weighted = weights * across(v, grads[head])
+            inner = jnp.sum(weighted, axis=0, keepdims=True)
+            change = (weighted - weights * inner).astype(BF16)
+            query_grads.append(down(k, change))
+            key_grad += jnp.dot(change, queries[head], preferred_element_type=F32)
+            value_grad += jnp.dot(weights.astype(BF16), grads[head], preferred_element_type=F32)
+        q_out[:, pair_columns(pair)] = (join_heads(query_grads).T * scale).astype(BF16)
+        memory_out[:, pair_columns(pair)] = key_grad.astype(BF16)
+        memory_out[:, pair_columns(pairs + pair)] = value_grad.astype(BF16)
+
+
+def text_attention(clips, scale, queries, memory, grad=None):
+    spec = lambda value: pl.BlockSpec(
+        (value.shape[0] // clips, value.shape[1]), lambda clip: (clip, 0)
+    )
+    back = grad is not None
+    operands = (queries, memory) + ((grad,) if back else ())
+    results = (queries, memory) if back else (queries,)
+    size = memory.shape[0] // clips * queries.size
+    outs = pl.pallas_call(
+        functools.partial(text_attention_back_kernel if back else text_attention_kernel, scale),
+        grid=(clips,),
+        out_shape=[jax.ShapeDtypeStruct(value.shape, BF16) for value in results],
+        in_specs=[spec(value) for value in operands],
+        out_specs=[spec(value) for value in results],
+        compiler_params=pltpu.CompilerParams(vmem_limit_bytes=32 << 20),
+        cost_estimate=pl.CostEstimate(
+            flops=(20 if back else 8) * size,
+            bytes_accessed=2 * sum(value.size for value in operands + results),
+            transcendentals=size // HD,
+        ),
+        name="text_attention_back" if back else "text_attention",
+    )(*operands)
+    return outs if back else outs[0]
+
+
 PIECE = (192, 384)
 LAGS = (0, 1, 3, 4, 5, 6, 7)
 
 
 def sum_kernel(plan, weights, *refs):
     chunks = len(plan)
-    tall = sum(entry[1] for entry in plan)
     lefts, rights = refs[:weights], refs[weights : 2 * weights]
     vector_in = refs[2 * weights]
     outputs = refs[2 * weights + 1 : 3 * weights + 1]
@@ -815,11 +890,9 @@
         total,
         fx_in,
         fc_in,
-        wide_stage,
-        tall_stage,
+        stage,
         left_buf,
         right_buf,
-        tall_buf,
         vector,
         vector_got,
         vector_z,
@@ -864,19 +937,8 @@
         return i % 2 == 0
 
     def loads(j):
-        weight, is_tall, column = plan[j]
+        weight, column = plan[j]
         slot = j % 2
-        if is_tall:
-            copies = [
-                pltpu.make_async_copy(
-                    rights[weight].at[:, pl.ds(column, 384)],
-                    right_buf.at[slot, :, pl.ds(0, 384)],
-                    load_sem.at[1, slot],
-                )
-            ]
-            if j == 0:
-                copies.append(pltpu.make_async_copy(lefts[weight], tall_buf, load_sem.at[2, 0]))
-            return copies
         return [
             pltpu.make_async_copy(lefts[weight], left_buf.at[slot], load_sem.at[0, slot]),
             pltpu.make_async_copy(
@@ -905,29 +967,14 @@
 
     def multiply(i, half, target, slot):
         buffer = i % 2
-
-        @pl.when(i >= tall)
-        def _():
-            right = right_buf.at[buffer, :, pl.ds(pl.multiple_of(half * 768, 128), 768)]
-
-            @pl.loop(0, 4)
-            def _(zz):
-                out = down(left_buf[buffer, :, columns(zz)], right[...]).astype(BF16)
-                for q in range(2):
-                    for yy in range(2):
-                        target[slot, q, zz, yy] = out[192 * yy : 192 * yy + 192, 384 * q : 384 * q + 384]
-
-        @pl.when(i < tall)
-        def _():
-            right = right_buf.at[buffer, :, pl.ds(0, 384)]
-
-            @pl.loop(0, 4)
-            def _(zz):
+        right = right_buf.at[buffer, :, pl.ds(pl.multiple_of(half * 768, 128), 768)]
+
+        @pl.loop(0, 4)
+        def _(zz):
+            out = down(left_buf[buffer, :, columns(zz)], right[...]).astype(BF16)
+            for q in range(2):
                 for yy in range(2):
-                    left = tall_buf[:, columns((2 * zz + yy) * 2 + half)]
-                    out = down(left, right[...]).astype(BF16)
-                    for q in range(2):
-                        target[slot, q, zz, yy] = out[192 * q : 192 * q + 192]
+                    target[slot, q, zz, yy] = out[192 * yy : 192 * yy + 192, 384 * q : 384 * q + 384]
 
     def add_to(slot, q, zz, yy, other):
         here = mine[slot, q, zz, yy].astype(F32)
@@ -1055,15 +1102,7 @@
             z_copy(i, k).start()
 
     def put(i, quarter, value):
-        slot = i % 2
-
-        @pl.when(i >= tall)
-        def _():
-            wide_stage[slot, :, columns(quarter)] = value
-
-        @pl.when(i < tall)
-        def _():
-            tall_stage[slot, pl.ds(pl.multiple_of(quarter * 192, 64), 192)] = value
+        stage[i % 2, :, columns(quarter)] = value
 
     def fourth(i):
         slot = i % 4
@@ -1080,14 +1119,9 @@
         fc_copy(i, 1).start()
 
     def store(j):
-        weight, is_tall, column = plan[j]
-        slot = j % 2
-        if is_tall:
-            return pltpu.make_async_copy(
-                tall_stage.at[slot], outputs[weight].at[:, pl.ds(column, 384)], stage_sem.at[0, slot]
-            )
+        weight, column = plan[j]
         return pltpu.make_async_copy(
-            wide_stage.at[slot], outputs[weight].at[:, pl.ds(column, 1536)], stage_sem.at[1, slot]
+            stage.at[j % 2], outputs[weight].at[:, pl.ds(column, 1536)], stage_sem.at[j % 2]
         )
 
     def sixth(i):
@@ -1175,10 +1209,11 @@
 def sum_products(products, vectors):
     lefts = [left for left, _ in products]
     rights = [right for _, right in products]
-    height, width = lefts[0].shape[1], rights[0].shape[1]
-    plan = [(0, True, column) for column in range(0, width, 384)]
-    for weight in range(1, len(products)):
-        plan += [(weight, False, column) for column in range(0, rights[weight].shape[1], 1536)]
+    plan = [
+        (weight, column)
+        for weight, right in enumerate(rights)
+        for column in range(0, right.shape[1], 1536)
+    ]
     out_shapes = [
         jax.ShapeDtypeStruct((left.shape[1] // 8, right.shape[1]), BF16) for left, right in products
     ]
@@ -1204,10 +1239,8 @@
             block(4),
             block(4, 2),
             pltpu.VMEM((2, 192, 1536), BF16),
-            pltpu.VMEM((2, 768, 384), BF16),
             pltpu.VMEM((2, depth, 1536), BF16),
             pltpu.VMEM((2, depth, 1536), BF16),
-            pltpu.VMEM((depth, height), BF16),
             pltpu.VMEM((3,) + vectors.shape, F32),
             pltpu.VMEM((3,) + vectors.shape, F32),
             pltpu.VMEM((4,) + vectors.shape, F32),
@@ -1217,8 +1250,8 @@
             dma((2, 4, 3)),
             dma((2, 4)),
             dma((2, 4, 2)),
+            dma((2,)),
             dma((2, 2)),
-            dma((3, 2)),
             dma((2, 6)),
         ],
         compiler_params=pltpu.CompilerParams(
@@ -1255,98 +1288,66 @@
     entries = rows * groups * fsdp_count * width
     group_width = width // groups
 
-    def by_group(value):
-        return value.reshape(-1, 3, groups, group_width).transpose(0, 2, 1, 3).reshape(value.shape)
-
-    def by_kind(value):
-        return value.reshape(-1, groups, 3, group_width).transpose(0, 2, 1, 3).reshape(value.shape)
-
     gains = (self_gain, self_bias, cross_gain, cross_bias, final_gain, final_bias)
-    early = (by_group(query_key_value), self_output)
+    early = (query_key_value, self_output)
     (qkv_whole, self_output_whole), vectors = gather_weights(early, pack_vectors(gains), 1)
     qkv_whole, expand_weight = lax.optimization_barrier((qkv_whole, expand_weight))
-    part = expand_weight.shape[0] // groups
-    expand_whole = lax.all_gather(
-        lax.dynamic_slice_in_dim(expand_weight, lax.axis_index("seq") * part, part, 0),
-        ("fsdp", "seq"),
-        axis=0,
-        tiled=True,
-    )
+    expand_whole = gather_quarters(expand_weight)
     vectors = vectors[:, :6, : width // fsdp_count]
     gains = [vectors[:, i].reshape(width) for i in range(6)]
 
     hidden = hidden_states.reshape(rows, width).astype(F32)
     normed_one, norm_one_back = jax.vjp(layer_norm, hidden, gains[0], gains[1])
     normed_one = normed_one.astype(BF16)
-    projected = product_blocks(normed_one, qkv_whole, groups)
+    projected = product_blocks(normed_one, qkv_whole, 3, groups)
     regrouped = lax.all_to_all(projected, "seq", split_axis=0, concat_axis=0, tiled=True)
     regrouped = regrouped.reshape(groups, clips, frames, 3 * group_width)
     context_heads, logsum = attention(regrouped, scale)
     context_heads = context_heads.reshape(groups, rows, group_width)
     context = lax.all_to_all(context_heads, "seq", split_axis=0, concat_axis=0, tiled=True)
-    late = (cross_query, cross_memory, cross_output, contract_weight)
-    context, late = lax.optimization_barrier((context, late))
+    late = (cross_query, cross_memory, cross_output)
+    context, late, expand_whole, contract_weight = lax.optimization_barrier(
+        (context, late, expand_whole, contract_weight)
+    )
+    contract_whole = gather_quarters(contract_weight)
     late, _ = gather_weights(late, None, 2)
-    cross_query_whole, cross_memory_whole, cross_output_whole, contract_whole = late
+    cross_query_whole, cross_memory_whole, cross_output_whole = late
     context = context.transpose(1, 0, 2).reshape(rows, width)
     attended = product(context, self_output_whole)
     first = hidden + attended
     normed_two, norm_two_back = jax.vjp(layer_norm, first, gains[2], gains[3])
     normed_two = normed_two.astype(BF16)
-    cross_q = product(normed_two, cross_query_whole).astype(BF16).reshape(clips, frames, H, HD)
+    cross_q = product(normed_two, cross_query_whole).astype(BF16)
     text_rows = text_states.reshape(clips * TEXT, width)
-    memory = product(text_rows, cross_memory_whole).astype(BF16).reshape(clips, TEXT, 2, H, HD)
-    cross_keys = memory[:, :, 0]
-    cross_values = memory[:, :, 1]
-    cross_scores = (
-        jnp.einsum("cqhd,ckhd->chqk", cross_q, cross_keys, preferred_element_type=F32) * scale
-    )
-    highest = jnp.max(cross_scores, axis=-1, keepdims=True)
-    raised = jnp.exp(cross_scores - highest)
-    cross_weights = raised / jnp.sum(raised, axis=-1, keepdims=True)
-    cross_rounded = cross_weights.astype(BF16)
-    cross_context = jnp.einsum(
-        "chqk,ckhd->cqhd", cross_rounded, cross_values, preferred_element_type=F32
-    )
-    cross_context = cross_context.astype(BF16).reshape(rows, width)
+    memory = product(text_rows, cross_memory_whole).astype(BF16)
+    cross_context = text_attention(clips, scale, cross_q, memory)
     crossed = product(cross_context, cross_output_whole)
     second = first + crossed
     normed_three, norm_three_back = jax.vjp(layer_norm, second, gains[4], gains[5])
     normed_three = normed_three.astype(BF16)
     preact = product(normed_three, expand_whole)
-    activated, gelu_back = jax.vjp(gelu_exact, preact)
-    activated = activated.astype(BF16)
+    below = 0.5 + 0.5 * lax.erf(preact * 0.5**0.5)
+    density = jnp.exp(preact * preact * -0.5) * (0.5 / jnp.pi) ** 0.5
+    activated = (preact * below).astype(BF16)
+    slope = (below + preact * density).astype(BF16)
     upstream = output_cotangent.reshape(rows, width).astype(F32)
     grad_mixed = output_cotangent.reshape(rows, width)
+    contract_term = product_left(activated, grad_mixed).astype(BF16)
+    grad_mixed, contract_term, contract_whole = lax.optimization_barrier(
+        (grad_mixed, contract_term, contract_whole)
+    )
+    contract_part = lax.psum_scatter(
+        contract_term, ("fsdp", "seq"), scatter_dimension=0, tiled=True
+    )
+    contract_gradient = lax.all_gather(contract_part, "seq", axis=0, tiled=True)
     grad_activated = product_right(grad_mixed, contract_whole)
-    grad_preact = gelu_back(grad_activated)[0].astype(BF16)
+    grad_preact = (grad_activated * slope.astype(F32)).astype(BF16)
     grad_normed_three = product_right(grad_preact, expand_whole)
     grad_second, final_gain_term, final_bias_term = norm_three_back(grad_normed_three)
     grad_second = upstream + grad_second
     grad_crossed = grad_second.astype(BF16)
-    grad_cross_context = (
-        product_right(grad_crossed, cross_output_whole).astype(BF16).reshape(clips, frames, H, HD)
-    )
-    grad_cross_weights = jnp.einsum(
-        "cqhd,ckhd->chqk", grad_cross_context, cross_values, preferred_element_type=F32
-    )
-    cross_inner = jnp.sum(cross_weights * grad_cross_weights, axis=-1, keepdims=True)
-    grad_cross_scores = (cross_weights * (grad_cross_weights - cross_inner)).astype(BF16)
-    grad_cross_q = (
-        jnp.einsum("chqk,ckhd->cqhd", grad_cross_scores, cross_keys, preferred_element_type=F32)
-        * scale
-    )
-    grad_cross_q = grad_cross_q.astype(BF16).reshape(rows, width)
-    grad_cross_keys = (
-        jnp.einsum("chqk,cqhd->ckhd", grad_cross_scores, cross_q, preferred_element_type=F32)
-        * scale
-    )
-    grad_cross_values = jnp.einsum(
-        "chqk,cqhd->ckhd", cross_rounded, grad_cross_context, preferred_element_type=F32
-    )
-    grad_memory = jnp.stack([grad_cross_keys, grad_cross_values], axis=2).reshape(
-        clips * TEXT, 2 * width
-    )
+    grad_cross_context = product_right(grad_crossed, cross_output_whole).astype(BF16)
+    grad_cross_q, grad_memory = text_attention(clips, scale, cross_q, memory, grad_cross_context)
     grad_normed_two = product_right(grad_cross_q, cross_query_whole)
     grad_first, cross_gain_term, cross_bias_term = norm_two_back(grad_normed_two)
     grad_first = grad_second + grad_first
@@ -1371,7 +1372,14 @@
     )
     output = output.astype(BF16)
     grad_projected, output, squares = lax.optimization_barrier((grad_projected, output, squares))
-    grad_projected = grad_projected.transpose(1, 0, 2).reshape(rows, 3 * width)
+    grad_projected = jnp.concatenate(
+        [
+            grad_projected[group, :, kind * group_width : (kind + 1) * group_width]
+            for kind in range(3)
+            for group in range(groups)
+        ],
+        1,
+    )
     grad_normed_one = product_right(grad_projected, qkv_whole)
     grad_hidden, gain_one_term, bias_one_term = norm_one_back(grad_normed_one)
     grad_hidden = grad_first + grad_hidden
@@ -1390,17 +1398,17 @@
     deep = lambda value: jnp.pad(value, ((0, rows - value.shape[0]), (0, 0)))
     gradients, totals = sum_products(
         [
-            (activated, grad_mixed),
             (normed_three, grad_preact),
             (cross_context, grad_crossed),
             (normed_two, grad_cross_q),
-            (deep(text_rows), deep(grad_memory.astype(BF16))),
+            (deep(text_rows), deep(grad_memory)),
             (context, grad_attended),
             (normed_one, grad_projected),
         ],
         terms,
     )
     gradients = [gradient.astype(F32) for gradient in gradients]
+    contract_gradient = contract_gradient.astype(F32)
     layer_rms = jnp.sqrt(totals[6, :4] / entries)
     shard = width // fsdp_count
     vector_gradients = lax.dynamic_slice_in_dim(
@@ -1411,17 +1419,17 @@
         grad_hidden.reshape(clips, frames, width),
         vector_gradients[0],
         vector_gradients[1],
-        by_kind(gradients[6]),
         gradients[5],
+        gradients[4],
         vector_gradients[2],
         vector_gradients[3],
+        gradients[2],
         gradients[3],
-        gradients[4],
-        gradients[2],
+        gradients[1],
         vector_gradients[4],
         vector_gradients[5],
-        gradients[1],
         gradients[0],
+        contract_gradient,
         layer_rms,
     )
 

time: 1230 us -> 1100 us (0.89)
  Pallas kernels: 759 us -> 671 us
  local copies, waits for them, and re-layouts: 98.5 us -> 44.2 us
  waiting for transfers between devices: 56.6 us -> 104 us
  matrix products: 153 us -> 130 us
    pallas_call x1, Pallas kernels: 401 us -> 317 us  [sum_products(): pl.pallas_call(functools.partial(sum_kernel, tuple(plan), len(products)),...]
    reshape x13 -> x0, local copies, waits for them, and re-layouts: 53.1 us -> none  [the longest x3 17.2 us: by_kind(): value.reshape(-1, groups, 3, group_width).transpose(0, 2, 1, 3)]
    dot_general x6, matrix products: 78.7 us -> 50.8 us  [product(): return jnp.dot(left, right, preferred_element_type=jnp.float32)]
    pallas_call x2, Pallas kernels: 292 us -> 272 us  [gather_weights(): pl.pallas_call(functools.partial(gather_kernel, plan, vectors is not None...]
    all_to_all x1, waiting for transfers between devices: 0.01 us -> 19.4 us  [on_blocks(): lax.all_to_all(grad_context, 'seq', split_axis=0, concat_axis=0, tiled=True)]
    pallas_call x1 -> x3, Pallas kernels: 12.8 us -> 29.1 us  [the longest x2 15 us: text_attention(): pl.pallas_call(functools.partial(text_attention_back_kernel if back else...]
    all_to_all x1, waiting for transfers between devices: 33.5 us -> 46 us  [on_blocks(): lax.all_to_all(grad_regrouped, 'seq', split_axis=0, concat_axis=0, tiled=...]
    unnamed x159 -> x115, local copies, waits for them, and re-layouts: 15.9 us -> 25.6 us
  transfers between devices with their start and end apart: 4 -> 7, of which waited for: 2 -> 5; matrix products, arithmetic and copies ran while one was open for 8% -> 18% of each run, Pallas kernels for 18% -> 51%
where the time goes in v3:
time: 1100 us
  Pallas kernels  671 us (61%)
  matrix products  130 us (12%)
  waiting for transfers between devices  104 us (9%)
  blocking collectives  80.7 us (7%)
  local copies, waits for them, and re-layouts  44.2 us (4%)
  other arithmetic  36.7 us (3%)
  between operations  15 us (1%)
  starting transfers between devices  13.9 us (1%)
    pallas_call x1, Pallas kernels, sum_products(): pl.pallas_call(functools.partial(sum_kernel, tuple(plan), len(products)),...  317 us
    pallas_call x2, Pallas kernels, gather_weights(): pl.pallas_call(functools.partial(gather_kernel, plan, vectors is not None...  272 us
    all_to_all x1, blocking collectives, on_blocks(): lax.all_to_all(projected, 'seq', split_axis=0, concat_axis=0, tiled=True)  80.7 us
    dot_general x6, matrix products, product_right(): lax.dot_general(left, right, (((1,), (1,)), ((), ())), preferred_element_...  62.9 us
    dot_general x6, matrix products, product(): return jnp.dot(left, right, preferred_element_type=jnp.float32)  50.8 us
    all_to_all x1, waiting for transfers between devices, on_blocks(): lax.all_to_all(grad_regrouped, 'seq', split_axis=0, concat_axis=0, tiled=...  46 us
    pallas_call x1, Pallas kernels, attention_back(): pl.pallas_call(functools.partial(attention_back_kernel, scale), grid=(cli...  33.3 us
    unnamed x115, local copies, waits for them, and re-layouts  25.6 us
  transfers between devices with their start and end apart: 7, of which 5 were waited for; matrix products, arithmetic and copies ran while one was open for 18% of the time, Pallas kernels for 51%

profile of v3, /device:TPU:0, one launch (start us, length us, event | category | flops | bytes accessed | tf_op | source)
XLA Modules:
  0.0 1096.1 jit_solution(9436638516902697128)
XLA Ops:
  12.0 107.4 %gather_weights.2 = (bf16[4,2,1,4,48,4608]{5,4,3,2,1,0:T(8,128)(2,1)}, bf16[4,2,1,4,48,1536]{5,4,3,2,1,0:T(8,128)(2,1)}, f32[8,8,256]{2,1,0:T(8,128)}) custom-call(bf16[1,4,48,4608]{3,2,1,0:T(8,128)(2,1)} %bitcast.156, bf16[1,4,48,1536]{3,2,1,0:T(8,128)(2,1)} %bitcast.159, f32[8,256]{1,0:T(8,128)} %pad_convert_fusion.refs_2_), custom_call_target="tpu_custom_call" | custom-call | tf_op jit(solution)/shard_map/gather_weights/pallas_call | solution.py:567
  124.7 14.1 %product_blocks.1 = bf16[4,512,1152]{2,1,0:T(8,128)(2,1)} custom-call(bf16[512,1536]{1,0:T(8,128)(2,1)S(1)} %fusion.7.left.refs_5_, bf16[1536,4608]{1,0:T(8,128)(2,1)} %bitcast.133, bf16[1536,4608]{1,0:T(8,128)(2,1)} %bitcast.134, bf16[1536,4608]{1,0:T(8,128)(2,1)} %bitcast.135), custom_call_target="tpu_custom_call" | custom-call | flops 7247757312 | bytes 20447232 | tf_op jit(solution)/shard_map/product_blocks/pallas_call | solution.py:616
  138.9 80.7 %all_to_all.20 = bf16[4,512,1152]{2,1,0:T(8,128)(2,1)} all-to-all(bf16[4,512,1152]{2,1,0:T(8,128)(2,1)} %product_blocks.1), channel_id=1, replica_groups=mesh['seq'=4,'fsdp'=8] {'seq'}, dimensions={0} | all-to-all | bytes 9437184 | tf_op jit(solution)/shard_map/all_to_all | solution.py:1303
  219.6 20.1 %attention.1 = (bf16[4,2,256,384]{3,2,1,0:T(8,128)(2,1)}, f32[2,3,2,1024]{3,2,1,0:T(2,128)S(1)}) custom-call(bf16[4,2,256,1152]{3,2,1,0:T(8,128)(2,1)} %bitcast.146, bf16[4,2,256,1152]{3,2,1,0:T(8,128)(2,1)} %bitcast.147, bf16[4,2,256,1152]{3,2,1,0:T(8,128)(2,1)} %bitcast.148), custom_call_target="tpu_custom_call" | custom-call | flops 6442450944 | bytes 6291456 | tf_op jit(solution)/shard_map/attention/pallas_call | solution.py:700
  243.3 22.6 %all-to-all-done.1 = bf16[4,512,384]{2,1,0:T(8,128)(2,1)S(1)} async-done(((bf16[4,512,384]{2,1,0:T(8,128)(2,1)}), bf16[4,512,384]{2,1,0:T(8,128)(2,1)S(1)}, u32[]{:S(2)}, u32[]{:S(2)}) %all-to-all-start.1) | async-done | bytes 1572896 | tf_op jit(solution)/shard_map/all_to_all | solution.py:1307
  266.0 9.4 all-gather.4.cloned.1.call-done
  279.2 164.3 %gather_weights.3 = (bf16[4,2,1,4,48,1536]{5,4,3,2,1,0:T(8,128)(2,1)}, bf16[4,2,1,4,48,3072]{5,4,3,2,1,0:T(8,128)(2,1)}, bf16[4,2,1,4,48,1536]{5,4,3,2,1,0:T(8,128)(2,1)}) custom-call(bf16[1,4,48,1536]{3,2,1,0:T(8,128)(2,1)} %bitcast.160, bf16[1,4,48,3072]{3,2,1,0:T(8,128)(2,1)} %bitcast.158, bf16[1,4,48,1536]{3,2,1,0:T(8,128)(2,1)} %bitcast.161), custom_call_target="tpu_custom_call" | custom-call | tf_op jit(solution)/shard_map/gather_weights/pallas_call | solution.py:567
  443.6 5.9 fusion.22
  465.5 19.6 %multiply_convert_fusion.1 = (bf16[512,6144]{1,0:T(8,128)(2,1)}, f32[512,6144]{1,0:T(8,128)}) fusion(bf16[512,1536]{1,0:T(8,128)(2,1)S(1)} %add_convert_fusion.1.refs_0_, bf16[1536,6144]{1,0:T(8,128)(2,1)} %all-gather.4.cloned.1.call-done), kind=kOutput, calls=%fused_computation.3 | convolution fusion | flops 9679405056 | bytes 39321600 | tf_op jit(solution)/shard_map/dot_general | solution.py:31
  485.1 16.1 %convolution_convert_fusion = bf16[6144,1536]{1,0:T(8,128)(2,1)} fusion(bf16[512,6144]{1,0:T(8,128)(2,1)} %get-tuple-element.69, bf16[512,1536]{1,0:T(8,128)(2,1)S(1)} %bitcast.141), kind=kOutput, calls=%fused_computation | convolution fusion | flops 9673113600 | bytes 26738688 | tf_op jit(solution)/shard_map/dot_general | solution.py:35
  501.2 18.9 %multiply_convert_fusion.refs_6_ = bf16[512,6144]{1,0:T(8,128)(2,1)} fusion(bf16[512,1536]{1,0:T(8,128)(2,1)} %bitcast.140, bf16[6144,1536]{1,0:T(8,128)(2,1)} %all-gather.6.cloned.1.call-done, f32[512,6144]{1,0:T(8,128)} %get-tuple-element.120), kind=kOutput, calls=%fused_computation.1 | convolution fusion | flops 9701425152 | bytes 39321600 | tf_op jit(solution)/shard_map/dot_general | solution.py:41
  520.1 19.3 %multiply_reduce_fusion = (f32[1536]{0:T(1024)S(1)}, f32[512]{0:T(512)S(1)}, f32[1536]{0:T(1024)S(1)}, f32[512,1536]{1,0:T(8,128)}) fusion(f32[512,1536]{1,0:T(8,128)} %copy-done.12, f32[512]{0:T(512)S(1)} %fusion.14, f32[512]{0:T(512)S(1)} %broadcast_multiply_fusion, f32[1536]{0:T(1024)S(1)} %mul.236, bf16[512,6144]{1,0:T(8,128)(2,1)} %multiply_convert_fusion.refs_6_, ...), kind=kOutput, calls=%fused_computation.25 | convolution fusion | flops 9669963776 | bytes 31481856 | tf_op jit(solution)/shard_map/dot_general | solution.py:41
  545.5 7.0 convolution_convert_fusion.3.grad_ref
  552.5 11.9 %text_attention_back.1 = (bf16[512,1536]{1,0:T(8,128)(2,1)S(1)}, bf16[128,3072]{1,0:T(8,128)(2,1)S(1)}) custom-call(bf16[512,1536]{1,0:T(8,128)(2,1)S(1)} %convolution_convert_fusion.4.q_ref, bf16[128,3072]{1,0:T(8,128)(2,1)S(1)} %fusion.memory_ref, bf16[512,1536]{1,0:T(8,128)(2,1)S(1)} %convolution_convert_fusion.3.grad_ref), custom_call_target="tpu_custom_call" | custom-call | flops 1006632960 | bytes 6291456 | tf_op jit(solution)/shard_map/text_attention_back/pallas_call | solution.py:855
  574.2 4.7 all-to-all-start.2
  582.2 19.4 %all-to-all-done.2 = bf16[4,512,384]{2,1,0:T(8,128)(2,1)S(1)} async-done(((bf16[4,512,384]{2,1,0:T(8,128)(2,1)}), bf16[4,512,384]{2,1,0:T(8,128)(2,1)S(1)}, u32[]{:S(2)}, u32[]{:S(2)}) %all-to-all-start.2) | async-done | bytes 1572896 | tf_op jit(solution)/shard_map/all_to_all | solution.py:1357
  601.7 33.3 %attention_back.1 = bf16[4,2,256,1152]{3,2,1,0:T(8,128)(2,1)} custom-call(bf16[4,2,256,1152]{3,2,1,0:T(8,128)(2,1)} %bitcast.149, bf16[4,2,256,1152]{3,2,1,0:T(8,128)(2,1)} %bitcast.150, bf16[4,2,256,1152]{3,2,1,0:T(8,128)(2,1)} %bitcast.151, bf16[4,2,256,384]{3,2,1,0:T(8,128)(2,1)S(1)} %bitcast.132, f32[2,3,2,1024]{3,2,1,0:T(2,128)S(1)} %get-tuple-element.67.logsum_ref), custom_call_target="tpu_custom_call" | custom-call | flops 16106127360 | bytes 11010048 | tf_op jit(solution)/shard_map/attention_back/pallas_call | solution.py:782
  634.9 5.2 all-to-all-start.3
  640.3 17.8 %multiply_reduce_fusion.5 = (f32[]{:T(128)}, f32[]{:T(128)}, bf16[512,1536]{1,0:T(8,128)(2,1)}) fusion(f32[512,1536]{1,0:T(8,128)S(1)} %copy-done.13, bf16[512,6144]{1,0:T(8,128)(2,1)} %get-tuple-element.69, bf16[6144,1536]{1,0:T(8,128)(2,1)} %all-gather.6.cloned.1.call-done), kind=kOutput, calls=%fused_computation.31 | convolution fusion | flops 9668395008 | bytes 29884424 | tf_op jit(solution)/shard_map/dot_general | solution.py:31
  660.7 46.0 %all-to-all-done.3 = bf16[4,512,1152]{2,1,0:T(8,128)(2,1)} async-done(((bf16[4,512,1152]{2,1,0:T(8,128)(2,1)}), bf16[4,512,1152]{2,1,0:T(8,128)(2,1)}, u32[]{:S(2)}, u32[]{:S(2)}) %all-to-all-start.3) | async-done | bytes 4718624 | tf_op jit(solution)/shard_map/all_to_all | solution.py:1362
  728.3 6.7 reduce-scatter.2.cloned.1.call-done
  735.2 12.1 %fusion.18 = (f32[1536]{0:T(1024)S(1)}, f32[512]{0:T(512)S(1)}, f32[512,1536]{1,0:T(8,128)S(1)}) fusion(f32[1536]{0:T(1024)S(1)} %copy-done.33, f32[512]{0:T(512)S(1)} %bitcast.163, bf16[2,256,1536]{2,1,0:T(8,128)(2,1)S(1)} %copy-done.8, bf16[512,4608]{1,0:T(8,128)(2,1)} %bitcast_dynamic-update-slice_fusion.refs_11_, bf16[1536,4608]{1,0:T(8,128)(2,1)} %bitcast.136), kind=kOutput, calls=%fused_computation.87 | convolution fusion | flops 7252473856 | bytes 23609344 | tf_op jit(solution)/shard_map/dot_general | solution.py:41
  749.6 317.2 %sum_products.1 = (bf16[192,6144]{1,0:T(8,128)(2,1)}, bf16[192,1536]{1,0:T(8,128)(2,1)}, bf16[192,1536]{1,0:T(8,128)(2,1)}, bf16[192,3072]{1,0:T(8,128)(2,1)}, b...) custom-call(bf16[512,1536]{1,0:T(8,128)(2,1)} %copy-done.22, bf16[512,1536]{1,0:T(8,128)(2,1)} %copy-done.3, ...), custom_call_target="tpu_custom_call" | custom-call | tf_op jit(solution)/shard_map/sum_products/pallas_call | solution.py:1225
  1066.8 4.5 convert_element_type.120
  (204 shorter events, 96.6 us)
Async XLA Ops:
  7.2 112.2 %copy-start = (bf16[192,6144]{1,0:T(8,128)(2,1)S(1)}, bf16[192,6144]{1,0:T(8,128)(2,1)}, u32[]{:S(2)}) copy-start(bf16[192,6144]{1,0:T(8,128)(2,1)} %param.29) | copy-start | bytes 7077892
  7.2 268.2 %all-gather.4.cloned.1.call-start = ((), (), s32[]{:S(2)}) async-start(), calls=%async_computation.5 | async-start | bytes 19464192 | tf_op jit(solution)/shard_map/all_gather | solution.py:595
  124.0 14.8 %copy-start.38 = (f32[1,2,2,128]{3,1,2,0:T(2,128)}, f32[1,2,2,128]{3,1,2,0:T(2,128)S(1)}, u32[]{:S(2)}) copy-start(f32[1,2,2,128]{3,1,2,0:T(2,128)S(1)} %copy.42) | copy-start | bytes 6148
  124.0 14.8 %copy-start.34 = (f32[512]{0:T(512)}, f32[512]{0:T(512)S(1)}, u32[]{:S(2)}) copy-start(f32[512]{0:T(512)S(1)} %rsqrt.30) | copy-start | bytes 6148
  124.0 14.8 %copy-start.36 = (f32[1,2,2,128]{3,1,2,0:T(2,128)}, f32[1,2,2,128]{3,1,2,0:T(2,128)S(1)}, u32[]{:S(2)}) copy-start(f32[1,2,2,128]{3,1,2,0:T(2,128)S(1)} %copy.41) | copy-start | bytes 6148
  124.7 14.1 %copy-start.2 = (bf16[512,1536]{1,0:T(8,128)(2,1)}, bf16[512,1536]{1,0:T(8,128)(2,1)S(1)}, u32[]{:S(2)}) copy-start(bf16[512,1536]{1,0:T(8,128)(2,1)S(1)} %fusion.7.left.refs_5_) | copy-start | bytes 4718596
  239.7 26.3 %all-to-all-start.1 = ((bf16[4,512,384]{2,1,0:T(8,128)(2,1)}), bf16[4,512,384]{2,1,0:T(8,128)(2,1)S(1)}, u32[]{:S(2)}, u32[]{:S(2)}) async-start(bf16[4,512,384]{2,1,0:T(8,128)(2,1)} %bitcast.6), calls=%async_computation.1 | async-start | bytes 3145728 | tf_op jit(solution)/shard_map/all_to_all | solution.py:1307
  243.3 257.9 %all-gather.6.cloned.1.call-start = ((), (), s32[]{:S(2)}) async-start(), calls=%async_computation.6 | async-start | bytes 19464192 | tf_op jit(solution)/shard_map/all_gather | solution.py:595
  277.3 457.7 %reduce-scatter.2.cloned.1.call-start = ((), (), s32[]{:S(2)}) async-start(), calls=%async_computation.7 | async-start | bytes 19464192 | tf_op jit(solution)/shard_map/reduce_scatter | solution.py:1339
  465.5 19.6 %copy-start.22 = (bf16[512,1536]{1,0:T(8,128)(2,1)}, bf16[512,1536]{1,0:T(8,128)(2,1)S(1)}, u32[]{:S(2)}) copy-start(bf16[512,1536]{1,0:T(8,128)(2,1)S(1)} %add_convert_fusion.1.refs_0_) | copy-start | bytes 4718596
  465.5 19.6 %copy-start.16 = (bf16[2,256,1536]{2,1,0:T(8,128)(2,1)S(1)}, bf16[2,256,1536]{2,1,0:T(8,128)(2,1)}, u32[]{:S(2)}) copy-start(bf16[2,256,1536]{2,1,0:T(8,128)(2,1)} %param.31) | copy-start | bytes 4718596
  543.9 24.5 %copy-start.5 = (f32[512,1536]{1,0:T(8,128)}, f32[512,1536]{1,0:T(8,128)S(1)}, u32[]{:S(2)}) copy-start(f32[512,1536]{1,0:T(8,128)S(1)} %get-tuple-element.103) | copy-start | bytes 9437188
  543.9 20.5 %slice-start.7 = ((s8[4718592]{0:T(1024)(128)(4,1)}), s8[4194304]{0:T(1024)(128)(4,1)S(1)}, s32[]{:S(2)}) async-start(s8[4718592]{0:T(1024)(128)(4,1)} %bitcast.181), calls=%async_computation.16 | async-start | bytes 8388608
  545.5 18.9 %slice-start.8 = ((s8[4718592]{0:T(1024)(128)(4,1)}), s8[524288]{0:T(1024)(128)(4,1)S(1)}, s32[]{:S(2)}) async-start(s8[4718592]{0:T(1024)(128)(4,1)} %bitcast.181), calls=%async_computation.17 | async-start | bytes 1048576
  552.5 12.0 %copy-start.15 = (f32[512,1536]{1,0:T(8,128)S(1)}, f32[512,1536]{1,0:T(8,128)}, u32[]{:S(2)}) copy-start(f32[512,1536]{1,0:T(8,128)} %copy-done.14) | copy-start | bytes 9437188
  574.2 27.5 %all-to-all-start.2 = ((bf16[4,512,384]{2,1,0:T(8,128)(2,1)}), bf16[4,512,384]{2,1,0:T(8,128)(2,1)S(1)}, u32[]{:S(2)}, u32[]{:S(2)}) async-start(bf16[4,512,384]{2,1,0:T(8,128)(2,1)} %bitcast.142), calls=%async_computation.2 | async-start | bytes 3145728 | tf_op jit(solution)/shard_map/all_to_all | solution.py:1357
  634.9 71.8 %all-to-all-start.3 = ((bf16[4,512,1152]{2,1,0:T(8,128)(2,1)}), bf16[4,512,1152]{2,1,0:T(8,128)(2,1)}, u32[]{:S(2)}, u32[]{:S(2)}) async-start(bf16[4,512,1152]{2,1,0:T(8,128)(2,1)} %bitcast.152), calls=%async_computation.3 | async-start | bytes 9437184 | tf_op jit(solution)/shard_map/all_to_all | solution.py:1362
  640.2 444.4 %all-gather.8.cloned.1.call-start = ((), (), s32[]{:S(2)}) async-start(), calls=%async_computation.8 | async-start | bytes 2949120 | tf_op jit(solution)/shard_map/all_gather | solution.py:1342
  715.7 19.4 %copy-start.8 = (bf16[2,256,1536]{2,1,0:T(8,128)(2,1)S(1)}, bf16[2,256,1536]{2,1,0:T(8,128)(2,1)}, u32[]{:S(2)}) copy-start(bf16[2,256,1536]{2,1,0:T(8,128)(2,1)} %param.16) | copy-start | bytes 4718596
  715.7 19.4 %copy-start.33 = (f32[1536]{0:T(1024)S(1)}, f32[1536]{0:T(1024)}, u32[]{:S(2)}) copy-start(f32[1536]{0:T(1024)} %copy-done.32) | copy-start | bytes 18436
  715.7 19.4 %copy-start.37 = (f32[1,2,2,128]{3,1,2,0:T(2,128)S(1)}, f32[1,2,2,128]{3,1,2,0:T(2,128)}, u32[]{:S(2)}) copy-start(f32[1,2,2,128]{3,1,2,0:T(2,128)} %copy-done.36) | copy-start | bytes 6148
  735.1 12.1 %copy-start.39 = (f32[1,2,2,128]{3,1,2,0:T(2,128)S(1)}, f32[1,2,2,128]{3,1,2,0:T(2,128)}, u32[]{:S(2)}) copy-start(f32[1,2,2,128]{3,1,2,0:T(2,128)} %copy-done.38) | copy-start | bytes 6148
  735.1 12.1 %copy-start.35 = (f32[512]{0:T(512)S(1)}, f32[512]{0:T(512)}, u32[]{:S(2)}) copy-start(f32[512]{0:T(512)} %copy-done.34) | copy-start | bytes 6148
  1066.8 10.7 copy-start.29
  (34 other events, 172.1 us)
Sparse Core Ops, SparseCore 0:
  120.4 154.9 all-gather.3
  278.9 190.7 all-gather.5
  501.3 233.6 reduce-scatter.1
  736.5 36.1 all-gather.7

commit v4 on v3

--- a/solution.py
+++ b/solution.py
@@ -388,7 +388,7 @@
 Z_SHIFTS = [[(i, (i + 2 * k) % 8) for i in range(8)] for k in (1, 2, 3)]
 
 
-CHUNK = 768
+CHUNK = 384
 
 
 def gather_kernel(plan, has_vectors, *refs):
@@ -870,15 +870,20 @@
 
 
 PIECE = (192, 384)
-LAGS = (0, 1, 3, 4, 5, 6, 7)
+EARLY = 32
+OVER_X = 1
+STAGES = 7
+SLOTS = 6
 
 
 def sum_kernel(plan, weights, *refs):
     chunks = len(plan)
-    lefts, rights = refs[:weights], refs[weights : 2 * weights]
-    vector_in = refs[2 * weights]
-    outputs = refs[2 * weights + 1 : 3 * weights + 1]
-    vector_out = refs[3 * weights + 1]
+    late = chunks - 3
+    lefts, rights = refs[:weights], refs[weights : 2 * weights - 1]
+    refs = refs[2 * weights - 1 :]
+    heads_in, projection, hidden_in, grad_in, gain_in, vector_in = refs[:6]
+    outputs = refs[6 : 6 + weights]
+    heads, hidden_out, vector_out = refs[6 + weights : 9 + weights]
     (
         mine,
         c_out,
@@ -887,38 +892,53 @@
         y_in,
         second_in,
         z_in,
+        early_z_in,
+        early_y_in,
+        early_x_in,
         total,
         fx_in,
         fc_in,
         stage,
         left_buf,
         right_buf,
+        weight_buf,
+        normed_grad,
+        hidden,
+        grad,
+        gain,
         vector,
         vector_got,
         vector_z,
         c_sem,
-        first_sem,
-        second_sem,
+        x_sem,
+        y_sem,
+        second_x_sem,
+        second_y_sem,
         z_sem,
+        early_sem,
         fx_sem,
         fc_sem,
         stage_sem,
         load_sem,
         vector_sem,
-    ) = refs[3 * weights + 2 :]
+        heads_sem,
+        own_sem,
+    ) = refs[9 + weights :]
+    rights = rights + (heads,)
     seq = lax.axis_index("seq")
     fsdp = lax.axis_index("fsdp")
     x, c = seq // 2, seq % 2
     z, y = fsdp // 2, fsdp % 2
     x_device = (2 * (1 - x) + c, fsdp)
     c_device = (2 * x + 1 - c, fsdp)
+    far_device = (3 - seq, fsdp)
     y_device = (seq, 2 * z + 1 - y)
 
     def z_device(k):
         return (seq, 2 * ((z + k) % 4) + y)
 
     barrier = pltpu.get_barrier_semaphore()
-    partners = [x_device, c_device, y_device] + [z_device(k) for k in (1, 2, 3)]
+    partners = [x_device, c_device, far_device, y_device] + [z_device(k) for k in (1, 2, 3)]
     for partner in partners:
         pl.semaphore_signal(barrier, inc=1, device_id=partner, device_id_type=MESH)
     pl.semaphore_wait(barrier, len(partners))
@@ -933,8 +953,41 @@
             device_id_type=MESH,
         )
 
-    def x_first(i):
-        return i % 2 == 0
+    def columns(block):
+        return pl.ds(pl.multiple_of(block * 384, 128), 384)
+
+    neighbours = (x_device, c_device, far_device)
+
+    def heads_send(which, kind):
+        return remote(
+            heads_in.at[neighbours[which][0], :, pl.ds(kind * 384, 384)],
+            heads.at[:, columns(kind * 4 + seq)],
+            heads_sem.at[:, which, kind],
+            neighbours[which],
+        )
+
+    def heads_arrival(which, kind):
+        region = heads.at[:, columns(kind * 4 + neighbours[which][0])]
+        return remote(region, region, heads_sem.at[:, which, kind], neighbours[which])
+
+    def heads_own(kind):
+        return pltpu.make_async_copy(
+            heads_in.at[seq, :, pl.ds(kind * 384, 384)],
+            heads.at[:, columns(kind * 4 + seq)],
+            own_sem.at[kind],
+        )
+
+    def whole(kind):
+        return pltpu.make_async_copy(
+            projection.at[:, pl.ds(kind * 1536, 1536)], weight_buf, own_sem.at[3]
+        )
+
+    operands = [
+        pltpu.make_async_copy(hidden_in, hidden, own_sem.at[4]),
+        pltpu.make_async_copy(grad_in, grad, own_sem.at[5]),
+        pltpu.make_async_copy(gain_in, gain, own_sem.at[6]),
+        pltpu.make_async_copy(vector_in, vector.at[0], own_sem.at[7]),
+    ]
 
     def loads(j):
         weight, column = plan[j]
@@ -951,6 +1004,10 @@
 
             @pl.when(i == j)
             def _():
+                if j >= late:
+                    heads_own(j - late).wait()
+                    for which in range(3):
+                        heads_arrival(which, j - late).wait_recv()
                 for copy in loads(j):
                     copy.start()
 
@@ -961,9 +1018,6 @@
             def _():
                 for copy in loads(j):
                     copy.wait()
-
-    def columns(block):
-        return pl.ds(pl.multiple_of(block * 384, 128), 384)
 
     def multiply(i, half, target, slot):
         buffer = i % 2
@@ -976,44 +1030,134 @@
                 for yy in range(2):
                     target[slot, q, zz, yy] = out[192 * yy : 192 * yy + 192, 384 * q : 384 * q + 384]
 
-    def add_to(slot, q, zz, yy, other):
-        here = mine[slot, q, zz, yy].astype(F32)
-        mine[slot, q, zz, yy] = (here + other.astype(F32)).astype(BF16)
+    def multiply_back(i):
+        for kind in range(3):
+
+            @pl.when(i == late + kind)
+            def _():
+                whole(kind).wait()
+
+                @pl.loop(0, right_buf.shape[1] // 128)
+                def _(block):
+                    rows = pl.ds(pl.multiple_of(block * 128, 128), 128)
+                    term = across(right_buf[i % 2, rows, :], weight_buf[...])
+                    if kind:
+                        normed_grad[rows, :] += term
+                    else:
+                        normed_grad[rows, :] = term
+
+                if kind < 2:
+                    whole(kind + 1).start()
+
+    def norm_back():
+        for copy in operands:
+            copy.wait()
+
+        def block(index, terms):
+            rows = pl.ds(pl.multiple_of(index * 32, 32), 32)
+            value = hidden[rows, :].astype(F32)
+            center = value - jnp.mean(value, axis=1, keepdims=True)
+            inverse = lax.rsqrt(jnp.mean(center * center, axis=1, keepdims=True) + 1e-05)
+            normed = center * inverse
+            change = normed_grad[rows, :]
+            scaled = change * gain[0:1, :]
+            first_mean = jnp.mean(scaled, axis=1, keepdims=True)
+            second_mean = jnp.mean(scaled * normed, axis=1, keepdims=True)
+            grad[rows, :] += inverse * (scaled - first_mean - normed * second_mean)
+            gains, biases = terms
+            return (
+                gains + jnp.sum(change * normed, axis=0, keepdims=True),
+                biases + jnp.sum(change, axis=0, keepdims=True),
+            )
+
+        zero = jnp.zeros((1, gain.shape[1]), F32)
+        gains, biases = lax.fori_loop(0, hidden.shape[0] // 32, block, (zero, zero))
+        vector[0, 0:1, :] = gains
+        vector[0, 1:2, :] = biases
+
+    def add_to(slot, q, zz, yy, rows, other):
+        here = mine[slot, q, zz, yy, rows].astype(F32)
+        mine[slot, q, zz, yy, rows] = (here + other.astype(F32)).astype(BF16)
+
+    early_rows = pl.ds(0, EARLY)
+    other_rows = pl.ds(EARLY, PIECE[0] - EARLY)
 
     def c_copy(i):
         return remote(c_out.at[i % 2], c_in.at[i % 2], c_sem.at[:, i % 2], c_device)
 
-    def x_copy(i):
-        slot = i // 2 % 2
-        return remote(mine.at[i % 5, 1 - x], x_in.at[slot], first_sem.at[:, i % 4], x_device)
-
-    def y_copy(i):
-        slot = i // 2 % 2
-        return remote(mine.at[i % 5, :, :, 1 - y], y_in.at[slot], first_sem.at[:, i % 4], y_device)
-
-    def second_y_copy(i):
-        slot = i % 4
-        return remote(mine.at[i % 5, x, :, 1 - y], second_in.at[slot], second_sem.at[:, slot], y_device)
-
-    def second_x_copy(i):
-        slot = i % 4
-        return remote(mine.at[i % 5, 1 - x, :, y], second_in.at[slot], second_sem.at[:, slot], x_device)
+    def x_copy(i, count):
+        region = pl.ds(0, count)
+        return remote(
+            mine.at[i % 5, 1 - x, region, :, other_rows],
+            x_in.at[i % 4, region],
+            x_sem.at[:, i % 4],
+            x_device,
+        )
+
+    def y_copy(i, count):
+        return remote(
+            mine.at[i % 5, :, pl.ds(count, 4 - count), 1 - y, other_rows],
+            y_in.at[i % 4, :, pl.ds(0, 4 - count)],
+            y_sem.at[:, i % 4],
+            y_device,
+        )
+
+    def second_y_copy(i, count):
+        region = pl.ds(0, count)
+        return remote(
+            mine.at[i % 5, x, region, 1 - y, other_rows],
+            second_in.at[i % 5, region],
+            second_y_sem.at[:, i % 5],
+            y_device,
+        )
+
+    def second_x_copy(i, count):
+        region = pl.ds(count, 4 - count)
+        return remote(
+            mine.at[i % 5, 1 - x, region, y, other_rows],
+            second_in.at[i % 5, region],
+            second_x_sem.at[:, i % 5],
+            x_device,
+        )
 
     def z_copy(i, k):
-        slot = i % 4
         return remote(
-            mine.at[i % 5, x, (z + k) % 4, y],
-            z_in.at[slot, k - 1],
-            z_sem.at[:, slot, k - 1],
+            mine.at[i % 5, x, (z + k) % 4, y, other_rows],
+            z_in.at[i % 4, k - 1],
+            z_sem.at[:, i % 4, k - 1],
             z_device(k),
         )
 
+    def early_z_copy(i, k):
+        return remote(
+            mine.at[i % 5, :, (z + k) % 4, :, early_rows],
+            early_z_in.at[i % 4, k - 1],
+            early_sem.at[:, i % 4, k - 1],
+            z_device(k),
+        )
+
+    def early_y_copy(i):
+        return remote(
+            mine.at[i % 5, :, z, 1 - y, early_rows],
+            early_y_in.at[i % 4],
+            early_sem.at[:, i % 4, 3],
+            y_device,
+        )
+
+    def early_x_copy(i):
+        return remote(
+            mine.at[i % 5, 1 - x, z, y, early_rows],
+            early_x_in.at[i % 4],
+            early_sem.at[:, i % 4, 4],
+            x_device,
+        )
+
     def fx_copy(i):
-        slot = i % 4
+        slot = i % SLOTS
         return remote(total.at[slot], fx_in.at[slot], fx_sem.at[:, slot], x_device)
 
     def fc_copy(i, which):
-        slot = i % 4
+        slot = i % SLOTS
         source = fx_in.at[slot] if which else total.at[slot]
         return remote(source, fc_in.at[slot, which], fc_sem.at[:, slot, which], c_device)
 
@@ -1027,90 +1171,114 @@
         multiply(i, 1 - c, c_out, i % 2)
         c_copy(i).start()
         multiply(i, c, mine, i % 5)
+        multiply_back(i)
 
     def first(i):
-        slot = i % 5
-        got = i % 2
         c_copy(i).wait_recv()
 
-        @pl.when(x_first(i))
-        def _():
-            for q, last in ((1 - x, False), (x, True)):
-
-                @pl.loop(0, 4)
+        def add_c(q, zz, yy, rows):
+            add_to(i % 5, q, zz, yy, rows, c_in[i % 2, q, zz, yy, rows])
+
+        for k in (1, 2, 3):
+            for q in range(2):
+                for yy in range(2):
+                    add_c(q, (z + k) % 4, yy, early_rows)
+            early_z_copy(i, k).start()
+
+        def run(i, count):
+            @pl.loop(0, count)
+            def _(zz):
+                for yy in range(2):
+                    add_c(1 - x, zz, yy, other_rows)
+
+            x_copy(i, count).start()
+
+            @pl.loop(count, 4)
+            def _(zz):
+                for q in range(2):
+                    add_c(q, zz, 1 - y, other_rows)
+
+            y_copy(i, count).start()
+
+            @pl.loop(0, count)
+            def _(zz):
+                for yy in range(2):
+                    add_c(x, zz, yy, other_rows)
+
+            @pl.loop(count, 4)
+            def _(zz):
+                for q in range(2):
+                    add_c(q, zz, y, other_rows)
+
+        run(i, OVER_X)
+        for q in range(2):
+            for yy in range(2):
+                add_c(q, z, yy, early_rows)
+
+    def second(i):
+        own, slot = i % 5, i % 4
+
+        def run(i, count):
+            def add_x(yy):
+                @pl.loop(0, count)
                 def _(zz):
-                    for yy in range(2):
-                        add_to(slot, q, zz, yy, c_in[got, q, zz, yy])
-
-                if not last:
-                    x_copy(i).start()
-
-        @pl.when(jnp.logical_not(x_first(i)))
-        def _():
-            for yy, last in ((1 - y, False), (y, True)):
-
-                @pl.loop(0, 4)
+                    add_to(own, x, zz, yy, other_rows, x_in[slot, zz, yy])
+
+            def add_y(q):
+                @pl.loop(count, 4)
                 def _(zz):
-                    for q in range(2):
-                        add_to(slot, q, zz, yy, c_in[got, q, zz, yy])
-
-                if not last:
-                    y_copy(i).start()
-
-    def second(i):
-        slot = i % 5
-        got = i // 2 % 2
-
-        @pl.when(x_first(i))
-        def _():
-            x_copy(i).wait()
-            for yy, last in ((1 - y, False), (y, True)):
-
-                @pl.loop(0, 4)
-                def _(zz):
-                    add_to(slot, x, zz, yy, x_in[got, zz, yy])
-
-                if not last:
-                    second_y_copy(i).start()
-
-        @pl.when(jnp.logical_not(x_first(i)))
-        def _():
-            y_copy(i).wait()
-            for q, last in ((1 - x, False), (x, True)):
-
-                @pl.loop(0, 4)
-                def _(zz):
-                    add_to(slot, q, zz, y, y_in[got, q, zz])
-
-                if not last:
-                    second_x_copy(i).start()
+                    add_to(own, q, zz, y, other_rows, y_in[slot, q, zz - count])
+
+            x_copy(i, count).wait()
+            add_x(1 - y)
+            second_y_copy(i, count).start()
+            y_copy(i, count).wait()
+            add_y(1 - x)
+            second_x_copy(i, count).start()
+            add_x(y)
+            add_y(x)
+
+        run(i, OVER_X)
+        for k in (1, 2, 3):
+            early_z_copy(i, k).wait()
+
+        def add_early(q, yy):
+            others = [early_z_in[slot, k, q, yy].astype(F32) for k in range(3)]
+            add_to(own, q, z, yy, early_rows, others[0] + others[1] + others[2])
+
+        for q in range(2):
+            add_early(q, 1 - y)
+        early_y_copy(i).start()
+        for q in range(2):
+            add_early(q, y)
 
     def third(i):
-        slot = i % 4
-
-        @pl.when(x_first(i))
-        def _():
-            second_y_copy(i).wait()
-
-        @pl.when(jnp.logical_not(x_first(i)))
-        def _():
-            second_x_copy(i).wait()
-
+        own, slot = i % 5, i % 4
+
+        def run(i, count):
+            second_y_copy(i, count).wait()
+            second_x_copy(i, count).wait()
+
+        run(i, OVER_X)
         for k in (1, 2, 3):
             zz = (z + k) % 4
-            add_to(i % 5, x, zz, y, second_in[slot, zz])
+            add_to(own, x, zz, y, other_rows, second_in[own, zz])
             z_copy(i, k).start()
-
-    def put(i, quarter, value):
-        stage[i % 2, :, columns(quarter)] = value
+        early_y_copy(i).wait()
+        add_to(own, 1 - x, z, y, early_rows, early_y_in[slot, 1 - x])
+        early_x_copy(i).start()
+        add_to(own, x, z, y, early_rows, early_y_in[slot, x])
 
     def fourth(i):
-        slot = i % 4
-        result = mine[i % 5, x, z, y].astype(F32) + second_in[slot, z].astype(F32)
+        own, slot = i % 5, i % 4
+        result = mine[own, x, z, y, other_rows].astype(F32) + second_in[own, z].astype(F32)
         for k in (1, 2, 3):
             z_copy(i, k).wait()
             result = result + z_in[slot, k - 1].astype(F32)
-        total[slot] = result.astype(BF16)
+        total[i % SLOTS, other_rows] = result.astype(BF16)
+        early_x_copy(i).wait()
+        result = mine[own, x, z, y, early_rows].astype(F32) + early_x_in[slot].astype(F32)
+        total[i % SLOTS, early_rows] = result.astype(BF16)
         fx_copy(i).start()
         fc_copy(i, 0).start()
 
@@ -1125,19 +1293,22 @@
         )
 
     def sixth(i):
-        slot = i % 4
+        slot = i % SLOTS
         for j in range(2, chunks):
 
             @pl.when(i == j)
             def _():
                 store(j - 2).wait()
 
+        def put(quarter, value):
+            stage[i % 2, :, columns(quarter)] = value
+
         fc_copy(i, 0).wait()
         fc_copy(i, 1).wait()
-        put(i, 2 * c + x, total[slot])
-        put(i, 2 * c + 1 - x, fx_in[slot])
-        put(i, 2 * (1 - c) + x, fc_in[slot, 0])
-        put(i, 2 * (1 - c) + 1 - x, fc_in[slot, 1])
+        put(2 * c + x, total[slot])
+        put(2 * c + 1 - x, fx_in[slot])
+        put(2 * (1 - c) + x, fc_in[slot, 0])
+        put(2 * (1 - c) + 1 - x, fc_in[slot, 1])
         for j in range(chunks):
 
             @pl.when(i == j)
@@ -1155,15 +1326,18 @@
         source = (z + 4 - k) % 4
         return remote(vector_z.at[source], vector_z.at[source], vector_sem.at[:, 2 + k], z_device(k))
 
-    def vector_step(t):
-        @pl.when(t == 0)
+    hidden_store = pltpu.make_async_copy(grad, hidden_out, own_sem.at[5])
+
+    def vector_step(step):
+        @pl.when(step == 0)
         def _():
-            pltpu.sync_copy(vector_in, vector.at[0])
+            norm_back()
+            hidden_store.start()
             vector_copy(0).start()
 
         for leg in range(3):
 
-            @pl.when(t == leg + 1)
+            @pl.when(step == leg + 1)
             def _():
                 vector_copy(leg).wait()
                 both = vector[leg] + vector_got[leg]
@@ -1175,7 +1349,7 @@
                     for k in (1, 2, 3):
                         vector_z_copy(k).start()
 
-        @pl.when(t == 4)
+        @pl.when(step == 4)
         def _():
             for k in (1, 2, 3):
                 vector_z_copy(k).wait_send()
@@ -1184,82 +1358,112 @@
             pltpu.sync_copy(vector.at[0], vector_out)
 
     start_loads(0)
-
-    @pl.loop(0, chunks + LAGS[-1])
+    for kind in range(3):
+        heads_own(kind).start()
+        for which in range(3):
+            heads_send(which, kind).start()
+    whole(0).start()
+    for copy in operands:
+        copy.start()
+
+    @pl.loop(0, chunks + STAGES - 1)
     def _(t):
         @pl.when(t + 1 < chunks)
         def _():
             start_loads(t + 1)
 
-        stages = (begin, first, second, third, fourth, fifth, sixth)
-        for lag, run in zip(LAGS[::-1], stages[::-1]):
+        for lag, run in ((1, first), (0, begin), (2, second), (3, third), (4, fourth), (5, fifth), (6, sixth)):
             i = t - lag
 
             @pl.when(jnp.logical_and(i >= 0, i < chunks))
             def _():
                 run(i)
 
-        vector_step(t)
+        vector_step(t - chunks)
 
     for j in (chunks - 2, chunks - 1):
         c_copy(j).wait_send()
         store(j).wait()
-
-
-def sum_products(products, vectors):
-    lefts = [left for left, _ in products]
-    rights = [right for _, right in products]
+    for kind in range(3):
+        for which in range(3):
+            heads_send(which, kind).wait_send()
+    hidden_store.wait()
+
+
+def sum_products(lefts, rights, heads, projection, hidden, grad, gain, vectors):
+    weights = len(lefts)
+    widths = [right.shape[1] for right in rights] + [projection.shape[1]]
     plan = [
         (weight, column)
-        for weight, right in enumerate(rights)
-        for column in range(0, right.shape[1], 1536)
+        for weight, width in enumerate(widths)
+        for column in range(0, width, 1536)
     ]
+    depth, width = hidden.shape
     out_shapes = [
-        jax.ShapeDtypeStruct((left.shape[1] // 8, right.shape[1]), BF16) for left, right in products
+        jax.ShapeDtypeStruct((left.shape[1] // 8, columns), BF16)
+        for left, columns in zip(lefts, widths)
     ]
-    out_shapes.append(jax.ShapeDtypeStruct(vectors.shape, F32))
-    depth = lefts[0].shape[0]
+    out_shapes += [
+        jax.ShapeDtypeStruct((depth, widths[-1]), BF16),
+        jax.ShapeDtypeStruct(grad.shape, F32),
+        jax.ShapeDtypeStruct(vectors.shape, F32),
+    ]
+    inputs = (*lefts, *rights, heads, projection, hidden, grad, gain, vectors)
     anywhere = pl.BlockSpec(memory_space=pl.ANY)
     dma = pltpu.SemaphoreType.DMA
-    block = lambda *lead: pltpu.VMEM(lead + PIECE, BF16)
-    *sums, total = pl.pallas_call(
-        functools.partial(sum_kernel, tuple(plan), len(products)),
+    rest = PIECE[0] - EARLY
+    block = lambda *lead, rows=PIECE[0]: pltpu.VMEM(lead + (rows, PIECE[1]), BF16)
+    results = pl.pallas_call(
+        functools.partial(sum_kernel, tuple(plan), weights),
         out_shape=out_shapes,
-        in_specs=[anywhere] * (2 * len(products) + 1),
+        in_specs=[anywhere] * len(inputs),
         out_specs=[anywhere] * len(out_shapes),
         scratch_shapes=[
             block(5, 2, 4, 2),
             block(2, 2, 4, 2),
             block(2, 2, 4, 2),
-            block(2, 4, 2),
-            block(2, 2, 4),
-            block(4, 4),
-            block(4, 3),
-            block(4),
-            block(4),
-            block(4, 2),
+            block(4, OVER_X, 2, rows=rest),
+            block(4, 2, 4 - OVER_X, rows=rest),
+            block(5, 4, rows=rest),
+            block(4, 3, rows=rest),
+            block(4, 3, 2, 2, rows=EARLY),
+            block(4, 2, rows=EARLY),
+            block(4, rows=EARLY),
+            block(SLOTS),
+            block(SLOTS),
+            block(SLOTS, 2),
             pltpu.VMEM((2, 192, 1536), BF16),
             pltpu.VMEM((2, depth, 1536), BF16),
             pltpu.VMEM((2, depth, 1536), BF16),
+            pltpu.VMEM((width, 1536), BF16),
+            pltpu.VMEM((depth, width), F32),
+            pltpu.VMEM((depth, width), BF16),
+            pltpu.VMEM((depth, width), F32),
+            pltpu.VMEM(gain.shape, F32),
             pltpu.VMEM((3,) + vectors.shape, F32),
             pltpu.VMEM((3,) + vectors.shape, F32),
             pltpu.VMEM((4,) + vectors.shape, F32),
             dma((2, 2)),
             dma((2, 4)),
             dma((2, 4)),
+            dma((2, 5)),
+            dma((2, 5)),
             dma((2, 4, 3)),
-            dma((2, 4)),
-            dma((2, 4, 2)),
+            dma((2, 4, 5)),
+            dma((2, SLOTS)),
+            dma((2, SLOTS, 2)),
             dma((2,)),
             dma((2, 2)),
             dma((2, 6)),
+            dma((2, 3, 3)),
+            dma((8,)),
         ],
         compiler_params=pltpu.CompilerParams(
             collective_id=3, has_side_effects=True, vmem_limit_bytes=60 << 20
         ),
         name="sum_products",
-    )(*lefts, *rights, vectors)
-    return sums, total
+    )(*inputs)
+    return results[:weights], results[-2], results[-1]
 
 
 def on_blocks(
@@ -1297,8 +1501,7 @@
     gains = [vectors[:, i].reshape(width) for i in range(6)]
 
     hidden = hidden_states.reshape(rows, width).astype(F32)
-    normed_one, norm_one_back = jax.vjp(layer_norm, hidden, gains[0], gains[1])
-    normed_one = normed_one.astype(BF16)
+    normed_one = layer_norm(hidden, gains[0], gains[1]).astype(BF16)
     projected = product_blocks(normed_one, qkv_whole, 3, groups)
     regrouped = lax.all_to_all(projected, "seq", split_axis=0, concat_axis=0, tiled=True)
     regrouped = regrouped.reshape(groups, clips, frames, 3 * group_width)
@@ -1339,7 +1542,6 @@
     contract_part = lax.psum_scatter(
         contract_term, ("fsdp", "seq"), scatter_dimension=0, tiled=True
     )
-    contract_gradient = lax.all_gather(contract_part, "seq", axis=0, tiled=True)
     grad_activated = product_right(grad_mixed, contract_whole)
     grad_preact = (grad_activated * slope.astype(F32)).astype(BF16)
     grad_normed_three = product_right(grad_preact, expand_whole)
@@ -1354,12 +1556,8 @@
     grad_attended = grad_first.astype(BF16)
     grad_context = product_right(grad_attended, self_output_whole).astype(BF16)
     grad_context = grad_context.reshape(rows, groups, group_width).transpose(1, 0, 2)
+    grad_context, activated = lax.optimization_barrier((grad_context, activated))
     grad_heads = lax.all_to_all(grad_context, "seq", split_axis=0, concat_axis=0, tiled=True)
-    grad_heads = grad_heads.reshape(groups, clips, frames, group_width)
-    grad_regrouped = attention_back(regrouped, grad_heads, logsum, scale)
-    grad_regrouped, activated = lax.optimization_barrier((grad_regrouped, activated))
-    grad_regrouped = grad_regrouped.reshape(groups, rows, 3 * group_width)
-    grad_projected = lax.all_to_all(grad_regrouped, "seq", split_axis=0, concat_axis=0, tiled=True)
     mixed = product(activated, contract_whole)
     output = second + mixed
     squares = jnp.stack(
@@ -1371,42 +1569,38 @@
         ]
     )
     output = output.astype(BF16)
-    grad_projected, output, squares = lax.optimization_barrier((grad_projected, output, squares))
-    grad_projected = jnp.concatenate(
-        [
-            grad_projected[group, :, kind * group_width : (kind + 1) * group_width]
-            for kind in range(3)
-            for group in range(groups)
-        ],
-        1,
-    )
-    grad_normed_one = product_right(grad_projected, qkv_whole)
-    grad_hidden, gain_one_term, bias_one_term = norm_one_back(grad_normed_one)
-    grad_hidden = grad_first + grad_hidden
+    zeros = jnp.zeros_like(cross_gain_term)
     terms = jnp.stack(
         [
-            gain_one_term,
-            bias_one_term,
+            zeros,
+            zeros,
             cross_gain_term,
             cross_bias_term,
             final_gain_term,
             final_bias_term,
             jnp.pad(squares, (0, width - 4)),
-            jnp.zeros_like(gain_one_term),
+            zeros,
         ]
     )
     deep = lambda value: jnp.pad(value, ((0, rows - value.shape[0]), (0, 0)))
-    gradients, totals = sum_products(
-        [
-            (normed_three, grad_preact),
-            (cross_context, grad_crossed),
-            (normed_two, grad_cross_q),
-            (deep(text_rows), deep(grad_memory)),
-            (context, grad_attended),
-            (normed_one, grad_projected),
-        ],
+    text_operands = (deep(text_rows), deep(grad_memory))
+    grad_heads, output, terms, text_operands = lax.optimization_barrier(
+        (grad_heads, output, terms, text_operands)
+    )
+    grad_heads = grad_heads.reshape(groups, clips, frames, group_width)
+    grad_regrouped = attention_back(regrouped, grad_heads, logsum, scale)
+    gradients, grad_hidden, totals = sum_products(
+        [normed_three, cross_context, normed_two, text_operands[0], context, normed_one],
+        [grad_preact, grad_crossed, grad_cross_q, text_operands[1], grad_attended],
+        grad_regrouped.reshape(groups, rows, 3 * group_width),
+        qkv_whole,
+        hidden_states.reshape(rows, width),
+        grad_first,
+        jnp.broadcast_to(gains[0], (8, width)),
         terms,
     )
+    gradients, contract_part = lax.optimization_barrier((gradients, contract_part))
+    contract_gradient = lax.all_gather(contract_part, "seq", axis=0, tiled=True)
     gradients = [gradient.astype(F32) for gradient in gradients]
     contract_gradient = contract_gradient.astype(F32)
     layer_rms = jnp.sqrt(totals[6, :4] / entries)

time: 1100 us -> 971 us (0.88)
  waiting for transfers between devices: 104 us -> 38.8 us
  Pallas kernels: 671 us -> 639 us
  local copies, waits for them, and re-layouts: 44.2 us -> 25.8 us
  matrix products: 130 us -> 118 us
    all_to_all x1 -> x0, waiting for transfers between devices: 46 us -> none  [on_blocks(): lax.all_to_all(grad_regrouped, 'seq', split_axis=0, concat_axis=0, tiled=...]
    pallas_call x2, Pallas kernels: 272 us -> 253 us  [gather_weights(): pl.pallas_call(functools.partial(gather_kernel, plan, vectors is not None...]
    unnamed x115 -> x79, local copies, waits for them, and re-layouts: 25.6 us -> 8.14 us
    pallas_call x1, Pallas kernels: 317 us -> 303 us  [sum_products(): pl.pallas_call(functools.partial(sum_kernel, tuple(plan), weights), out_s...]
    all_to_all x1, waiting for transfers between devices: 19.4 us -> 5.67 us  [on_blocks(): lax.all_to_all(grad_context, 'seq', split_axis=0, concat_axis=0, tiled=True)]
    dot_general x6 -> x5, matrix products: 62.9 us -> 51.4 us  [product_right(): lax.dot_general(left, right, (((1,), (1,)), ((), ())), preferred_element_...]
  transfers between devices with their start and end apart: 7 -> 6, of which waited for: 5 -> 4; matrix products, arithmetic and copies ran while one was open for 18% -> 16% of each run, Pallas kernels for 51% -> 56%
where the time goes in v4:
time: 971 us; the launch traced here: 964 us
  Pallas kernels  639 us (66%)
  matrix products  118 us (12%)
  blocking collectives  84.8 us (9%)
  waiting for transfers between devices  38.8 us (4%)
  other arithmetic  34 us (4%)
  local copies, waits for them, and re-layouts  25.8 us (3%)
  between operations  14.7 us (2%)
    pallas_call x1, Pallas kernels, sum_products(): pl.pallas_call(functools.partial(sum_kernel, tuple(plan), weights), out_s...  303 us
    pallas_call x2, Pallas kernels, gather_weights(): pl.pallas_call(functools.partial(gather_kernel, plan, vectors is not None...  253 us
    all_to_all x1, blocking collectives, on_blocks(): lax.all_to_all(projected, 'seq', split_axis=0, concat_axis=0, tiled=True)  84.8 us
    dot_general x5, matrix products, product_right(): lax.dot_general(left, right, (((1,), (1,)), ((), ())), preferred_element_...  51.4 us
    dot_general x6, matrix products, product(): return jnp.dot(left, right, preferred_element_type=jnp.float32)  50.4 us
    pallas_call x1, Pallas kernels, attention_back(): pl.pallas_call(functools.partial(attention_back_kernel, scale), grid=(cli...  33.3 us
    pallas_call x1, Pallas kernels, attention(): pl.pallas_call(functools.partial(attention_kernel, scale), grid=(clips, p...  20.1 us
    all_to_all x1, waiting for transfers between devices, on_blocks(): lax.all_to_all(context_heads, 'seq', split_axis=0, concat_axis=0, tiled=T...  20 us
  transfers between devices with their start and end apart: 6, of which 4 were waited for; matrix products, arithmetic and copies ran while one was open for 16% of the time, Pallas kernels for 56%

profile of v4, /device:TPU:0, one launch (start us, length us, event | category | flops | bytes accessed | tf_op | source)
XLA Modules:
  0.0 963.9 jit_solution(10143121897645250079)
XLA Ops:
  12.0 100.4 %gather_weights.2 = (bf16[4,2,1,4,48,4608]{5,4,3,2,1,0:T(8,128)(2,1)}, bf16[4,2,1,4,48,1536]{5,4,3,2,1,0:T(8,128)(2,1)}, f32[8,8,256]{2,1,0:T(8,128)}) custom-call(bf16[1,4,48,4608]{3,2,1,0:T(8,128)(2,1)} %bitcast.104, bf16[1,4,48,1536]{3,2,1,0:T(8,128)(2,1)} %bitcast.107, f32[8,256]{1,0:T(8,128)} %pad_convert_fusion.refs_2_), custom_call_target="tpu_custom_call" | custom-call | tf_op jit(solution)/shard_map/gather_weights/pallas_call | solution.py:567
  117.6 14.1 %product_blocks.1 = bf16[4,512,1152]{2,1,0:T(8,128)(2,1)} custom-call(bf16[512,1536]{1,0:T(8,128)(2,1)S(1)} %fusion.4.left.refs_5_, bf16[1536,4608]{1,0:T(8,128)(2,1)} %bitcast.80, bf16[1536,4608]{1,0:T(8,128)(2,1)} %bitcast.81, bf16[1536,4608]{1,0:T(8,128)(2,1)} %bitcast.82), custom_call_target="tpu_custom_call" | custom-call | flops 7247757312 | bytes 20447232 | tf_op jit(solution)/shard_map/product_blocks/pallas_call | solution.py:616
  131.8 84.8 %all_to_all.15 = bf16[4,512,1152]{2,1,0:T(8,128)(2,1)} all-to-all(bf16[4,512,1152]{2,1,0:T(8,128)(2,1)} %product_blocks.1), channel_id=1, replica_groups=mesh['seq'=4,'fsdp'=8] {'seq'}, dimensions={0} | all-to-all | bytes 9437184 | tf_op jit(solution)/shard_map/all_to_all | solution.py:1506
  216.5 20.1 %attention.1 = (bf16[4,2,256,384]{3,2,1,0:T(8,128)(2,1)}, f32[2,3,2,1024]{3,2,1,0:T(2,128)S(1)}) custom-call(bf16[4,2,256,1152]{3,2,1,0:T(8,128)(2,1)} %bitcast.95, bf16[4,2,256,1152]{3,2,1,0:T(8,128)(2,1)} %bitcast.96, bf16[4,2,256,1152]{3,2,1,0:T(8,128)(2,1)} %bitcast.97), custom_call_target="tpu_custom_call" | custom-call | flops 6442450944 | bytes 6291456 | tf_op jit(solution)/shard_map/attention/pallas_call | solution.py:700
  236.7 3.6 all-to-all-start.1
  240.3 20.0 %all-to-all-done.1 = bf16[4,512,384]{2,1,0:T(8,128)(2,1)S(1)} async-done(((bf16[4,512,384]{2,1,0:T(8,128)(2,1)}), bf16[4,512,384]{2,1,0:T(8,128)(2,1)S(1)}, u32[]{:S(2)}, u32[]{:S(2)}) %all-to-all-start.1) | async-done | bytes 1572896 | tf_op jit(solution)/shard_map/all_to_all | solution.py:1510
  260.3 3.8 all-gather.4.cloned.1.call-done
  268.2 152.6 %gather_weights.3 = (bf16[4,2,1,4,48,1536]{5,4,3,2,1,0:T(8,128)(2,1)}, bf16[4,2,1,4,48,3072]{5,4,3,2,1,0:T(8,128)(2,1)}, bf16[4,2,1,4,48,1536]{5,4,3,2,1,0:T(8,128)(2,1)}) custom-call(bf16[1,4,48,1536]{3,2,1,0:T(8,128)(2,1)} %bitcast.108, bf16[1,4,48,3072]{3,2,1,0:T(8,128)(2,1)} %bitcast.106, bf16[1,4,48,1536]{3,2,1,0:T(8,128)(2,1)} %bitcast.109), custom_call_target="tpu_custom_call" | custom-call | tf_op jit(solution)/shard_map/gather_weights/pallas_call | solution.py:567
  420.8 5.6 fusion.15
  442.3 19.5 %multiply_convert_fusion.1 = (bf16[512,6144]{1,0:T(8,128)(2,1)}, f32[512,6144]{1,0:T(8,128)}) fusion(bf16[512,1536]{1,0:T(8,128)(2,1)S(1)} %add_convert_fusion.1.refs_0_, bf16[1536,6144]{1,0:T(8,128)(2,1)} %all-gather.4.cloned.1.call-done), kind=kOutput, calls=%fused_computation.3 | convolution fusion | flops 9679405056 | bytes 39321600 | tf_op jit(solution)/shard_map/dot_general | solution.py:31
  461.9 16.0 %convolution_convert_fusion = bf16[6144,1536]{1,0:T(8,128)(2,1)} fusion(bf16[512,6144]{1,0:T(8,128)(2,1)} %get-tuple-element.78, bf16[512,1536]{1,0:T(8,128)(2,1)S(1)} %bitcast.93), kind=kOutput, calls=%fused_computation | convolution fusion | flops 9673113600 | bytes 26738688 | tf_op jit(solution)/shard_map/dot_general | solution.py:35
  480.1 20.5 %multiply_convert_fusion.refs_6_ = bf16[512,6144]{1,0:T(8,128)(2,1)} fusion(bf16[512,1536]{1,0:T(8,128)(2,1)} %bitcast.92, bf16[6144,1536]{1,0:T(8,128)(2,1)} %all-gather.6.cloned.1.call-done, f32[512,6144]{1,0:T(8,128)} %get-tuple-element.138), kind=kOutput, calls=%fused_computation.1 | convolution fusion | flops 9701425152 | bytes 39321600 | tf_op jit(solution)/shard_map/dot_general | solution.py:41
  500.6 19.3 %multiply_reduce_fusion.4 = (f32[1536]{0:T(1024)S(1)}, f32[512]{0:T(512)S(1)}, f32[1536]{0:T(1024)S(1)}, f32[512,1536]{1,0:T(8,128)}) fusion(f32[512,1536]{1,0:T(8,128)} %copy-done.5, f32[512]{0:T(512)S(1)} %fusion.9, f32[512]{0:T(512)S(1)} %broadcast_multiply_fusion, f32[1536]{0:T(1024)S(1)} %mul.202, bf16[512,6144]{1,0:T(8,128)(2,1)} %multiply_convert_fusion.refs_6_, ...), kind=kOutput, calls=%fused_computation.23 | convolution fusion | flops 9669963776 | bytes 31481856 | tf_op jit(solution)/shard_map/dot_general | solution.py:41
  519.9 4.3 fusion.13
  525.8 6.0 convolution_convert_fusion.3.grad_ref
  531.8 11.9 %text_attention_back.1 = (bf16[512,1536]{1,0:T(8,128)(2,1)S(1)}, bf16[128,3072]{1,0:T(8,128)(2,1)S(1)}) custom-call(bf16[512,1536]{1,0:T(8,128)(2,1)S(1)} %convolution_convert_fusion.4.q_ref, bf16[128,3072]{1,0:T(8,128)(2,1)S(1)} %fusion.memory_ref, bf16[512,1536]{1,0:T(8,128)(2,1)S(1)} %convolution_convert_fusion.3.grad_ref), custom_call_target="tpu_custom_call" | custom-call | flops 1006632960 | bytes 6291456 | tf_op jit(solution)/shard_map/text_attention_back/pallas_call | solution.py:855
  554.1 5.4 all-to-all-start.2
  559.6 17.8 %multiply_reduce_fusion.3 = (f32[]{:T(128)}, f32[]{:T(128)}, bf16[512,1536]{1,0:T(8,128)(2,1)}) fusion(f32[512,1536]{1,0:T(8,128)} %copy-done.5, bf16[512,6144]{1,0:T(8,128)(2,1)} %get-tuple-element.78, bf16[6144,1536]{1,0:T(8,128)(2,1)} %all-gather.6.cloned.1.call-done), kind=kOutput, calls=%fused_computation.22 | convolution fusion | flops 9668395008 | bytes 29884424 | tf_op jit(solution)/shard_map/dot_general | solution.py:31
  582.8 5.7 all-to-all-done.2
  588.5 33.3 %attention_back.1 = bf16[4,2,256,1152]{3,2,1,0:T(8,128)(2,1)} custom-call(bf16[4,2,256,1152]{3,2,1,0:T(8,128)(2,1)} %bitcast.98, bf16[4,2,256,1152]{3,2,1,0:T(8,128)(2,1)} %bitcast.99, bf16[4,2,256,1152]{3,2,1,0:T(8,128)(2,1)} %bitcast.100, bf16[4,2,256,384]{3,2,1,0:T(8,128)(2,1)S(1)} %bitcast.79, f32[2,3,2,1024]{3,2,1,0:T(2,128)S(1)} %get-tuple-element.84.logsum_ref), custom_call_target="tpu_custom_call" | custom-call | flops 16106127360 | bytes 11010048 | tf_op jit(solution)/shard_map/attention_back/pallas_call | solution.py:782
  622.4 303.2 %sum_products.1 = (bf16[192,6144]{1,0:T(8,128)(2,1)}, bf16[192,1536]{1,0:T(8,128)(2,1)}, bf16[192,1536]{1,0:T(8,128)(2,1)}, bf16[192,3072]{1,0:T(8,128)(2,1)}, b...) custom-call(bf16[512,1536]{1,0:T(8,128)(2,1)} %copy-done.11, ...), custom_call_target="tpu_custom_call" | custom-call | tf_op jit(solution)/shard_map/sum_products/pallas_call | solution.py:1416
  928.5 4.5 convert_element_type.116
  940.3 9.2 all-gather.8.cloned.1.call-done
  949.5 4.6 convert_element_type.117
  (158 shorter events, 63.0 us)
Async XLA Ops:
  7.2 105.2 %copy-start = (bf16[192,6144]{1,0:T(8,128)(2,1)S(1)}, bf16[192,6144]{1,0:T(8,128)(2,1)}, u32[]{:S(2)}) copy-start(bf16[192,6144]{1,0:T(8,128)(2,1)} %param.29) | copy-start | bytes 7077892
  7.2 256.9 %all-gather.4.cloned.1.call-start = ((), (), s32[]{:S(2)}) async-start(), calls=%async_computation.4 | async-start | bytes 19464192 | tf_op jit(solution)/shard_map/all_gather | solution.py:595
  117.6 14.1 %copy-start.2 = (bf16[512,1536]{1,0:T(8,128)(2,1)}, bf16[512,1536]{1,0:T(8,128)(2,1)S(1)}, u32[]{:S(2)}) copy-start(bf16[512,1536]{1,0:T(8,128)(2,1)S(1)} %fusion.4.left.refs_5_) | copy-start | bytes 4718596
  236.7 23.6 %all-to-all-start.1 = ((bf16[4,512,384]{2,1,0:T(8,128)(2,1)}), bf16[4,512,384]{2,1,0:T(8,128)(2,1)S(1)}, u32[]{:S(2)}, u32[]{:S(2)}) async-start(bf16[4,512,384]{2,1,0:T(8,128)(2,1)} %bitcast.6), calls=%async_computation.1 | async-start | bytes 3145728 | tf_op jit(solution)/shard_map/all_to_all | solution.py:1510
  240.2 237.7 %all-gather.6.cloned.1.call-start = ((), (), s32[]{:S(2)}) async-start(), calls=%async_computation.5 | async-start | bytes 19464192 | tf_op jit(solution)/shard_map/all_gather | solution.py:595
  260.3 6.3 copy-start.14
  266.1 659.5 %reduce-scatter.2.cloned.1.call-start = ((), (), s32[]{:S(2)}) async-start(), calls=%async_computation.6 | async-start | bytes 19464192 | tf_op jit(solution)/shard_map/reduce_scatter | solution.py:1542
  268.2 158.2 %copy-start.9 = (bf16[4,64,8,384]{3,2,0,1:T(8,128)(2,1)}, bf16[4,64,8,384]{3,2,0,1:T(8,128)(2,1)S(1)}, u32[]{:S(2)}) copy-start(bf16[4,64,8,384]{3,2,0,1:T(8,128)(2,1)S(1)} %copy.40) | copy-start | bytes 4718596
  420.8 6.1 slice-start
  420.8 6.1 slice-start.1
  420.8 6.1 slice-start.2
  426.4 10.3 %copy-start.6 = (f32[512,1536]{1,0:T(8,128)}, f32[512,1536]{1,0:T(8,128)S(1)}, u32[]{:S(2)}) copy-start(f32[512,1536]{1,0:T(8,128)S(1)} %get-tuple-element.125) | copy-start | bytes 9437188
  426.4 4.6 slice-start.5
  429.2 7.5 slice-start.9
  431.0 5.8 slice-start.10
  442.3 19.6 %copy-start.11 = (bf16[512,1536]{1,0:T(8,128)(2,1)}, bf16[512,1536]{1,0:T(8,128)(2,1)S(1)}, u32[]{:S(2)}) copy-start(bf16[512,1536]{1,0:T(8,128)(2,1)S(1)} %add_convert_fusion.1.refs_0_) | copy-start | bytes 4718596
  442.3 19.6 %copy-start.15 = (bf16[2,256,1536]{2,1,0:T(8,128)(2,1)S(1)}, bf16[2,256,1536]{2,1,0:T(8,128)(2,1)}, u32[]{:S(2)}) copy-start(bf16[2,256,1536]{2,1,0:T(8,128)(2,1)} %param.31) | copy-start | bytes 4718596
  524.2 19.6 %slice-start.7 = ((s8[4718592]{0:T(1024)(128)(4,1)}), s8[4194304]{0:T(1024)(128)(4,1)S(1)}, s32[]{:S(2)}) async-start(s8[4718592]{0:T(1024)(128)(4,1)} %bitcast.125), calls=%async_computation.15 | async-start | bytes 8388608
  525.8 18.0 %slice-start.8 = ((s8[4718592]{0:T(1024)(128)(4,1)}), s8[524288]{0:T(1024)(128)(4,1)S(1)}, s32[]{:S(2)}) async-start(s8[4718592]{0:T(1024)(128)(4,1)} %bitcast.125), calls=%async_computation.16 | async-start | bytes 1048576
  531.8 12.0 %copy-start.7 = (f32[512,1536]{1,0:T(8,128)S(1)}, f32[512,1536]{1,0:T(8,128)}, u32[]{:S(2)}) copy-start(f32[512,1536]{1,0:T(8,128)} %copy-done.6) | copy-start | bytes 9437188
  554.1 34.4 %all-to-all-start.2 = ((bf16[4,512,384]{2,1,0:T(8,128)(2,1)}), bf16[4,512,384]{2,1,0:T(8,128)(2,1)S(1)}, u32[]{:S(2)}, u32[]{:S(2)}) async-start(bf16[4,512,384]{2,1,0:T(8,128)(2,1)} %bitcast.90), calls=%async_computation.2 | async-start | bytes 3145728 | tf_op jit(solution)/shard_map/all_to_all | solution.py:1560
  559.6 389.9 %all-gather.8.cloned.1.call-start = ((), (), s32[]{:S(2)}) async-start(), calls=%async_computation.7 | async-start | bytes 2949120 | tf_op jit(solution)/shard_map/all_gather | solution.py:1603
  588.5 33.3 %copy-start.26 = (f32[1536]{0:T(1024)S(1)}, f32[1536]{0:T(1024)}, u32[]{:S(2)}) copy-start(f32[1536]{0:T(1024)} %copy-done.25) | copy-start | bytes 18436
  949.5 4.7 copy-start.17
  (20 other events, 55.0 us)
Sparse Core Ops, SparseCore 0:
  113.4 150.6 all-gather.3
  267.6 183.6 all-gather.5
  478.0 248.6 reduce-scatter.1
  925.8 23.6 all-gather.7

commit v5 on v4

--- a/solution.py
+++ b/solution.py
@@ -382,253 +382,6 @@
     )
 
 
-CORE_PAIRS = [(0, 1), (1, 0), (2, 3), (3, 2)]
-X_PAIRS = [(0, 2), (2, 0), (1, 3), (3, 1)]
-Y_PAIRS = [(i, i ^ 1) for i in range(8)]
-Z_SHIFTS = [[(i, (i + 2 * k) % 8) for i in range(8)] for k in (1, 2, 3)]
-
-
-CHUNK = 384
-
-
-def gather_kernel(plan, has_vectors, *refs):
-    weights = len({entry[0] for entry in plan})
-    inputs = refs[:weights]
-    refs = refs[weights:]
-    if has_vectors:
-        vector_in, refs = refs[0], refs[1:]
-    outputs = refs[:weights]
-    refs = refs[weights:]
-    if has_vectors:
-        vector_out, refs = refs[0], refs[1:]
-    zs_sem, zr_sem, ys_sem, yr_sem, xs_sem, xr_sem, cs_sem, cr_sem, own_sem, vs_sem, vr_sem = refs
-    seq = lax.axis_index("seq")
-    fsdp = lax.axis_index("fsdp")
-    x, c = seq // 2, seq % 2
-    z, y = fsdp // 2, fsdp % 2
-    x_seq = 2 * (1 - x) + c
-    c_seq = 2 * x + 1 - c
-    y_fsdp = 2 * z + 1 - y
-
-    def at_z(k):
-        return 2 * ((z + k) % 4) + y
-
-    barrier = pltpu.get_barrier_semaphore()
-    partners = [(x_seq, fsdp), (c_seq, fsdp), (seq, y_fsdp)] + [(seq, at_z(k)) for k in (1, 2, 3)]
-    if has_vectors:
-        partners += [(seq, 2 * ((z + k) % 4) + 1 - y) for k in (1, 2, 3)]
-    for partner in partners:
-        pl.semaphore_signal(barrier, inc=1, device_id=partner, device_id_type=MESH)
-    pl.semaphore_wait(barrier, len(partners))
-
-    if has_vectors:
-        vector_sends = []
-        for k in range(1, 8):
-            copy = pltpu.make_async_remote_copy(
-                src_ref=vector_in,
-                dst_ref=vector_out.at[fsdp],
-                send_sem=vs_sem.at[k],
-                recv_sem=vr_sem.at[k],
-                device_id=(seq, (fsdp + k) % 8),
-                device_id_type=MESH,
-            )
-            copy.start()
-            vector_sends.append(copy)
-        own = pltpu.make_async_copy(vector_in, vector_out.at[fsdp], vs_sem.at[0])
-        own.start()
-
-    def part(entry):
-        weight, block, column, split = entry
-        first = 2 * c + x if split else 2 * c
-        count = 1 if split else 2
-        return weight, block, pl.ds(column, CHUNK), pl.ds(first, count)
-
-    def remote(region, send, recv, device):
-        return pltpu.make_async_remote_copy(
-            src_ref=region,
-            dst_ref=region,
-            send_sem=send,
-            recv_sem=recv,
-            device_id=device,
-            device_id_type=MESH,
-        )
-
-    sends = []
-
-    def send(copy):
-        copy.start()
-        sends.append(copy)
-
-    def start_z(i):
-        weight, block, columns, mine = part(plan[i])
-        source = inputs[weight].at[block, mine, :, columns]
-        target = outputs[weight].at[z, y, block, mine, :, columns]
-        for k in (1, 2, 3):
-            copy = pltpu.make_async_remote_copy(
-                src_ref=source,
-                dst_ref=target,
-                send_sem=zs_sem.at[i, k],
-                recv_sem=zr_sem.at[i, k],
-                device_id=(seq, at_z(k)),
-                device_id_type=MESH,
-            )
-            send(copy)
-        pltpu.make_async_copy(source, target, own_sem.at[i]).start()
-
-    def start_y(i):
-        weight, block, columns, mine = part(plan[i])
-        output = outputs[weight]
-        for k in (1, 2, 3):
-            region = output.at[(z + 4 - k) % 4, y, block, mine, :, columns]
-            remote(region, zs_sem.at[i, k], zr_sem.at[i, k], (seq, at_z(k))).wait_recv()
-        source = inputs[weight].at[block, mine, :, columns]
-        target = output.at[z, y, block, mine, :, columns]
-        pltpu.make_async_copy(source, target, own_sem.at[i]).wait()
-        region = output.at[:, y, block, mine, :, columns]
-        send(remote(region, ys_sem.at[i], yr_sem.at[i], (seq, y_fsdp)))
-
-    def start_x(i):
-        weight, block, columns, mine = part(plan[i])
-        output = outputs[weight]
-        region = output.at[:, 1 - y, block, mine, :, columns]
-        remote(region, ys_sem.at[i], yr_sem.at[i], (seq, y_fsdp)).wait_recv()
-        region = output.at[:, :, block, mine, :, columns]
-        if plan[i][3]:
-            send(remote(region, xs_sem.at[i], xr_sem.at[i], (x_seq, fsdp)))
-        send(remote(region, cs_sem.at[i, 0], cr_sem.at[i, 0], (c_seq, fsdp)))
-
-    def start_core(i):
-        if plan[i][3]:
-            weight, block, columns, _ = part(plan[i])
-            region = outputs[weight].at[:, :, block, pl.ds(2 * c + 1 - x, 1), :, columns]
-            remote(region, xs_sem.at[i], xr_sem.at[i], (x_seq, fsdp)).wait_recv()
-            send(remote(region, cs_sem.at[i, 1], cr_sem.at[i, 1], (c_seq, fsdp)))
-
-    def finish(i):
-        weight, block, columns, _ = part(plan[i])
-        other = 2 * (1 - c)
-        output = outputs[weight]
-        if plan[i][3]:
-            for j, quarter in ((0, other + x), (1, other + 1 - x)):
-                region = output.at[:, :, block, pl.ds(quarter, 1), :, columns]
-                remote(region, cs_sem.at[i, j], cr_sem.at[i, j], (c_seq, fsdp)).wait_recv()
-        else:
-            region = output.at[:, :, block, pl.ds(other, 2), :, columns]
-            remote(region, cs_sem.at[i, 0], cr_sem.at[i, 0], (c_seq, fsdp)).wait_recv()
-
-    chunks = len(plan)
-    ahead = 3
-    for i in range(min(ahead, chunks)):
-        start_z(i)
-    for t in range(chunks + 2):
-        if t + ahead < chunks:
-            start_z(t + ahead)
-        if t < chunks:
-            start_y(t)
-        if 0 <= t - 1 < chunks:
-            start_x(t - 1)
-        if 0 <= t - 2 < chunks:
-            start_core(t - 2)
-    for i in range(chunks):
-        finish(i)
-    for copy in sends:
-        copy.wait_send()
-    if has_vectors:
-        own.wait()
-        for k in range(1, 8):
-            vector_sends[k - 1].wait_send()
-            region = vector_out.at[(fsdp + 8 - k) % 8]
-            remote(region, vs_sem.at[k], vr_sem.at[k], (seq, (fsdp + k) % 8)).wait_recv()
-
-
-def gather_plan(shapes):
-    places = [
-        (weight, block, column)
-        for weight, (rows, columns) in enumerate(shapes)
-        for block in range(rows // 192)
-        for column in range(0, columns, CHUNK)
-    ]
-    return tuple(place + ((len(places) - 1 - i) % 3 != 0,) for i, place in enumerate(places))
-
-
-def gather_weights(shards, vectors, collective_id):
-    shapes = [shard.shape for shard in shards]
-    plan = gather_plan(shapes)
-    chunks = len(plan)
-    inputs = [shard.reshape(rows // 192, 4, 48, columns) for shard, (rows, columns) in zip(shards, shapes)]
-    out_shapes = [
-        jax.ShapeDtypeStruct((4, 2, rows // 192, 4, 48, columns), BF16) for rows, columns in shapes
-    ]
-    if vectors is not None:
-        inputs.append(vectors)
-        out_shapes.append(jax.ShapeDtypeStruct((8,) + vectors.shape, vectors.dtype))
-    anywhere = pl.BlockSpec(memory_space=pl.ANY)
-    dma = pltpu.SemaphoreType.DMA
-    results = pl.pallas_call(
-        functools.partial(gather_kernel, plan, vectors is not None),
-        out_shape=out_shapes,
-        in_specs=[anywhere] * len(inputs),
-        out_specs=[anywhere] * len(out_shapes),
-        scratch_shapes=[
-            dma((chunks, 4)),
-            dma((chunks, 4)),
-            dma((chunks,)),
-            dma((chunks,)),
-            dma((chunks,)),
-            dma((chunks,)),
-            dma((chunks, 2)),
-            dma((chunks, 2)),
-            dma((chunks,)),
-            dma((8,)),
-            dma((8,)),
-        ],
-        compiler_params=pltpu.CompilerParams(collective_id=collective_id, has_side_effects=True),
-        name="gather_weights",
-    )(*inputs)
-    whole = [result.reshape(8 * rows, columns) for result, (rows, columns) in zip(results, shapes)]
-    return whole, results[-1]
-
-
-def gather_quarters(shard):
-    part = shard.shape[0] // lax.axis_size("seq")
-    mine = lax.dynamic_slice_in_dim(shard, lax.axis_index("seq") * part, part, 0)
-    return lax.all_gather(mine, ("fsdp", "seq"), axis=0, tiled=True)
-
-
-def pack_vectors(vectors):
-    stacked = jnp.stack([vector.astype(F32) for vector in vectors])
-    return jnp.pad(stacked, ((0, 8 - stacked.shape[0]), (0, (-stacked.shape[1]) % 128)))
-
-
-def blocks_kernel(left, *refs):
-    *rights, out = refs
-    width = rights[0].shape[1]
-    for kind, right in enumerate(rights):
-        out[0, :, kind * width : (kind + 1) * width] = jnp.dot(
-            left[...], right[...], preferred_element_type=F32
-        ).astype(BF16)
-
-
-def product_blocks(left, right, kinds, groups):
-    rows, depth = left.shape
-    width = right.shape[1] // (kinds * groups)
-    spec = lambda kind: pl.BlockSpec((depth, width), lambda i: (0, kind * groups + i))
-    return pl.pallas_call(
-        blocks_kernel,
-        grid=(groups,),
-        out_shape=jax.ShapeDtypeStruct((groups, rows, kinds * width), BF16),
-        in_specs=[pl.BlockSpec((rows, depth), lambda i: (0, 0))] + [spec(k) for k in range(kinds)],
-        out_specs=pl.BlockSpec((1, rows, kinds * width), lambda i: (i, 0, 0)),
-        compiler_params=pltpu.CompilerParams(vmem_limit_bytes=48 << 20),
-        cost_estimate=pl.CostEstimate(
-            flops=2 * rows * right.size,
-            bytes_accessed=2 * (rows * depth + right.size + rows * right.shape[1]),
-            transcendentals=0,
-        ),
-        name="product_blocks",
-    )(left, *[right] * kinds)
-
-
 QUERIES = 256
 
 
@@ -688,35 +441,6 @@
             outs.append(total / summed)
             logsum_ref[0, 0, head : head + 1, rows] = highest + jnp.log(summed)
         out_ref[block, 0] = join_heads(outs).T.astype(BF16)
-
-
-def attention(qkv, scale):
-    blocks, clips, frames, width = qkv.shape
-    pairs = width // (3 * 2 * HD)
-    length = blocks * frames
-    spec = lambda offset: pl.BlockSpec(
-        (blocks, 1, frames, 2 * HD), lambda clip, pair: (0, clip, 0, offset + pair)
-    )
-    return pl.pallas_call(
-        functools.partial(attention_kernel, scale),
-        grid=(clips, pairs),
-        out_shape=(
-            jax.ShapeDtypeStruct((blocks, clips, frames, pairs * 2 * HD), BF16),
-            jax.ShapeDtypeStruct((clips, pairs, 2, length), F32),
-        ),
-        in_specs=[spec(0), spec(pairs), spec(2 * pairs)],
-        out_specs=(
-            spec(0),
-            pl.BlockSpec((1, 1, 2, length), lambda clip, pair: (clip, pair, 0, 0)),
-        ),
-        compiler_params=pltpu.CompilerParams(vmem_limit_bytes=48 << 20),
-        cost_estimate=pl.CostEstimate(
-            flops=clips * pairs * 2 * 4 * length * length * 2 * HD,
-            bytes_accessed=4 * clips * pairs * length * 2 * HD * 2,
-            transcendentals=clips * pairs * 2 * length * length,
-        ),
-        name="attention",
-    )(qkv, qkv, qkv)
 
 
 def attention_back_kernel(
@@ -800,6 +524,423 @@
         ),
         name="attention_back",
     )(qkv, qkv, qkv, grad, logsum)
+
+
+def forward_kernel(plan, weights, scale, *refs):
+    inputs = refs[:weights]
+    vector_in, hidden_in = refs[weights : weights + 2]
+    refs = refs[weights + 2 :]
+    outputs = refs[:weights]
+    vector_out, normed_out, heads, logsum_out, context = refs[weights : weights + 5]
+    (
+        vector_land,
+        vector,
+        hidden,
+        normed,
+        weight_buf,
+        product_buf,
+        q_buf,
+        k_buf,
+        v_buf,
+        context_buf,
+        logsum_buf,
+        z_send,
+        z_recv,
+        y_sem,
+        x_sem,
+        c_sem,
+        own_sem,
+        vector_sem,
+        load_sem,
+        product_send,
+        product_recv,
+        block_sem,
+        context_sem,
+        context_own,
+    ) = refs[weights + 5 :]
+    seq = lax.axis_index("seq")
+    fsdp = lax.axis_index("fsdp")
+    x, c = seq // 2, seq % 2
+    z, y = fsdp // 2, fsdp % 2
+    x_seq = 2 * (1 - x) + c
+    c_seq = 2 * x + 1 - c
+    neighbours = (x_seq, c_seq, 3 - seq)
+    y_fsdp = 2 * z + 1 - y
+    chunks = len(plan)
+    clips, pairs = logsum_buf.shape[:2]
+    frames = hidden.shape[0] // clips
+
+    def at_z(k):
+        return (seq, 2 * ((z + k) % 4) + y)
+
+    barrier = pltpu.get_barrier_semaphore()
+    partners = [(other, fsdp) for other in neighbours] + [(seq, (fsdp + k) % 8) for k in range(1, 8)]
+    for partner in partners:
+        pl.semaphore_signal(barrier, inc=1, device_id=partner, device_id_type=MESH)
+    pl.semaphore_wait(barrier, len(partners))
+
+    def remote(source, target, send, recv, device):
+        return pltpu.make_async_remote_copy(
+            src_ref=source,
+            dst_ref=target,
+            send_sem=send,
+            recv_sem=recv,
+            device_id=device,
+            device_id_type=MESH,
+        )
+
+    def over(region, sems, device):
+        return remote(region, region, sems.at[0], sems.at[1], device)
+
+    sends = []
+
+    def send(copy):
+        copy.start()
+        sends.append(copy)
+
+    def vector_copy(k):
+        return remote(
+            vector_in,
+            vector_land.at[fsdp],
+            vector_sem.at[0, k],
+            vector_sem.at[1, k],
+            (seq, (fsdp + k) % 8),
+        )
+
+    def vector_arrival(k):
+        region = vector_land.at[(fsdp + 8 - k) % 8]
+        return over(region, vector_sem.at[:, k], (seq, (fsdp + k) % 8))
+
+    own_vector = pltpu.make_async_copy(vector_in, vector_land.at[fsdp], vector_sem.at[0, 0])
+    hidden_load = pltpu.make_async_copy(hidden_in, hidden, vector_sem.at[1, 0])
+    normed_store = pltpu.make_async_copy(normed, normed_out, vector_sem.at[1, 0])
+    vector_store = pltpu.make_async_copy(vector, vector_out, vector_sem.at[0, 0])
+
+    def norm():
+        own_vector.wait()
+        for k in range(1, 8):
+            vector_arrival(k).wait_recv()
+        hidden_load.wait()
+        vector[...] = sum(vector_land[f] for f in range(8))
+        vector_store.start()
+
+        @pl.loop(0, hidden.shape[0] // 32)
+        def _(block):
+            rows = pl.ds(pl.multiple_of(block * 32, 32), 32)
+            value = hidden[rows, :].astype(F32)
+            center = value - jnp.mean(value, axis=1, keepdims=True)
+            inverse = lax.rsqrt(jnp.mean(center * center, axis=1, keepdims=True) + 1e-05)
+            normed[rows, :] = (center * inverse * vector[0:1, :] + vector[1:2, :]).astype(BF16)
+
+        normed_store.start()
+
+    def part(entry):
+        weight, block, column, width, split = entry
+        first = 2 * c + x if split else 2 * c
+        return weight, block, pl.ds(column, width), pl.ds(first, 1 if split else 2)
+
+    def start_z(i):
+        weight, block, columns, mine = part(plan[i])
+        source = inputs[weight].at[block, mine, :, columns]
+        target = outputs[weight].at[z, y, block, mine, :, columns]
+        for k in (1, 2, 3):
+            send(remote(source, target, z_send.at[i, k - 1], z_recv.at[i, k - 1], at_z(k)))
+        pltpu.make_async_copy(source, target, own_sem.at[i]).start()
+
+    def start_y(i):
+        weight, block, columns, mine = part(plan[i])
+        output = outputs[weight]
+        for k in (1, 2, 3):
+            region = output.at[(z + 4 - k) % 4, y, block, mine, :, columns]
+            remote(region, region, z_send.at[i, k - 1], z_recv.at[i, k - 1], at_z(k)).wait_recv()
+        source = inputs[weight].at[block, mine, :, columns]
+        target = output.at[z, y, block, mine, :, columns]
+        pltpu.make_async_copy(source, target, own_sem.at[i]).wait()
+        region = output.at[:, y, block, mine, :, columns]
+        send(over(region, y_sem.at[:, i], (seq, y_fsdp)))
+
+    def start_x(i):
+        weight, block, columns, mine = part(plan[i])
+        output = outputs[weight]
+        region = output.at[:, 1 - y, block, mine, :, columns]
+        over(region, y_sem.at[:, i], (seq, y_fsdp)).wait_recv()
+        region = output.at[:, :, block, mine, :, columns]
+        if plan[i][4]:
+            send(over(region, x_sem.at[:, i], (x_seq, fsdp)))
+        send(over(region, c_sem.at[:, i, 0], (c_seq, fsdp)))
+
+    def start_core(i):
+        if plan[i][4]:
+            weight, block, columns, _ = part(plan[i])
+            region = outputs[weight].at[:, :, block, pl.ds(2 * c + 1 - x, 1), :, columns]
+            over(region, x_sem.at[:, i], (x_seq, fsdp)).wait_recv()
+            send(over(region, c_sem.at[:, i, 1], (c_seq, fsdp)))
+
+    def finish(i):
+        weight, block, columns, _ = part(plan[i])
+        other = 2 * (1 - c)
+        output = outputs[weight]
+        if plan[i][4]:
+            for j, quarter in ((0, other + x), (1, other + 1 - x)):
+                region = output.at[:, :, block, pl.ds(quarter, 1), :, columns]
+                over(region, c_sem.at[:, i, j], (c_seq, fsdp)).wait_recv()
+        else:
+            region = output.at[:, :, block, pl.ds(other, 2), :, columns]
+            over(region, c_sem.at[:, i, 0], (c_seq, fsdp)).wait_recv()
+
+    def weight_load(i):
+        region = outputs[0].at[:, :, 0, :, :, pl.ds(384 * i, 384)]
+        return pltpu.make_async_copy(region, weight_buf.at[i % 2], load_sem.at[i % 2])
+
+    def product_copy(i):
+        kind, group = i // 4, i % 4
+        target = heads.at[seq, :, pl.ds(384 * kind, 384)]
+        away = remote(
+            product_buf.at[i % 2],
+            target,
+            product_send.at[i],
+            product_recv.at[kind, seq],
+            (group, fsdp),
+        )
+        here = pltpu.make_async_copy(product_buf.at[i % 2], target, product_send.at[i])
+        return group, away, here
+
+    def start_product(i):
+        group, away, here = product_copy(i)
+
+        @pl.when(seq != group)
+        def _():
+            away.start()
+
+        @pl.when(seq == group)
+        def _():
+            here.start()
+
+    def wait_product(i):
+        group, away, here = product_copy(i)
+
+        @pl.when(seq != group)
+        def _():
+            away.wait_send()
+
+        @pl.when(seq == group)
+        def _():
+            here.wait()
+
+    def project(i):
+        weight_load(i).wait()
+        if i >= 2:
+            wait_product(i - 2)
+        right = weight_buf[i % 2].reshape(-1, 384)
+
+        @pl.loop(0, normed.shape[0] // 256)
+        def _(block):
+            rows = pl.ds(pl.multiple_of(block * 256, 256), 256)
+            out = jnp.dot(normed[rows, :], right, preferred_element_type=F32)
+            product_buf[i % 2, rows, :] = out.astype(BF16)
+
+        start_product(i)
+
+    def wait_heads():
+        for i in (10, 11):
+            wait_product(i)
+        for kind in range(3):
+            for other in neighbours:
+                region = heads.at[other, :, pl.ds(384 * kind, 384)]
+                remote(
+                    region, region, product_send.at[0], product_recv.at[kind, other], (other, fsdp)
+                ).wait_recv()
+
+    def block_loads(step):
+        clip, pair = step // pairs, step % pairs
+        return [
+            pltpu.make_async_copy(
+                heads.at[:, pl.ds(clip * frames, frames), pl.ds(384 * kind + 128 * pair, 128)],
+                buffer.at[step % 2, :, 0],
+                block_sem.at[kind, step % 2],
+            )
+            for kind, buffer in enumerate((q_buf, k_buf, v_buf))
+        ]
+
+    def start_blocks(step):
+        for copy in block_loads(step):
+            copy.start()
+
+    def context_region(step, group):
+        clip, pair = step // pairs, step % pairs
+        column = pl.multiple_of(group * 384 + pair * 128, 128)
+        return context.at[pl.ds(clip * frames, frames), pl.ds(column, 128)]
+
+    def context_copy(step, which):
+        other = neighbours[which]
+        return remote(
+            context_buf.at[step % 2, other, 0],
+            context_region(step, seq),
+            context_sem.at[0, step, which],
+            context_sem.at[1, step, which],
+            (other, fsdp),
+        )
+
+    def context_here(step):
+        return pltpu.make_async_copy(
+            context_buf.at[step % 2, seq, 0], context_region(step, seq), context_own.at[step]
+        )
+
+    def context_sent(step):
+        for which in range(3):
+            context_copy(step, which).wait_send()
+        context_here(step).wait()
+
+    def attend(step):
+        for copy in block_loads(step):
+            copy.wait()
+        if step + 1 < clips * pairs:
+            start_blocks(step + 1)
+        if step >= 2:
+            context_sent(step - 2)
+        slot = step % 2
+        attention_kernel(
+            scale,
+            q_buf.at[slot],
+            k_buf.at[slot],
+            v_buf.at[slot],
+            context_buf.at[slot],
+            logsum_buf.at[step // pairs, step % pairs],
+        )
+        for which in range(3):
+            context_copy(step, which).start()
+        context_here(step).start()
+
+    steps = clips * pairs
+    projections = 12
+    attention_start = projections + 7
+    beside = {2: [norm]}
+    for i in range(projections):
+        beside.setdefault(i + 4, []).extend(
+            [functools.partial(finish, i), lambda i=i: weight_load(i).start()]
+        )
+        beside.setdefault(i + 5, []).insert(0, functools.partial(project, i))
+    beside.setdefault(attention_start, []).extend([wait_heads, lambda: start_blocks(0)])
+    for step in range(steps):
+        beside.setdefault(attention_start + 1 + 2 * step, []).append(functools.partial(attend, step))
+
+    hidden_load.start()
+    own_vector.start()
+    for k in range(1, 8):
+        send(vector_copy(k))
+    ahead = 3
+    for i in range(ahead):
+        start_z(i)
+    for t in range(chunks + 2):
+        if t + ahead < chunks:
+            start_z(t + ahead)
+        if t < chunks:
+            start_y(t)
+        if 0 <= t - 1 < chunks:
+            start_x(t - 1)
+        if 0 <= t - 2 < chunks:
+            start_core(t - 2)
+        for run in beside.pop(t, []):
+            run()
+    for i in range(projections, chunks):
+        finish(i)
+    for copy in sends:
+        copy.wait_send()
+    normed_store.wait()
+    vector_store.wait()
+    for step in (steps - 2, steps - 1):
+        context_sent(step)
+    for step in range(steps):
+        for which in range(3):
+            region = context_region(step, neighbours[which])
+            over(region, context_sem.at[:, step, which], (neighbours[which], fsdp)).wait_recv()
+    pltpu.sync_copy(logsum_buf, logsum_out)
+
+
+def forward_plan(shapes):
+    places = []
+    for weight, (rows, columns) in enumerate(shapes):
+        blocks = rows // 192
+        for block in range(blocks):
+            last = weight == len(shapes) - 1 and block == blocks - 1
+            width = 384 if weight == 0 or last else 768
+            places += [(weight, block, column, width) for column in range(0, columns, width)]
+    return tuple(
+        place + ((len(places) - 1 - i) * 5 % 9 >= 4,) for i, place in enumerate(places)
+    )
+
+
+def forward(shards, vectors, hidden, clips, scale):
+    shapes = [shard.shape for shard in shards]
+    plan = forward_plan(shapes)
+    chunks, weights = len(plan), len(shards)
+    rows, width = hidden.shape
+    frames, group = rows // clips, width // 4
+    pairs = group // (2 * HD)
+    inputs = [shard.reshape(depth // 192, 4, 48, columns) for shard, (depth, columns) in zip(shards, shapes)]
+    inputs += [vectors, hidden]
+    out_shapes = [
+        jax.ShapeDtypeStruct((4, 2, depth // 192, 4, 48, columns), BF16) for depth, columns in shapes
+    ]
+    logsum_shape = (clips, pairs, 1, 1, 2, 4 * frames)
+    out_shapes += [
+        jax.ShapeDtypeStruct(vectors.shape, F32),
+        jax.ShapeDtypeStruct(hidden.shape, BF16),
+        jax.ShapeDtypeStruct((4, rows, 3 * group), BF16),
+        jax.ShapeDtypeStruct(logsum_shape, F32),
+        jax.ShapeDtypeStruct(hidden.shape, BF16),
+    ]
+    anywhere = pl.BlockSpec(memory_space=pl.ANY)
+    dma = pltpu.SemaphoreType.DMA
+    pair_block = pltpu.VMEM((2, 4, 1, frames, 2 * HD), BF16)
+    results = pl.pallas_call(
+        functools.partial(forward_kernel, plan, weights, scale),
+        out_shape=out_shapes,
+        in_specs=[anywhere] * len(inputs),
+        out_specs=[anywhere] * len(out_shapes),
+        scratch_shapes=[
+            pltpu.VMEM((8,) + vectors.shape, F32),
+            pltpu.VMEM(vectors.shape, F32),
+            pltpu.VMEM(hidden.shape, BF16),
+            pltpu.VMEM(hidden.shape, BF16),
+            pltpu.VMEM((2, 4, 2, 4, 48, 384), BF16),
+            pltpu.VMEM((2, rows, 384), BF16),
+            pair_block,
+            pair_block,
+            pair_block,
+            pair_block,
+            pltpu.VMEM(logsum_shape, F32),
+            dma((chunks, 3)),
+            dma((chunks, 3)),
+            dma((2, chunks)),
+            dma((2, chunks)),
+            dma((2, chunks, 2)),
+            dma((chunks,)),
+            dma((2, 8)),
+            dma((2,)),
+            dma((12,)),
+            dma((3, 4)),
+            dma((3, 2)),
+            dma((2, clips * pairs, 3)),
+            dma((clips * pairs,)),
+        ],
+        compiler_params=pltpu.CompilerParams(
+            collective_id=1, has_side_effects=True, vmem_limit_bytes=48 << 20
+        ),
+        name="forward",
+    )(*inputs)
+    wholes = [
+        result.reshape(8 * depth, columns) for result, (depth, columns) in zip(results, shapes)
+    ]
+    vector, normed, heads, logsum, context = results[weights:]
+    return wholes, vector, normed, heads, logsum.reshape(clips, pairs, 2, 4 * frames), context
+
+
+def place_vectors(vectors):
+    stacked = jnp.stack([vector.astype(F32) for vector in vectors])
+    count, shard = stacked.shape
+    whole = jnp.zeros((8, 8 * shard), F32)
+    return lax.dynamic_update_slice(whole, stacked, (0, lax.axis_index("fsdp") * shard))
 
 
 def text_weights(scale, queries, keys):
@@ -1493,29 +1634,32 @@
     group_width = width // groups
 
     gains = (self_gain, self_bias, cross_gain, cross_bias, final_gain, final_bias)
-    early = (query_key_value, self_output)
-    (qkv_whole, self_output_whole), vectors = gather_weights(early, pack_vectors(gains), 1)
-    qkv_whole, expand_weight = lax.optimization_barrier((qkv_whole, expand_weight))
-    expand_whole = gather_quarters(expand_weight)
-    vectors = vectors[:, :6, : width // fsdp_count]
-    gains = [vectors[:, i].reshape(width) for i in range(6)]
-
+    wholes, gains, normed_one, regrouped, logsum, context = forward(
+        (
+            query_key_value,
+            self_output,
+            cross_query,
+            cross_memory,
+            cross_output,
+            expand_weight,
+            contract_weight,
+        ),
+        place_vectors(gains),
+        hidden_states.reshape(rows, width),
+        clips,
+        scale,
+    )
+    (
+        qkv_whole,
+        self_output_whole,
+        cross_query_whole,
+        cross_memory_whole,
+        cross_output_whole,
+        expand_whole,
+        contract_whole,
+    ) = wholes
+    regrouped = regrouped.reshape(groups, clips, frames, 3 * group_width)
     hidden = hidden_states.reshape(rows, width).astype(F32)
-    normed_one = layer_norm(hidden, gains[0], gains[1]).astype(BF16)
-    projected = product_blocks(normed_one, qkv_whole, 3, groups)
-    regrouped = lax.all_to_all(projected, "seq", split_axis=0, concat_axis=0, tiled=True)
-    regrouped = regrouped.reshape(groups, clips, frames, 3 * group_width)
-    context_heads, logsum = attention(regrouped, scale)
-    context_heads = context_heads.reshape(groups, rows, group_width)
-    context = lax.all_to_all(context_heads, "seq", split_axis=0, concat_axis=0, tiled=True)
-    late = (cross_query, cross_memory, cross_output)
-    context, late, expand_whole, contract_weight = lax.optimization_barrier(
-        (context, late, expand_whole, contract_weight)
-    )
-    contract_whole = gather_quarters(contract_weight)
-    late, _ = gather_weights(late, None, 2)
-    cross_query_whole, cross_memory_whole, cross_output_whole = late
-    context = context.transpose(1, 0, 2).reshape(rows, width)
     attended = product(context, self_output_whole)
     first = hidden + attended
     normed_two, norm_two_back = jax.vjp(layer_norm, first, gains[2], gains[3])

time: 971 us -> 933 us (0.961)
  blocking collectives: 84.8 us -> 0 us
  Pallas kernels: 639 us -> 721 us
  waiting for transfers between devices: 38.8 us -> 12.7 us
    all_to_all x1 -> x0, blocking collectives: 84.8 us -> none  [on_blocks(): lax.all_to_all(projected, 'seq', split_axis=0, concat_axis=0, tiled=True)]
    pallas_call x4 -> x1, Pallas kernels: 287 us -> 369 us  [forward(): pl.pallas_call(functools.partial(forward_kernel, plan, weights, scale), o...]
    all_to_all x1 -> x0, waiting for transfers between devices: 20 us -> none  [on_blocks(): lax.all_to_all(context_heads, 'seq', split_axis=0, concat_axis=0, tiled=T...]
  transfers between devices with their start and end apart: 6 -> 3, of which waited for: 4 -> 2; matrix products, arithmetic and copies ran while one was open for 16% -> 11% of each run, Pallas kernels for 56% -> 38%
where the time goes in v5:
time: 933 us; the launch traced here: 926 us
  Pallas kernels  721 us (77%)
  matrix products  118 us (13%)
  other arithmetic  30.4 us (3%)
  local copies, waits for them, and re-layouts  24.5 us (3%)
  between operations  14.7 us (2%)
  waiting for transfers between devices  12.7 us (1%)
    pallas_call x1, Pallas kernels, forward(): pl.pallas_call(functools.partial(forward_kernel, plan, weights, scale), o...  369 us
    pallas_call x1, Pallas kernels, sum_products(): pl.pallas_call(functools.partial(sum_kernel, tuple(plan), weights), out_s...  304 us
    dot_general x5, matrix products, product_right(): lax.dot_general(left, right, (((1,), (1,)), ((), ())), preferred_element_...  51.3 us
    dot_general x6, matrix products, product(): return jnp.dot(left, right, preferred_element_type=jnp.float32)  50.8 us
    pallas_call x1, Pallas kernels, attention_back(): pl.pallas_call(functools.partial(attention_back_kernel, scale), grid=(cli...  33.3 us
  transfers between devices with their start and end apart: 3, of which 2 were waited for; matrix products, arithmetic and copies ran while one was open for 11% of the time, Pallas kernels for 38%

profile of v5, /device:TPU:0, one launch (start us, length us, event | category | flops | bytes accessed | tf_op | source)
XLA Modules:
  0.0 925.5 jit_solution(18005052383235977772)
XLA Ops:
  16.2 368.8 %forward.1 = (bf16[4,2,1,4,48,4608]{5,4,3,2,1,0:T(8,128)(2,1)}, bf16[4,2,1,4,48,1536]{5,4,3,2,1,0:T(8,128)(2,1)}, bf16[4,2,1,4,48,1536]{5,4,3,2,1,0:T(8,128)(2,1...) custom-call(bf16[1,4,48,4608]{3,2,1,0:T(8,128)(2,1)} %bitcast.94, ...), custom_call_target="tpu_custom_call" | custom-call | tf_op jit(solution)/shard_map/forward/pallas_call | solution.py:896
  385.1 6.4 fusion.8
  395.4 2.6 convolution_convert_fusion.4.q_ref
  401.2 3.3 text_attention.1.refs_1_
  404.5 3.3 fusion.7
  409.6 18.9 %multiply_convert_fusion.1 = (bf16[512,6144]{1,0:T(8,128)(2,1)}, f32[512,6144]{1,0:T(8,128)}) fusion(bf16[512,1536]{1,0:T(8,128)(2,1)S(1)} %add_convert_fusion.1.refs_0_, bf16[1536,6144]{1,0:T(8,128)(2,1)} %bitcast.104), kind=kOutput, calls=%fused_computation.3 | convolution fusion | flops 9679405056 | bytes 39321600 | tf_op jit(solution)/shard_map/dot_general | solution.py:31
  428.5 16.0 %convolution_convert_fusion = bf16[6144,1536]{1,0:T(8,128)(2,1)} fusion(bf16[512,6144]{1,0:T(8,128)(2,1)} %get-tuple-element.67, bf16[512,1536]{1,0:T(8,128)(2,1)S(1)} %bitcast.87), kind=kOutput, calls=%fused_computation | convolution fusion | flops 9673113600 | bytes 26738688 | tf_op jit(solution)/shard_map/dot_general | solution.py:35
  444.5 20.7 %multiply_convert_fusion.refs_6_ = bf16[512,6144]{1,0:T(8,128)(2,1)} fusion(bf16[512,1536]{1,0:T(8,128)(2,1)} %bitcast.86, bf16[6144,1536]{1,0:T(8,128)(2,1)} %bitcast.102, f32[512,6144]{1,0:T(8,128)} %get-tuple-element.127), kind=kOutput, calls=%fused_computation.1 | convolution fusion | flops 9701425152 | bytes 39321600 | tf_op jit(solution)/shard_map/dot_general | solution.py:41
  465.1 19.1 %multiply_reduce_fusion.4 = (f32[1536]{0:T(1024)S(1)}, f32[512]{0:T(512)S(1)}, f32[1536]{0:T(1024)S(1)}, f32[512,1536]{1,0:T(8,128)}) fusion(f32[512,1536]{1,0:T(8,128)} %copy-done.7, f32[512]{0:T(512)S(1)} %fusion.3, f32[512]{0:T(512)S(1)} %broadcast_multiply_fusion, f32[1536]{0:T(1024)S(1)} %get-tuple-element.104, ...), kind=kOutput, calls=%fused_computation.13 | convolution fusion | flops 9669963776 | bytes 31481856 | tf_op jit(solution)/shard_map/dot_general | solution.py:41
  484.2 4.3 fusion.6
  490.2 5.9 convolution_convert_fusion.3.grad_ref
  496.1 12.2 %text_attention_back.1 = (bf16[512,1536]{1,0:T(8,128)(2,1)S(1)}, bf16[128,3072]{1,0:T(8,128)(2,1)S(1)}) custom-call(bf16[512,1536]{1,0:T(8,128)(2,1)S(1)} %convolution_convert_fusion.4.q_ref, bf16[128,3072]{1,0:T(8,128)(2,1)S(1)} %fusion.memory_ref, bf16[512,1536]{1,0:T(8,128)(2,1)S(1)} %convolution_convert_fusion.3.grad_ref), custom_call_target="tpu_custom_call" | custom-call | flops 1006632960 | bytes 6291456 | tf_op jit(solution)/shard_map/text_attention_back/pallas_call | solution.py:996
  508.3 3.1 multiply_reduce_fusion.5
  512.4 2.4 fusion.4
  514.8 2.6 convolution_convert_fusion.2
  518.7 3.6 all-to-all-start
  522.4 18.0 %multiply_reduce_fusion.3 = (f32[]{:T(128)}, f32[]{:T(128)}, bf16[512,1536]{1,0:T(8,128)(2,1)}) fusion(f32[512,1536]{1,0:T(8,128)} %copy-done.7, bf16[512,6144]{1,0:T(8,128)(2,1)} %get-tuple-element.67, bf16[6144,1536]{1,0:T(8,128)(2,1)} %bitcast.103), kind=kOutput, calls=%fused_computation.12 | convolution fusion | flops 9668395008 | bytes 29884424 | tf_op jit(solution)/shard_map/dot_general | solution.py:31
  540.4 2.7 select_maximum_fusion
  547.1 3.7 all-to-all-done
  550.8 33.3 %attention_back.1 = bf16[4,2,256,1152]{3,2,1,0:T(8,128)(2,1)} custom-call(bf16[4,2,256,1152]{3,2,1,0:T(8,128)(2,1)} %bitcast.106, bf16[4,2,256,1152]{3,2,1,0:T(8,128)(2,1)} %bitcast.107, bf16[4,2,256,1152]{3,2,1,0:T(8,128)(2,1)} %bitcast.108, bf16[4,2,256,384]{3,2,1,0:T(8,128)(2,1)S(1)} %bitcast.73, f32[2,3,2,1024]{3,2,1,0:T(2,128)S(1)} %bitcast.78), custom_call_target="tpu_custom_call" | custom-call | flops 16106127360 | bytes 11010048 | tf_op jit(solution)/shard_map/attention_back/pallas_call | solution.py:506
  584.7 303.9 %sum_products.1 = (bf16[192,6144]{1,0:T(8,128)(2,1)}, bf16[192,1536]{1,0:T(8,128)(2,1)}, bf16[192,1536]{1,0:T(8,128)(2,1)}, bf16[192,3072]{1,0:T(8,128)(2,1)}, b...) custom-call(bf16[512,1536]{1,0:T(8,128)(2,1)} %copy-done.11, ...), custom_call_target="tpu_custom_call" | custom-call | tf_op jit(solution)/shard_map/sum_products/pallas_call | solution.py:1557
  891.5 4.5 convert_element_type.105
  903.3 9.0 all-gather.2.cloned.1.call-done
  912.3 4.5 convert_element_type.106
  (127 shorter events, 38.2 us)
Async XLA Ops:
  7.2 881.5 %reduce-scatter.2.cloned.1.call-start = ((), (), s32[]{:S(2)}) async-start(), calls=%async_computation.2 | async-start | bytes 19464192 | tf_op jit(solution)/shard_map/reduce_scatter | solution.py:1686
  16.2 368.9 %copy-start.13 = (bf16[2,256,1536]{2,1,0:T(8,128)(2,1)S(1)}, bf16[2,256,1536]{2,1,0:T(8,128)(2,1)}, u32[]{:S(2)}) copy-start(bf16[2,256,1536]{2,1,0:T(8,128)(2,1)} %param.16) | copy-start | bytes 4718596
  385.0 6.4 copy-start.1
  391.4 13.1 %copy-start.8 = (f32[512,1536]{1,0:T(8,128)}, f32[512,1536]{1,0:T(8,128)S(1)}, u32[]{:S(2)}) copy-start(f32[512,1536]{1,0:T(8,128)S(1)} %get-tuple-element.116) | copy-start | bytes 9437188
  392.5 5.5 slice-start
  392.5 12.0 %slice-start.7 = ((s8[4718592]{0:T(1024)(128)(4,1)}), s8[4194304]{0:T(1024)(128)(4,1)S(1)}, s32[]{:S(2)}) async-start(s8[4718592]{0:T(1024)(128)(4,1)} %bitcast.118), calls=%async_computation.11 | async-start | bytes 8388608
  393.1 4.9 copy-start.10
  395.4 4.0 slice-start.1
  395.4 4.2 slice-start.2
  395.4 4.2 copy-start.18
  395.4 9.1 slice-start.8
  409.6 18.9 %copy-start.11 = (bf16[512,1536]{1,0:T(8,128)(2,1)}, bf16[512,1536]{1,0:T(8,128)(2,1)S(1)}, u32[]{:S(2)}) copy-start(bf16[512,1536]{1,0:T(8,128)(2,1)S(1)} %add_convert_fusion.1.refs_0_) | copy-start | bytes 4718596
  409.6 18.9 %copy-start.15 = (bf16[2,256,1536]{2,1,0:T(8,128)(2,1)S(1)}, bf16[2,256,1536]{2,1,0:T(8,128)(2,1)}, u32[]{:S(2)}) copy-start(bf16[2,256,1536]{2,1,0:T(8,128)(2,1)} %param.31) | copy-start | bytes 4718596
  484.2 4.3 copy-start.16
  488.6 19.7 %slice-start.5 = ((s8[4718592]{0:T(1024)(128)(4,1)}), s8[4194304]{0:T(1024)(128)(4,1)S(1)}, s32[]{:S(2)}) async-start(s8[4718592]{0:T(1024)(128)(4,1)} %bitcast.114), calls=%async_computation.9 | async-start | bytes 8388608
  490.2 18.1 %slice-start.6 = ((s8[4718592]{0:T(1024)(128)(4,1)}), s8[524288]{0:T(1024)(128)(4,1)S(1)}, s32[]{:S(2)}) async-start(s8[4718592]{0:T(1024)(128)(4,1)} %bitcast.114), calls=%async_computation.10 | async-start | bytes 1048576
  496.1 12.2 %copy-start.9 = (f32[512,1536]{1,0:T(8,128)S(1)}, f32[512,1536]{1,0:T(8,128)}, u32[]{:S(2)}) copy-start(f32[512,1536]{1,0:T(8,128)} %copy-done.8) | copy-start | bytes 9437188
  518.7 32.1 %all-to-all-start = ((bf16[4,512,384]{2,1,0:T(8,128)(2,1)}), bf16[4,512,384]{2,1,0:T(8,128)(2,1)S(1)}, u32[]{:S(2)}, u32[]{:S(2)}) async-start(bf16[4,512,384]{2,1,0:T(8,128)(2,1)} %bitcast.85), calls=%async_computation | async-start | bytes 3145728 | tf_op jit(solution)/shard_map/all_to_all | solution.py:1704
  522.3 20.8 %copy-start.19 = (bf16[2,64,1536]{2,1,0:T(8,128)(2,1)S(1)}, bf16[2,64,1536]{2,1,0:T(8,128)(2,1)}, u32[]{:S(2)}) copy-start(bf16[2,64,1536]{2,1,0:T(8,128)(2,1)} %param.17) | copy-start | bytes 1179652
  522.3 389.9 %all-gather.2.cloned.1.call-start = ((), (), s32[]{:S(2)}) async-start(), calls=%async_computation.3 | async-start | bytes 2949120 | tf_op jit(solution)/shard_map/all_gather | solution.py:1747
  550.8 33.3 %copy-start.25 = (f32[1536]{0:T(1024)S(1)}, f32[1536]{0:T(1024)}, u32[]{:S(2)}) copy-start(f32[1536]{0:T(1024)} %get-tuple-element.102) | copy-start | bytes 18436
  891.5 4.5 copy-start.20
  898.2 4.0 copy-start.22
  903.3 13.5 %copy-start.17 = (f32[512,1536]{1,0:T(8,128)S(1)}, f32[512,1536]{1,0:T(8,128)}, u32[]{:S(2)}) copy-start(f32[512,1536]{1,0:T(8,128)} %get-tuple-element.78) | copy-start | bytes 9437188
  (15 other events, 34.7 us)
Sparse Core Ops, SparseCore 0:
  444.6 245.0 reduce-scatter.1
  888.8 23.4 all-gather.1

commit v6 on v5

--- a/solution.py
+++ b/solution.py
@@ -448,13 +448,11 @@
 ):
     blocks = q_ref.shape[0] * q_ref.shape[2] // QUERIES
     frames = q_ref.shape[2]
-    pair = pl.program_id(1)
-    group = pl.num_programs(1) * 2 * HD
     k = k_ref[:, 0].reshape(-1, 2 * HD)
     v = v_ref[:, 0].reshape(-1, 2 * HD)
 
     def columns(kind):
-        return pl.ds(pl.multiple_of(kind * group + pair * 2 * HD, 2 * HD), 2 * HD)
+        return pl.ds(kind * 2 * HD, 2 * HD)
 
     for block in range(blocks):
         rows = slice(block * QUERIES, (block + 1) * QUERIES)
@@ -496,34 +494,8 @@
     out_ref[:, 0, :, columns(2)] = grad_values[...].reshape(-1, frames, 2 * HD).astype(BF16)
 
 
-def attention_back(qkv, grad, logsum, scale):
-    blocks, clips, frames, width = qkv.shape
-    pairs = width // (3 * 2 * HD)
-    length = blocks * frames
-    spec = lambda offset: pl.BlockSpec(
-        (blocks, 1, frames, 2 * HD), lambda clip, pair: (0, clip, 0, offset + pair)
-    )
-    return pl.pallas_call(
-        functools.partial(attention_back_kernel, scale),
-        grid=(clips, pairs),
-        out_shape=jax.ShapeDtypeStruct(qkv.shape, BF16),
-        in_specs=[
-            spec(0),
-            spec(pairs),
-            spec(2 * pairs),
-            spec(0),
-            pl.BlockSpec((1, 1, 2, length), lambda clip, pair: (clip, pair, 0, 0)),
-        ],
-        out_specs=pl.BlockSpec((blocks, 1, frames, width), lambda clip, pair: (0, clip, 0, 0)),
-        scratch_shapes=[pltpu.VMEM((length, 2 * HD), F32), pltpu.VMEM((length, 2 * HD), F32)],
-        compiler_params=pltpu.CompilerParams(vmem_limit_bytes=48 << 20),
-        cost_estimate=pl.CostEstimate(
-            flops=clips * pairs * 2 * 10 * length * length * 2 * HD,
-            bytes_accessed=7 * clips * pairs * length * 2 * HD * 2,
-            transcendentals=clips * pairs * 2 * length * length,
-        ),
-        name="attention_back",
-    )(qkv, qkv, qkv, grad, logsum)
+X_LAG = 2
+CORE_LAG = 4
 
 
 def forward_kernel(plan, weights, scale, *refs):
@@ -639,13 +611,22 @@
         first = 2 * c + x if split else 2 * c
         return weight, block, pl.ds(column, width), pl.ds(first, 1 if split else 2)
 
+    def own_copy(i):
+        weight, block, columns, _ = part(plan[i])
+        both = pl.ds(2 * c, 2)
+        return pltpu.make_async_copy(
+            inputs[weight].at[block, both, :, columns],
+            outputs[weight].at[z, y, block, both, :, columns],
+            own_sem.at[i],
+        )
+
     def start_z(i):
         weight, block, columns, mine = part(plan[i])
         source = inputs[weight].at[block, mine, :, columns]
         target = outputs[weight].at[z, y, block, mine, :, columns]
         for k in (1, 2, 3):
             send(remote(source, target, z_send.at[i, k - 1], z_recv.at[i, k - 1], at_z(k)))
-        pltpu.make_async_copy(source, target, own_sem.at[i]).start()
+        own_copy(i).start()
 
     def start_y(i):
         weight, block, columns, mine = part(plan[i])
@@ -653,27 +634,36 @@
         for k in (1, 2, 3):
             region = output.at[(z + 4 - k) % 4, y, block, mine, :, columns]
             remote(region, region, z_send.at[i, k - 1], z_recv.at[i, k - 1], at_z(k)).wait_recv()
-        source = inputs[weight].at[block, mine, :, columns]
-        target = output.at[z, y, block, mine, :, columns]
-        pltpu.make_async_copy(source, target, own_sem.at[i]).wait()
+        own_copy(i).wait()
         region = output.at[:, y, block, mine, :, columns]
         send(over(region, y_sem.at[:, i], (seq, y_fsdp)))
+
+    def x_copies(i, quarter):
+        weight, block, columns, _ = part(plan[i])
+        rest = (block, pl.ds(quarter, 1), slice(None), columns)
+        regions = [outputs[weight].at[(slice(None), 1 - y) + rest]]
+        regions += [outputs[weight].at[((z + k) % 4, y) + rest] for k in (1, 2, 3)]
+        return [
+            over(region, x_sem.at[:, i, j], (x_seq, fsdp)) for j, region in enumerate(regions)
+        ]
 
     def start_x(i):
         weight, block, columns, mine = part(plan[i])
         output = outputs[weight]
         region = output.at[:, 1 - y, block, mine, :, columns]
         over(region, y_sem.at[:, i], (seq, y_fsdp)).wait_recv()
+        if plan[i][4]:
+            for copy in x_copies(i, 2 * c + x):
+                send(copy)
         region = output.at[:, :, block, mine, :, columns]
-        if plan[i][4]:
-            send(over(region, x_sem.at[:, i], (x_seq, fsdp)))
         send(over(region, c_sem.at[:, i, 0], (c_seq, fsdp)))
 
     def start_core(i):
         if plan[i][4]:
             weight, block, columns, _ = part(plan[i])
+            for copy in x_copies(i, 2 * c + 1 - x):
+                copy.wait_recv()
             region = outputs[weight].at[:, :, block, pl.ds(2 * c + 1 - x, 1), :, columns]
-            over(region, x_sem.at[:, i], (x_seq, fsdp)).wait_recv()
             send(over(region, c_sem.at[:, i, 1], (c_seq, fsdp)))
 
     def finish(i):
@@ -813,13 +803,13 @@
 
     steps = clips * pairs
     projections = 12
-    attention_start = projections + 7
+    attention_start = projections + CORE_LAG + 5
     beside = {2: [norm]}
     for i in range(projections):
-        beside.setdefault(i + 4, []).extend(
+        beside.setdefault(i + CORE_LAG + 2, []).extend(
             [functools.partial(finish, i), lambda i=i: weight_load(i).start()]
         )
-        beside.setdefault(i + 5, []).insert(0, functools.partial(project, i))
+        beside.setdefault(i + CORE_LAG + 3, []).insert(0, functools.partial(project, i))
     beside.setdefault(attention_start, []).extend([wait_heads, lambda: start_blocks(0)])
     for step in range(steps):
         beside.setdefault(attention_start + 1 + 2 * step, []).append(functools.partial(attend, step))
@@ -831,15 +821,15 @@
     ahead = 3
     for i in range(ahead):
         start_z(i)
-    for t in range(chunks + 2):
+    for t in range(chunks + CORE_LAG):
         if t + ahead < chunks:
             start_z(t + ahead)
         if t < chunks:
             start_y(t)
-        if 0 <= t - 1 < chunks:
-            start_x(t - 1)
-        if 0 <= t - 2 < chunks:
-            start_core(t - 2)
+        if 0 <= t - X_LAG < chunks:
+            start_x(t - X_LAG)
+        if 0 <= t - CORE_LAG < chunks:
+            start_core(t - CORE_LAG)
         for run in beside.pop(t, []):
             run()
     for i in range(projections, chunks):
@@ -866,7 +856,7 @@
             width = 384 if weight == 0 or last else 768
             places += [(weight, block, column, width) for column in range(0, columns, width)]
     return tuple(
-        place + ((len(places) - 1 - i) * 5 % 9 >= 4,) for i, place in enumerate(places)
+        place + ((len(places) - 1 - i) * 3 % 5 >= 2,) for i, place in enumerate(places)
     )
 
 
@@ -913,7 +903,7 @@
             dma((chunks, 3)),
             dma((chunks, 3)),
             dma((2, chunks)),
-            dma((2, chunks)),
+            dma((2, chunks, 4)),
             dma((2, chunks, 2)),
             dma((chunks,)),
             dma((2, 8)),
@@ -933,7 +923,7 @@
         result.reshape(8 * depth, columns) for result, (depth, columns) in zip(results, shapes)
     ]
     vector, normed, heads, logsum, context = results[weights:]
-    return wholes, vector, normed, heads, logsum.reshape(clips, pairs, 2, 4 * frames), context
+    return wholes, vector, normed, heads, logsum, context
 
 
 def place_vectors(vectors):
@@ -1012,19 +1002,20 @@
 
 PIECE = (192, 384)
 EARLY = 32
+AFTER_LAG = 0
 OVER_X = 1
 STAGES = 7
 SLOTS = 6
 
 
-def sum_kernel(plan, weights, *refs):
+def sum_kernel(plan, weights, scale, *refs):
     chunks = len(plan)
     late = chunks - 3
     lefts, rights = refs[:weights], refs[weights : 2 * weights - 1]
     refs = refs[2 * weights - 1 :]
-    heads_in, projection, hidden_in, grad_in, gain_in, vector_in = refs[:6]
-    outputs = refs[6 : 6 + weights]
-    heads, hidden_out, vector_out = refs[6 + weights : 9 + weights]
+    regrouped, context_grad, logsum_in, projection, hidden_in, grad_in, gain_in, vector_in = refs[:8]
+    outputs = refs[8 : 8 + weights]
+    heads, hidden_out, vector_out = refs[8 + weights : 11 + weights]
     (
         mine,
         c_out,
@@ -1047,6 +1038,14 @@
         hidden,
         grad,
         gain,
+        q_buf,
+        k_buf,
+        v_buf,
+        context_buf,
+        logsum,
+        heads_buf,
+        key_grads,
+        value_grads,
         vector,
         vector_got,
         vector_z,
@@ -1063,8 +1062,10 @@
         load_sem,
         vector_sem,
         heads_sem,
+        heads_own_sem,
+        block_sem,
         own_sem,
-    ) = refs[9 + weights :]
+    ) = refs[11 + weights :]
     rights = rights + (heads,)
     seq = lax.axis_index("seq")
     fsdp = lax.axis_index("fsdp")
@@ -1098,25 +1099,87 @@
         return pl.ds(pl.multiple_of(block * 384, 128), 384)
 
     neighbours = (x_device, c_device, far_device)
-
-    def heads_send(which, kind):
+    clips, pairs = logsum.shape[:2]
+    frames = context_grad.shape[1] // clips
+    steps = clips * pairs
+
+    def block_loads(step):
+        rows = pl.ds(pl.multiple_of(step // pairs * frames, frames), frames)
+        first = step % pairs * 2 * HD
+        places = [(regrouped, q_buf, 0), (regrouped, k_buf, 384), (regrouped, v_buf, 768)]
+        places.append((context_grad, context_buf, 0))
+        return [
+            pltpu.make_async_copy(
+                source.at[:, rows, pl.ds(pl.multiple_of(column + first, 128), 128)],
+                buffer.at[:, 0],
+                block_sem.at[j],
+            )
+            for j, (source, buffer, column) in enumerate(places)
+        ]
+
+    def heads_region(step, kind, group):
+        rows = pl.ds(pl.multiple_of(step // pairs * frames, frames), frames)
+        column = (kind * 4 + group) * 384 + step % pairs * 2 * HD
+        return heads.at[rows, pl.ds(pl.multiple_of(column, 128), 128)]
+
+    def heads_send(step, which, kind):
+        other = neighbours[which]
         return remote(
-            heads_in.at[neighbours[which][0], :, pl.ds(kind * 384, 384)],
-            heads.at[:, columns(kind * 4 + seq)],
-            heads_sem.at[:, which, kind],
-            neighbours[which],
-        )
-
-    def heads_arrival(which, kind):
-        region = heads.at[:, columns(kind * 4 + neighbours[which][0])]
-        return remote(region, region, heads_sem.at[:, which, kind], neighbours[which])
-
-    def heads_own(kind):
+            heads_buf.at[other[0], 0, :, pl.ds(kind * 128, 128)],
+            heads_region(step, kind, seq),
+            heads_sem.at[:, step, which, kind],
+            other,
+        )
+
+    def heads_arrival(step, which, kind):
+        region = heads_region(step, kind, neighbours[which][0])
+        return remote(region, region, heads_sem.at[:, step, which, kind], neighbours[which])
+
+    def heads_own(step, kind):
         return pltpu.make_async_copy(
-            heads_in.at[seq, :, pl.ds(kind * 384, 384)],
-            heads.at[:, columns(kind * 4 + seq)],
-            own_sem.at[kind],
-        )
+            heads_buf.at[seq, 0, :, pl.ds(kind * 128, 128)],
+            heads_region(step, kind, seq),
+            heads_own_sem.at[step, kind],
+        )
+
+    logsum_load = pltpu.make_async_copy(logsum_in, logsum, block_sem.at[4])
+
+    def attention_step(t):
+        @pl.when(t == 0)
+        def _():
+            logsum_load.wait()
+
+        @pl.when(jnp.logical_and(t >= 1, t <= steps))
+        def _():
+            for kind in range(3):
+                heads_own(t - 1, kind).wait()
+                for which in range(3):
+                    heads_send(t - 1, which, kind).wait_send()
+
+        @pl.when(t < steps)
+        def _():
+            for copy in block_loads(t):
+                copy.wait()
+            attention_back_kernel(
+                scale,
+                q_buf,
+                k_buf,
+                v_buf,
+                context_buf,
+                logsum.at[t // pairs, t % pairs],
+                heads_buf,
+                key_grads,
+                value_grads,
+            )
+            for kind in range(3):
+                for which in range(3):
+                    heads_send(t, which, kind).start()
+                heads_own(t, kind).start()
+
+        @pl.when(t + 1 < steps)
+        def _():
+            for copy in block_loads(t + 1):
+                copy.start()
 
     def whole(kind):
         return pltpu.make_async_copy(
@@ -1146,9 +1209,9 @@
             @pl.when(i == j)
             def _():
                 if j >= late:
-                    heads_own(j - late).wait()
-                    for which in range(3):
-                        heads_arrival(which, j - late).wait_recv()
+                    for step in range(steps):
+                        for which in range(3):
+                            heads_arrival(step, which, j - late).wait_recv()
                 for copy in loads(j):
                     copy.start()
 
@@ -1499,10 +1562,9 @@
             pltpu.sync_copy(vector.at[0], vector_out)
 
     start_loads(0)
-    for kind in range(3):
-        heads_own(kind).start()
-        for which in range(3):
-            heads_send(which, kind).start()
+    for copy in block_loads(0):
+        copy.start()
+    logsum_load.start()
     whole(0).start()
     for copy in operands:
         copy.start()
@@ -1520,18 +1582,20 @@
             def _():
                 run(i)
 
+            if lag == AFTER_LAG:
+                attention_step(t)
+
         vector_step(t - chunks)
 
     for j in (chunks - 2, chunks - 1):
         c_copy(j).wait_send()
         store(j).wait()
-    for kind in range(3):
-        for which in range(3):
-            heads_send(which, kind).wait_send()
     hidden_store.wait()
 
 
-def sum_products(lefts, rights, heads, projection, hidden, grad, gain, vectors):
+def sum_products(
+    lefts, rights, regrouped, context_grad, logsum, projection, hidden, grad, gain, vectors, scale
+):
     weights = len(lefts)
     widths = [right.shape[1] for right in rights] + [projection.shape[1]]
     plan = [
@@ -1549,13 +1613,28 @@
         jax.ShapeDtypeStruct(grad.shape, F32),
         jax.ShapeDtypeStruct(vectors.shape, F32),
     ]
-    inputs = (*lefts, *rights, heads, projection, hidden, grad, gain, vectors)
+    inputs = (
+        *lefts,
+        *rights,
+        regrouped,
+        context_grad,
+        logsum,
+        projection,
+        hidden,
+        grad,
+        gain,
+        vectors,
+    )
+    clips, pairs, *_, length = logsum.shape
+    frames = depth // clips
+    pair_block = pltpu.VMEM((4, 1, frames, 2 * HD), BF16)
+    pair_grads = pltpu.VMEM((length, 2 * HD), F32)
     anywhere = pl.BlockSpec(memory_space=pl.ANY)
     dma = pltpu.SemaphoreType.DMA
     rest = PIECE[0] - EARLY
     block = lambda *lead, rows=PIECE[0]: pltpu.VMEM(lead + (rows, PIECE[1]), BF16)
     results = pl.pallas_call(
-        functools.partial(sum_kernel, tuple(plan), weights),
+        functools.partial(sum_kernel, tuple(plan), weights, scale),
         out_shape=out_shapes,
         in_specs=[anywhere] * len(inputs),
         out_specs=[anywhere] * len(out_shapes),
@@ -1581,6 +1660,14 @@
             pltpu.VMEM((depth, width), BF16),
             pltpu.VMEM((depth, width), F32),
             pltpu.VMEM(gain.shape, F32),
+            pair_block,
+            pair_block,
+            pair_block,
+            pair_block,
+            pltpu.VMEM(logsum.shape, F32),
+            pltpu.VMEM((4, 1, frames, 3 * 2 * HD), BF16),
+            pair_grads,
+            pair_grads,
             pltpu.VMEM((3,) + vectors.shape, F32),
             pltpu.VMEM((3,) + vectors.shape, F32),
             pltpu.VMEM((4,) + vectors.shape, F32),
@@ -1596,7 +1683,9 @@
             dma((2,)),
             dma((2, 2)),
             dma((2, 6)),
-            dma((2, 3, 3)),
+            dma((2, clips * pairs, 3, 3)),
+            dma((clips * pairs, 3)),
+            dma((5,)),
             dma((8,)),
         ],
         compiler_params=pltpu.CompilerParams(
@@ -1658,7 +1747,6 @@
         expand_whole,
         contract_whole,
     ) = wholes
-    regrouped = regrouped.reshape(groups, clips, frames, 3 * group_width)
     hidden = hidden_states.reshape(rows, width).astype(F32)
     attended = product(context, self_output_whole)
     first = hidden + attended
@@ -1731,17 +1819,18 @@
     grad_heads, output, terms, text_operands = lax.optimization_barrier(
         (grad_heads, output, terms, text_operands)
     )
-    grad_heads = grad_heads.reshape(groups, clips, frames, group_width)
-    grad_regrouped = attention_back(regrouped, grad_heads, logsum, scale)
     gradients, grad_hidden, totals = sum_products(
         [normed_three, cross_context, normed_two, text_operands[0], context, normed_one],
         [grad_preact, grad_crossed, grad_cross_q, text_operands[1], grad_attended],
-        grad_regrouped.reshape(groups, rows, 3 * group_width),
+        regrouped,
+        grad_heads,
+        logsum,
         qkv_whole,
         hidden_states.reshape(rows, width),
         grad_first,
         jnp.broadcast_to(gains[0], (8, width)),
         terms,
+        scale,
     )
     gradients, contract_part = lax.optimization_barrier((gradients, contract_part))
     contract_gradient = lax.all_gather(contract_part, "seq", axis=0, tiled=True)

time: 933 us -> 879 us (0.942)
  Pallas kernels: 721 us -> 665 us
    pallas_call x1, Pallas kernels: 369 us -> 336 us  [forward(): pl.pallas_call(functools.partial(forward_kernel, plan, weights, scale), o...]
    pallas_call x2 -> x1, Pallas kernels: 337 us -> 313 us  [sum_products(): pl.pallas_call(functools.partial(sum_kernel, tuple(plan), weights, scale)...]
  transfers between devices with their start and end apart: 3 -> 3, of which waited for: 2 -> 2; matrix products, arithmetic and copies ran while one was open for 11% -> 12% of each run, Pallas kernels for 38% -> 37%
where the time goes in v6:
time: 879 us; the launch traced here: 871 us
  Pallas kernels  665 us (76%)
  matrix products  113 us (13%)
  local copies, waits for them, and re-layouts  31.4 us (4%)
  other arithmetic  30.4 us (3%)
  between operations  14.9 us (2%)
  waiting for transfers between devices  13.2 us (2%)
    pallas_call x1, Pallas kernels, forward(): pl.pallas_call(functools.partial(forward_kernel, plan, weights, scale), o...  336 us
    pallas_call x1, Pallas kernels, sum_products(): pl.pallas_call(functools.partial(sum_kernel, tuple(plan), weights, scale)...  313 us
    dot_general x5, matrix products, product_right(): lax.dot_general(left, right, (((1,), (1,)), ((), ())), preferred_element_...  51 us
    dot_general x6, matrix products, product(): return jnp.dot(left, right, preferred_element_type=jnp.float32)  48.8 us
  transfers between devices with their start and end apart: 3, of which 2 were waited for; matrix products, arithmetic and copies ran while one was open for 12% of the time, Pallas kernels for 37%

profile of v6, /device:TPU:0, one launch (start us, length us, event | category | flops | bytes accessed | tf_op | source)
XLA Modules:
  0.0 871.3 jit_solution(5813711086593862966)
XLA Ops:
  16.2 336.0 %forward.1 = (bf16[4,2,1,4,48,4608]{5,4,3,2,1,0:T(8,128)(2,1)}, bf16[4,2,1,4,48,1536]{5,4,3,2,1,0:T(8,128)(2,1)}, bf16[4,2,1,4,48,1536]{5,4,3,2,1,0:T(8,128)(2,1...) custom-call(bf16[1,4,48,4608]{3,2,1,0:T(8,128)(2,1)} %bitcast.83, ...), custom_call_target="tpu_custom_call" | custom-call | tf_op jit(solution)/shard_map/forward/pallas_call | solution.py:886
  352.2 6.4 fusion.8
  362.6 2.6 convolution_convert_fusion.4.q_ref
  368.9 3.5 text_attention.1.refs_1_
  372.5 3.3 fusion.7
  377.5 17.0 %multiply_convert_fusion.1 = (bf16[512,6144]{1,0:T(8,128)(2,1)S(1)}, f32[512,6144]{1,0:T(8,128)}) fusion(bf16[512,1536]{1,0:T(8,128)(2,1)S(1)} %add_convert_fusion.1.refs_0_, bf16[1536,6144]{1,0:T(8,128)(2,1)} %bitcast.92), kind=kOutput, calls=%fused_computation.3 | convolution fusion | flops 9679405056 | bytes 39321600 | tf_op jit(solution)/shard_map/dot_general | solution.py:31
  394.5 2.6 copy-done.30
  397.1 13.1 %convolution_convert_fusion = bf16[6144,1536]{1,0:T(8,128)(2,1)} fusion(bf16[512,6144]{1,0:T(8,128)(2,1)S(1)} %get-tuple-element.67, bf16[512,1536]{1,0:T(8,128)(2,1)S(1)} %bitcast.76), kind=kOutput, calls=%fused_computation | convolution fusion | flops 9673113600 | bytes 26738688 | tf_op jit(solution)/shard_map/dot_general | solution.py:35
  410.2 18.8 %multiply_convert_fusion.refs_6_ = bf16[512,6144]{1,0:T(8,128)(2,1)} fusion(bf16[512,1536]{1,0:T(8,128)(2,1)S(1)} %bitcast.77, bf16[6144,1536]{1,0:T(8,128)(2,1)} %bitcast.90, f32[512,6144]{1,0:T(8,128)} %get-tuple-element.127), kind=kOutput, calls=%fused_computation.1 | convolution fusion | flops 9701425152 | bytes 39321600 | tf_op jit(solution)/shard_map/dot_general | solution.py:41
  429.1 19.0 %multiply_reduce_fusion.4 = (f32[1536]{0:T(1024)S(1)}, f32[512]{0:T(512)S(1)}, f32[1536]{0:T(1024)S(1)}, f32[512,1536]{1,0:T(8,128)}) fusion(f32[512,1536]{1,0:T(8,128)} %copy-done.10, f32[512]{0:T(512)S(1)} %fusion.3, f32[512]{0:T(512)S(1)} %broadcast_multiply_fusion, f32[1536]{0:T(1024)S(1)} %get-tuple-element.104, ...), kind=kOutput, calls=%fused_computation.13 | convolution fusion | flops 9669963776 | bytes 31481856 | tf_op jit(solution)/shard_map/dot_general | solution.py:41
  448.1 4.2 fusion.6
  454.0 6.3 convolution_convert_fusion.3.grad_ref
  460.3 12.0 %text_attention_back.1 = (bf16[512,1536]{1,0:T(8,128)(2,1)S(1)}, bf16[128,3072]{1,0:T(8,128)(2,1)S(1)}) custom-call(bf16[512,1536]{1,0:T(8,128)(2,1)S(1)} %copy-done.2, bf16[128,3072]{1,0:T(8,128)(2,1)S(1)} %fusion.memory_ref, bf16[512,1536]{1,0:T(8,128)(2,1)S(1)} %convolution_convert_fusion.3.grad_ref), custom_call_target="tpu_custom_call" | custom-call | flops 1006632960 | bytes 6291456 | tf_op jit(solution)/shard_map/text_attention_back/pallas_call | solution.py:986
  472.3 3.1 multiply_reduce_fusion.5
  476.4 2.5 fusion.4
  480.1 3.7 convolution_convert_fusion.2
  487.1 3.6 all-to-all-start
  490.8 17.9 %multiply_reduce_fusion.3 = (f32[]{:T(128)}, f32[]{:T(128)}, bf16[512,1536]{1,0:T(8,128)(2,1)}) fusion(f32[512,1536]{1,0:T(8,128)} %copy-done.10, bf16[512,6144]{1,0:T(8,128)(2,1)} %copy-done.30, bf16[6144,1536]{1,0:T(8,128)(2,1)} %bitcast.91), kind=kOutput, calls=%fused_computation.12 | convolution fusion | flops 9668395008 | bytes 29884424 | tf_op jit(solution)/shard_map/dot_general | solution.py:31
  508.7 2.7 select_maximum_fusion
  515.4 3.5 all-to-all-done.refs_12_
  520.1 313.4 %sum_products.1 = (bf16[192,6144]{1,0:T(8,128)(2,1)}, bf16[192,1536]{1,0:T(8,128)(2,1)}, bf16[192,1536]{1,0:T(8,128)(2,1)}, bf16[192,3072]{1,0:T(8,128)(2,1)}, b...) custom-call(bf16[512,1536]{1,0:T(8,128)(2,1)} %copy-done.15, ...), custom_call_target="tpu_custom_call" | custom-call | tf_op jit(solution)/shard_map/sum_products/pallas_call | solution.py:1636
  836.3 4.5 convert_element_type.105
  848.1 9.7 %all-gather.2.cloned.1.call-done = bf16[768,1536]{1,0:T(8,128)(2,1)} async-done(((bf16[192,1536]{1,0:T(8,128)(2,1)}), bf16[768,1536]{1,0:T(8,128)(2,1)}) %all-gather.2.cloned.1.call-update) | async-done | bytes 2359312 | tf_op jit(solution)/shard_map/all_gather | solution.py:1836
  857.8 4.5 convert_element_type.106
  (135 shorter events, 42.5 us)
Async XLA Ops:
  7.2 826.3 %reduce-scatter.2.cloned.1.call-start = ((), (), s32[]{:S(2)}) async-start(), calls=%async_computation.2 | async-start | bytes 19464192 | tf_op jit(solution)/shard_map/reduce_scatter | solution.py:1774
  16.2 336.0 %copy-start.17 = (bf16[2,256,1536]{2,1,0:T(8,128)(2,1)S(1)}, bf16[2,256,1536]{2,1,0:T(8,128)(2,1)}, u32[]{:S(2)}) copy-start(bf16[2,256,1536]{2,1,0:T(8,128)(2,1)} %param.16) | copy-start | bytes 4718596
  352.1 6.4 copy-start.3
  352.2 6.4 copy-start.9
  358.5 13.9 %copy-start.11 = (f32[512,1536]{1,0:T(8,128)}, f32[512,1536]{1,0:T(8,128)S(1)}, u32[]{:S(2)}) copy-start(f32[512,1536]{1,0:T(8,128)S(1)} %get-tuple-element.116) | copy-start | bytes 9437188
  359.7 5.6 slice-start
  359.7 12.8 %slice-start.7 = ((s8[4718592]{0:T(1024)(128)(4,1)}), s8[4194304]{0:T(1024)(128)(4,1)S(1)}, s32[]{:S(2)}) async-start(s8[4718592]{0:T(1024)(128)(4,1)} %bitcast.103), calls=%async_computation.11 | async-start | bytes 8388608
  360.2 4.9 copy-start.14
  362.6 4.8 slice-start.2
  362.6 4.8 copy-start.21
  362.6 9.9 %slice-start.8 = ((s8[4718592]{0:T(1024)(128)(4,1)}), s8[524288]{0:T(1024)(128)(4,1)S(1)}, s32[]{:S(2)}) async-start(s8[4718592]{0:T(1024)(128)(4,1)} %bitcast.103), calls=%async_computation.12 | async-start | bytes 1048576
  377.5 17.0 %copy-start.15 = (bf16[512,1536]{1,0:T(8,128)(2,1)}, bf16[512,1536]{1,0:T(8,128)(2,1)S(1)}, u32[]{:S(2)}) copy-start(bf16[512,1536]{1,0:T(8,128)(2,1)S(1)} %add_convert_fusion.1.refs_0_) | copy-start | bytes 4718596
  377.5 19.6 %copy-start.19 = (bf16[2,256,1536]{2,1,0:T(8,128)(2,1)S(1)}, bf16[2,256,1536]{2,1,0:T(8,128)(2,1)}, u32[]{:S(2)}) copy-start(bf16[2,256,1536]{2,1,0:T(8,128)(2,1)} %param.31) | copy-start | bytes 4718596
  452.3 20.0 %slice-start.5 = ((s8[4718592]{0:T(1024)(128)(4,1)}), s8[4194304]{0:T(1024)(128)(4,1)S(1)}, s32[]{:S(2)}) async-start(s8[4718592]{0:T(1024)(128)(4,1)} %bitcast.99), calls=%async_computation.9 | async-start | bytes 8388608
  454.0 6.3 copy-start.2
  454.0 18.3 %slice-start.6 = ((s8[4718592]{0:T(1024)(128)(4,1)}), s8[524288]{0:T(1024)(128)(4,1)S(1)}, s32[]{:S(2)}) async-start(s8[4718592]{0:T(1024)(128)(4,1)} %bitcast.99), calls=%async_computation.10 | async-start | bytes 1048576
  460.3 12.0 %copy-start.12 = (f32[512,1536]{1,0:T(8,128)S(1)}, f32[512,1536]{1,0:T(8,128)}, u32[]{:S(2)}) copy-start(f32[512,1536]{1,0:T(8,128)} %copy-done.11) | copy-start | bytes 9437188
  475.5 4.6 slice-start.3
  487.1 31.8 %all-to-all-start = ((bf16[4,512,384]{2,1,0:T(8,128)(2,1)}), bf16[4,512,384]{2,1,0:T(8,128)(2,1)S(1)}, u32[]{:S(2)}, u32[]{:S(2)}) async-start(bf16[4,512,384]{2,1,0:T(8,128)(2,1)} %bitcast.74), calls=%async_computation | async-start | bytes 3145728 | tf_op jit(solution)/shard_map/all_to_all | solution.py:1792
  490.7 20.7 %copy-start.22 = (bf16[2,64,1536]{2,1,0:T(8,128)(2,1)S(1)}, bf16[2,64,1536]{2,1,0:T(8,128)(2,1)}, u32[]{:S(2)}) copy-start(bf16[2,64,1536]{2,1,0:T(8,128)(2,1)} %param.17) | copy-start | bytes 1179652
  490.7 367.1 %all-gather.2.cloned.1.call-start = ((), (), s32[]{:S(2)}) async-start(), calls=%async_computation.3 | async-start | bytes 2949120 | tf_op jit(solution)/shard_map/all_gather | solution.py:1836
  508.7 10.2 %copy-start.28 = (f32[1536]{0:T(1024)S(1)}, f32[1536]{0:T(1024)}, u32[]{:S(2)}) copy-start(f32[1536]{0:T(1024)} %get-tuple-element.102) | copy-start | bytes 18436
  836.3 4.5 copy-start.23
  848.1 14.2 %copy-start.20 = (f32[512,1536]{1,0:T(8,128)S(1)}, f32[512,1536]{1,0:T(8,128)}, u32[]{:S(2)}) copy-start(f32[512,1536]{1,0:T(8,128)} %get-tuple-element.78) | copy-start | bytes 9437188
  (19 other events, 47.0 us)
Sparse Core Ops, SparseCore 0:
  410.4 257.2 reduce-scatter.1
  833.6 24.1 all-gather.1

commit v7 on v6

--- a/solution.py
+++ b/solution.py
@@ -915,7 +915,7 @@
             dma((clips * pairs,)),
         ],
         compiler_params=pltpu.CompilerParams(
-            collective_id=1, has_side_effects=True, vmem_limit_bytes=48 << 20
+            collective_id=1, has_side_effects=True, vmem_limit_bytes=60 << 20
         ),
         name="forward",
     )(*inputs)
@@ -933,7 +933,7 @@
     return lax.dynamic_update_slice(whole, stacked, (0, lax.axis_index("fsdp") * shard))
 
 
-def text_weights(scale, queries, keys):
+def text_weights(queries, keys):
     scores = across(keys, queries)
     raised = jnp.exp(scores - jnp.max(scores, axis=0, keepdims=True))
     return raised / jnp.sum(raised, axis=0, keepdims=True)
@@ -949,28 +949,33 @@
         queries = both_heads((q_ref[:, pair_columns(pair)].astype(F32) * scale).astype(BF16))
         k = memory_ref[:, pair_columns(pair)]
         v = memory_ref[:, pair_columns(pairs + pair)]
-        outs = [down(v, text_weights(scale, part, k).astype(BF16)) for part in queries]
+        outs = [down(v, text_weights(part, k).astype(BF16)) for part in queries]
         out_ref[:, pair_columns(pair)] = join_heads(outs).T.astype(BF16)
+
+
+def head_rows(value):
+    return jnp.concatenate(both_heads(value), 0)
+
+
+def join_rows(value):
+    rows = value.shape[1] // 2
+    return join_heads((value[:, :rows], value[:, rows:])).T
 
 
 def text_attention_back_kernel(scale, q_ref, memory_ref, grad_ref, q_out, memory_out):
     pairs = q_ref.shape[1] // (2 * HD)
     for pair in range(pairs):
-        queries = both_heads((q_ref[:, pair_columns(pair)].astype(F32) * scale).astype(BF16))
-        grads = both_heads(grad_ref[:, pair_columns(pair)])
+        queries = head_rows((q_ref[:, pair_columns(pair)].astype(F32) * scale).astype(BF16))
+        grads = head_rows(grad_ref[:, pair_columns(pair)])
         k = memory_ref[:, pair_columns(pair)]
         v = memory_ref[:, pair_columns(pairs + pair)]
-        query_grads = []
-        key_grad = value_grad = 0.0
-        for head in range(2):
-            weights = text_weights(scale, queries[head], k)
-            weighted = weights * across(v, grads[head])
-            inner = jnp.sum(weighted, axis=0, keepdims=True)
-            change = (weighted - weights * inner).astype(BF16)
-            query_grads.append(down(k, change))
-            key_grad += jnp.dot(change, queries[head], preferred_element_type=F32)
-            value_grad += jnp.dot(weights.astype(BF16), grads[head], preferred_element_type=F32)
-        q_out[:, pair_columns(pair)] = (join_heads(query_grads).T * scale).astype(BF16)
+        weights = text_weights(queries, k)
+        weighted = weights * across(v, grads)
+        inner = jnp.sum(weighted, axis=0, keepdims=True)
+        change = (weighted - weights * inner).astype(BF16)
+        key_grad = jnp.dot(change, queries, preferred_element_type=F32)
+        value_grad = jnp.dot(weights.astype(BF16), grads, preferred_element_type=F32)
+        q_out[:, pair_columns(pair)] = (join_rows(down(k, change)) * scale).astype(BF16)
         memory_out[:, pair_columns(pair)] = key_grad.astype(BF16)
         memory_out[:, pair_columns(pairs + pair)] = value_grad.astype(BF16)
 

time: 879 us -> 877 us (level)
    pallas_call x1, Pallas kernels: 313 us -> 322 us  [sum_products(): pl.pallas_call(functools.partial(sum_kernel, tuple(plan), weights, scale)...]
  transfers between devices with their start and end apart: 3 -> 3, of which waited for: 2 -> 1; matrix products, arithmetic and copies ran while one was open for 12% -> 12% of each run, Pallas kernels for 37% -> 38%
where the time goes in v7:
time: 877 us; the launch traced here: 869 us
  Pallas kernels  671 us (77%)
  matrix products  112 us (13%)
  other arithmetic  30.4 us (3%)
  local copies, waits for them, and re-layouts  27.6 us (3%)
  between operations  14.9 us (2%)
  waiting for transfers between devices  10.3 us (1%)
    pallas_call x1, Pallas kernels, forward(): pl.pallas_call(functools.partial(forward_kernel, plan, weights, scale), o...  337 us
    pallas_call x1, Pallas kernels, sum_products(): pl.pallas_call(functools.partial(sum_kernel, tuple(plan), weights, scale)...  322 us
    dot_general x5, matrix products, product_right(): lax.dot_general(left, right, (((1,), (1,)), ((), ())), preferred_element_...  50.7 us
    dot_general x6, matrix products, product(): return jnp.dot(left, right, preferred_element_type=jnp.float32)  48.1 us
  transfers between devices with their start and end apart: 3, of which 1 were waited for; matrix products, arithmetic and copies ran while one was open for 12% of the time, Pallas kernels for 38%

profile of v7, /device:TPU:0, one launch (start us, length us, event | category | flops | bytes accessed | tf_op | source)
XLA Modules:
  0.0 869.3 jit_solution(10812129501329460602)
XLA Ops:
  12.3 337.0 %forward.1 = (bf16[4,2,1,4,48,4608]{5,4,3,2,1,0:T(8,128)(2,1)}, bf16[4,2,1,4,48,1536]{5,4,3,2,1,0:T(8,128)(2,1)}, bf16[4,2,1,4,48,1536]{5,4,3,2,1,0:T(8,128)(2,1...) custom-call(bf16[1,4,48,4608]{3,2,1,0:T(8,128)(2,1)} %bitcast.79, ...), custom_call_target="tpu_custom_call" | custom-call | tf_op jit(solution)/shard_map/forward/pallas_call | solution.py:886
  349.4 5.8 fusion.8
  359.2 2.6 convolution_convert_fusion.4.q_ref
  365.6 3.5 text_attention.1.refs_1_
  369.1 3.3 fusion.7
  374.1 17.0 %multiply_convert_fusion.1 = (bf16[512,6144]{1,0:T(8,128)(2,1)S(1)}, f32[512,6144]{1,0:T(8,128)}) fusion(bf16[512,1536]{1,0:T(8,128)(2,1)S(1)} %add_convert_fusion.1.refs_0_, bf16[1536,6144]{1,0:T(8,128)(2,1)} %bitcast.92), kind=kOutput, calls=%fused_computation.3 | convolution fusion | flops 9679405056 | bytes 39321600 | tf_op jit(solution)/shard_map/dot_general | solution.py:31
  391.2 2.6 copy-done.26
  393.7 13.1 %convolution_convert_fusion = bf16[6144,1536]{1,0:T(8,128)(2,1)} fusion(bf16[512,6144]{1,0:T(8,128)(2,1)S(1)} %get-tuple-element.67, bf16[512,1536]{1,0:T(8,128)(2,1)S(1)} %bitcast.72), kind=kOutput, calls=%fused_computation | convolution fusion | flops 9673113600 | bytes 26738688 | tf_op jit(solution)/shard_map/dot_general | solution.py:35
  406.9 18.6 %multiply_convert_fusion.refs_6_ = bf16[512,6144]{1,0:T(8,128)(2,1)} fusion(bf16[512,1536]{1,0:T(8,128)(2,1)S(1)} %bitcast.73, bf16[6144,1536]{1,0:T(8,128)(2,1)} %bitcast.90, f32[512,6144]{1,0:T(8,128)} %get-tuple-element.127), kind=kOutput, calls=%fused_computation.1 | convolution fusion | flops 9701425152 | bytes 39321600 | tf_op jit(solution)/shard_map/dot_general | solution.py:41
  425.5 19.1 %multiply_reduce_fusion.4 = (f32[1536]{0:T(1024)S(1)}, f32[512]{0:T(512)S(1)}, f32[1536]{0:T(1024)S(1)}, f32[512,1536]{1,0:T(8,128)}) fusion(f32[512,1536]{1,0:T(8,128)} %copy-done.4, f32[512]{0:T(512)S(1)} %fusion.3, f32[512]{0:T(512)S(1)} %broadcast_multiply_fusion, f32[1536]{0:T(1024)S(1)} %get-tuple-element.104, ...), kind=kOutput, calls=%fused_computation.13 | convolution fusion | flops 9669963776 | bytes 31481856 | tf_op jit(solution)/shard_map/dot_general | solution.py:41
  444.6 4.2 fusion.6
  450.5 6.2 convolution_convert_fusion.3.grad_ref
  456.7 7.7 text_attention_back.1
  464.4 3.1 multiply_reduce_fusion.5
  468.6 2.5 fusion.4
  472.2 3.7 convolution_convert_fusion.2
  479.3 3.6 all-to-all-start
  483.0 17.8 %multiply_reduce_fusion.3 = (f32[]{:T(128)}, f32[]{:T(128)}, bf16[512,1536]{1,0:T(8,128)(2,1)}) fusion(f32[512,1536]{1,0:T(8,128)} %copy-done.4, bf16[512,6144]{1,0:T(8,128)(2,1)} %copy-done.26, bf16[6144,1536]{1,0:T(8,128)(2,1)} %bitcast.91), kind=kOutput, calls=%fused_computation.12 | convolution fusion | flops 9668395008 | bytes 29884424 | tf_op jit(solution)/shard_map/dot_general | solution.py:31
  500.7 2.7 select_maximum_fusion
  508.7 322.3 %sum_products.1 = (bf16[192,6144]{1,0:T(8,128)(2,1)}, bf16[192,1536]{1,0:T(8,128)(2,1)}, bf16[192,1536]{1,0:T(8,128)(2,1)}, bf16[192,3072]{1,0:T(8,128)(2,1)}, b...) custom-call(bf16[512,1536]{1,0:T(8,128)(2,1)} %copy-done.9, ...), custom_call_target="tpu_custom_call" | custom-call | tf_op jit(solution)/shard_map/sum_products/pallas_call | solution.py:1641
  833.9 4.5 convert_element_type.105
  838.4 2.2 convert_element_type.100
  845.7 10.2 %all-gather.2.cloned.1.call-done = bf16[768,1536]{1,0:T(8,128)(2,1)} async-done(((bf16[192,1536]{1,0:T(8,128)(2,1)}), bf16[768,1536]{1,0:T(8,128)(2,1)}) %all-gather.2.cloned.1.call-update) | async-done | bytes 2359312 | tf_op jit(solution)/shard_map/all_gather | solution.py:1841
  855.9 4.5 convert_element_type.106
  (127 shorter events, 36.6 us)
Async XLA Ops:
  7.2 823.8 %reduce-scatter.2.cloned.1.call-start = ((), (), s32[]{:S(2)}) async-start(), calls=%async_computation.2 | async-start | bytes 19464192 | tf_op jit(solution)/shard_map/reduce_scatter | solution.py:1779
  12.3 337.0 %copy-start.11 = (bf16[2,256,1536]{2,1,0:T(8,128)(2,1)S(1)}, bf16[2,256,1536]{2,1,0:T(8,128)(2,1)}, u32[]{:S(2)}) copy-start(bf16[2,256,1536]{2,1,0:T(8,128)(2,1)} %param.16) | copy-start | bytes 4718596
  355.2 13.9 %copy-start.5 = (f32[512,1536]{1,0:T(8,128)}, f32[512,1536]{1,0:T(8,128)S(1)}, u32[]{:S(2)}) copy-start(f32[512,1536]{1,0:T(8,128)S(1)} %get-tuple-element.116) | copy-start | bytes 9437188
  356.7 5.2 slice-start
  356.7 12.4 %slice-start.7 = ((s8[4718592]{0:T(1024)(128)(4,1)}), s8[4194304]{0:T(1024)(128)(4,1)S(1)}, s32[]{:S(2)}) async-start(s8[4718592]{0:T(1024)(128)(4,1)} %bitcast.103), calls=%async_computation.11 | async-start | bytes 8388608
  357.2 4.6 copy-start.8
  359.2 4.3 slice-start.1
  359.2 4.8 slice-start.2
  359.2 4.8 copy-start.15
  359.2 9.9 %slice-start.8 = ((s8[4718592]{0:T(1024)(128)(4,1)}), s8[524288]{0:T(1024)(128)(4,1)S(1)}, s32[]{:S(2)}) async-start(s8[4718592]{0:T(1024)(128)(4,1)} %bitcast.103), calls=%async_computation.12 | async-start | bytes 1048576
  374.1 17.0 %copy-start.9 = (bf16[512,1536]{1,0:T(8,128)(2,1)}, bf16[512,1536]{1,0:T(8,128)(2,1)S(1)}, u32[]{:S(2)}) copy-start(bf16[512,1536]{1,0:T(8,128)(2,1)S(1)} %add_convert_fusion.1.refs_0_) | copy-start | bytes 4718596
  374.1 19.6 %copy-start.13 = (bf16[2,256,1536]{2,1,0:T(8,128)(2,1)S(1)}, bf16[2,256,1536]{2,1,0:T(8,128)(2,1)}, u32[]{:S(2)}) copy-start(bf16[2,256,1536]{2,1,0:T(8,128)(2,1)} %param.31) | copy-start | bytes 4718596
  448.8 15.6 %slice-start.5 = ((s8[4718592]{0:T(1024)(128)(4,1)}), s8[4194304]{0:T(1024)(128)(4,1)S(1)}, s32[]{:S(2)}) async-start(s8[4718592]{0:T(1024)(128)(4,1)} %bitcast.99), calls=%async_computation.9 | async-start | bytes 8388608
  450.5 6.2 copy-start.2
  450.5 13.9 %slice-start.6 = ((s8[4718592]{0:T(1024)(128)(4,1)}), s8[524288]{0:T(1024)(128)(4,1)S(1)}, s32[]{:S(2)}) async-start(s8[4718592]{0:T(1024)(128)(4,1)} %bitcast.99), calls=%async_computation.10 | async-start | bytes 1048576
  456.7 7.8 copy-start.6
  467.6 4.6 slice-start.3
  479.3 28.2 %all-to-all-start = ((bf16[4,512,384]{2,1,0:T(8,128)(2,1)}), bf16[4,512,384]{2,1,0:T(8,128)(2,1)S(1)}, u32[]{:S(2)}, u32[]{:S(2)}) async-start(bf16[4,512,384]{2,1,0:T(8,128)(2,1)} %bitcast.70), calls=%async_computation | async-start | bytes 3145728 | tf_op jit(solution)/shard_map/all_to_all | solution.py:1797
  482.9 20.6 %copy-start.16 = (bf16[2,64,1536]{2,1,0:T(8,128)(2,1)S(1)}, bf16[2,64,1536]{2,1,0:T(8,128)(2,1)}, u32[]{:S(2)}) copy-start(bf16[2,64,1536]{2,1,0:T(8,128)(2,1)} %param.17) | copy-start | bytes 1179652
  482.9 373.0 %all-gather.2.cloned.1.call-start = ((), (), s32[]{:S(2)}) async-start(), calls=%async_computation.3 | async-start | bytes 2949120 | tf_op jit(solution)/shard_map/all_gather | solution.py:1841
  500.7 6.7 copy-start.23
  833.9 4.5 copy-start.17
  840.6 4.0 copy-start.19
  845.7 14.7 %copy-start.14 = (f32[512,1536]{1,0:T(8,128)S(1)}, f32[512,1536]{1,0:T(8,128)}, u32[]{:S(2)}) copy-start(f32[512,1536]{1,0:T(8,128)} %get-tuple-element.78) | copy-start | bytes 9437188
  (15 other events, 35.5 us)
Sparse Core Ops, SparseCore 0:
  407.0 266.2 reduce-scatter.1
  831.2 24.6 all-gather.1

commit v8 on v7

--- a/solution.py
+++ b/solution.py
@@ -856,7 +856,7 @@
             width = 384 if weight == 0 or last else 768
             places += [(weight, block, column, width) for column in range(0, columns, width)]
     return tuple(
-        place + ((len(places) - 1 - i) * 3 % 5 >= 2,) for i, place in enumerate(places)
+        place + ((len(places) - 1 - i) * 2 % 5 >= 2,) for i, place in enumerate(places)
     )
 
 

time: 877 us -> 872 us (level)
  Pallas kernels: 671 us -> 662 us
  transfers between devices with their start and end apart: 3 -> 3, of which waited for: 1 -> 2; matrix products, arithmetic and copies ran while one was open for 12% -> 12% of each run, Pallas kernels for 38% -> 37%
where the time goes in v8:
time: 872 us; the launch traced here: 864 us
  Pallas kernels  662 us (76%)
  matrix products  113 us (13%)
  other arithmetic  30.4 us (3%)
  local copies, waits for them, and re-layouts  27.5 us (3%)
  between operations  14.9 us (2%)
  waiting for transfers between devices  12.9 us (1%)
    pallas_call x1, Pallas kernels, forward(): pl.pallas_call(functools.partial(forward_kernel, plan, weights, scale), o...  336 us
    pallas_call x1, Pallas kernels, sum_products(): pl.pallas_call(functools.partial(sum_kernel, tuple(plan), weights, scale)...  314 us
    dot_general x5, matrix products, product_right(): lax.dot_general(left, right, (((1,), (1,)), ((), ())), preferred_element_...  51.8 us
    dot_general x6, matrix products, product(): return jnp.dot(left, right, preferred_element_type=jnp.float32)  48.2 us
  transfers between devices with their start and end apart: 3, of which 2 were waited for; matrix products, arithmetic and copies ran while one was open for 12% of the time, Pallas kernels for 37%

profile of v8, /device:TPU:0, one launch (start us, length us, event | category | flops | bytes accessed | tf_op | source)
XLA Modules:
  0.0 864.5 jit_solution(9332414161439261026)
XLA Ops:
  12.3 336.3 %forward.1 = (bf16[4,2,1,4,48,4608]{5,4,3,2,1,0:T(8,128)(2,1)}, bf16[4,2,1,4,48,1536]{5,4,3,2,1,0:T(8,128)(2,1)}, bf16[4,2,1,4,48,1536]{5,4,3,2,1,0:T(8,128)(2,1...) custom-call(bf16[1,4,48,4608]{3,2,1,0:T(8,128)(2,1)} %bitcast.79, ...), custom_call_target="tpu_custom_call" | custom-call | tf_op jit(solution)/shard_map/forward/pallas_call | solution.py:886
  348.7 5.8 fusion.8
  358.5 2.6 convolution_convert_fusion.4.q_ref
  364.8 3.5 text_attention.1.refs_1_
  368.4 3.3 fusion.7
  373.4 17.0 %multiply_convert_fusion.1 = (bf16[512,6144]{1,0:T(8,128)(2,1)S(1)}, f32[512,6144]{1,0:T(8,128)}) fusion(bf16[512,1536]{1,0:T(8,128)(2,1)S(1)} %add_convert_fusion.1.refs_0_, bf16[1536,6144]{1,0:T(8,128)(2,1)} %bitcast.92), kind=kOutput, calls=%fused_computation.3 | convolution fusion | flops 9679405056 | bytes 39321600 | tf_op jit(solution)/shard_map/dot_general | solution.py:31
  390.4 2.6 copy-done.26
  393.0 13.1 %convolution_convert_fusion = bf16[6144,1536]{1,0:T(8,128)(2,1)} fusion(bf16[512,6144]{1,0:T(8,128)(2,1)S(1)} %get-tuple-element.67, bf16[512,1536]{1,0:T(8,128)(2,1)S(1)} %bitcast.72), kind=kOutput, calls=%fused_computation | convolution fusion | flops 9673113600 | bytes 26738688 | tf_op jit(solution)/shard_map/dot_general | solution.py:35
  406.2 19.6 %multiply_convert_fusion.refs_6_ = bf16[512,6144]{1,0:T(8,128)(2,1)} fusion(bf16[512,1536]{1,0:T(8,128)(2,1)S(1)} %bitcast.73, bf16[6144,1536]{1,0:T(8,128)(2,1)} %bitcast.90, f32[512,6144]{1,0:T(8,128)} %get-tuple-element.127), kind=kOutput, calls=%fused_computation.1 | convolution fusion | flops 9701425152 | bytes 39321600 | tf_op jit(solution)/shard_map/dot_general | solution.py:41
  425.8 19.1 %multiply_reduce_fusion.4 = (f32[1536]{0:T(1024)S(1)}, f32[512]{0:T(512)S(1)}, f32[1536]{0:T(1024)S(1)}, f32[512,1536]{1,0:T(8,128)}) fusion(f32[512,1536]{1,0:T(8,128)} %copy-done.4, f32[512]{0:T(512)S(1)} %fusion.3, f32[512]{0:T(512)S(1)} %broadcast_multiply_fusion, f32[1536]{0:T(1024)S(1)} %get-tuple-element.104, ...), kind=kOutput, calls=%fused_computation.13 | convolution fusion | flops 9669963776 | bytes 31481856 | tf_op jit(solution)/shard_map/dot_general | solution.py:41
  444.9 4.2 fusion.6
  450.8 6.3 convolution_convert_fusion.3.grad_ref
  457.0 7.7 text_attention_back.1
  464.8 3.1 multiply_reduce_fusion.5
  468.9 2.5 fusion.4
  472.5 3.7 convolution_convert_fusion.2
  479.6 3.6 all-to-all-start
  483.2 17.9 %multiply_reduce_fusion.3 = (f32[]{:T(128)}, f32[]{:T(128)}, bf16[512,1536]{1,0:T(8,128)(2,1)}) fusion(f32[512,1536]{1,0:T(8,128)} %copy-done.4, bf16[512,6144]{1,0:T(8,128)(2,1)} %copy-done.26, bf16[6144,1536]{1,0:T(8,128)(2,1)} %bitcast.91), kind=kOutput, calls=%fused_computation.12 | convolution fusion | flops 9668395008 | bytes 29884424 | tf_op jit(solution)/shard_map/dot_general | solution.py:31
  501.1 2.7 select_maximum_fusion
  507.8 2.3 all-to-all-done.refs_12_
  511.3 314.5 %sum_products.1 = (bf16[192,6144]{1,0:T(8,128)(2,1)}, bf16[192,1536]{1,0:T(8,128)(2,1)}, bf16[192,1536]{1,0:T(8,128)(2,1)}, bf16[192,3072]{1,0:T(8,128)(2,1)}, b...) custom-call(bf16[512,1536]{1,0:T(8,128)(2,1)} %copy-done.9, ...), custom_call_target="tpu_custom_call" | custom-call | tf_op jit(solution)/shard_map/sum_products/pallas_call | solution.py:1641
  828.6 4.5 convert_element_type.105
  840.5 10.6 %all-gather.2.cloned.1.call-done = bf16[768,1536]{1,0:T(8,128)(2,1)} async-done(((bf16[192,1536]{1,0:T(8,128)(2,1)}), bf16[768,1536]{1,0:T(8,128)(2,1)}) %all-gather.2.cloned.1.call-update) | async-done | bytes 2359312 | tf_op jit(solution)/shard_map/all_gather | solution.py:1841
  851.0 4.5 convert_element_type.106
  (127 shorter events, 38.6 us)
Async XLA Ops:
  7.2 818.6 %reduce-scatter.2.cloned.1.call-start = ((), (), s32[]{:S(2)}) async-start(), calls=%async_computation.2 | async-start | bytes 19464192 | tf_op jit(solution)/shard_map/reduce_scatter | solution.py:1779
  12.3 336.3 %copy-start.11 = (bf16[2,256,1536]{2,1,0:T(8,128)(2,1)S(1)}, bf16[2,256,1536]{2,1,0:T(8,128)(2,1)}, u32[]{:S(2)}) copy-start(bf16[2,256,1536]{2,1,0:T(8,128)(2,1)} %param.16) | copy-start | bytes 4718596
  354.5 13.9 %copy-start.5 = (f32[512,1536]{1,0:T(8,128)}, f32[512,1536]{1,0:T(8,128)S(1)}, u32[]{:S(2)}) copy-start(f32[512,1536]{1,0:T(8,128)S(1)} %get-tuple-element.116) | copy-start | bytes 9437188
  355.9 5.2 slice-start
  355.9 12.4 %slice-start.7 = ((s8[4718592]{0:T(1024)(128)(4,1)}), s8[4194304]{0:T(1024)(128)(4,1)S(1)}, s32[]{:S(2)}) async-start(s8[4718592]{0:T(1024)(128)(4,1)} %bitcast.103), calls=%async_computation.11 | async-start | bytes 8388608
  356.5 4.6 copy-start.8
  358.5 4.3 slice-start.1
  358.5 4.8 slice-start.2
  358.5 4.8 copy-start.15
  358.5 9.9 %slice-start.8 = ((s8[4718592]{0:T(1024)(128)(4,1)}), s8[524288]{0:T(1024)(128)(4,1)S(1)}, s32[]{:S(2)}) async-start(s8[4718592]{0:T(1024)(128)(4,1)} %bitcast.103), calls=%async_computation.12 | async-start | bytes 1048576
  373.4 17.0 %copy-start.9 = (bf16[512,1536]{1,0:T(8,128)(2,1)}, bf16[512,1536]{1,0:T(8,128)(2,1)S(1)}, u32[]{:S(2)}) copy-start(bf16[512,1536]{1,0:T(8,128)(2,1)S(1)} %add_convert_fusion.1.refs_0_) | copy-start | bytes 4718596
  373.4 19.6 %copy-start.13 = (bf16[2,256,1536]{2,1,0:T(8,128)(2,1)S(1)}, bf16[2,256,1536]{2,1,0:T(8,128)(2,1)}, u32[]{:S(2)}) copy-start(bf16[2,256,1536]{2,1,0:T(8,128)(2,1)} %param.31) | copy-start | bytes 4718596
  449.1 15.7 %slice-start.5 = ((s8[4718592]{0:T(1024)(128)(4,1)}), s8[4194304]{0:T(1024)(128)(4,1)S(1)}, s32[]{:S(2)}) async-start(s8[4718592]{0:T(1024)(128)(4,1)} %bitcast.99), calls=%async_computation.9 | async-start | bytes 8388608
  450.8 6.3 copy-start.2
  450.8 14.0 %slice-start.6 = ((s8[4718592]{0:T(1024)(128)(4,1)}), s8[524288]{0:T(1024)(128)(4,1)S(1)}, s32[]{:S(2)}) async-start(s8[4718592]{0:T(1024)(128)(4,1)} %bitcast.99), calls=%async_computation.10 | async-start | bytes 1048576
  457.0 7.7 copy-start.6
  467.9 4.6 slice-start.3
  479.6 30.6 %all-to-all-start = ((bf16[4,512,384]{2,1,0:T(8,128)(2,1)}), bf16[4,512,384]{2,1,0:T(8,128)(2,1)S(1)}, u32[]{:S(2)}, u32[]{:S(2)}) async-start(bf16[4,512,384]{2,1,0:T(8,128)(2,1)} %bitcast.70), calls=%async_computation | async-start | bytes 3145728 | tf_op jit(solution)/shard_map/all_to_all | solution.py:1797
  483.1 20.7 %copy-start.16 = (bf16[2,64,1536]{2,1,0:T(8,128)(2,1)S(1)}, bf16[2,64,1536]{2,1,0:T(8,128)(2,1)}, u32[]{:S(2)}) copy-start(bf16[2,64,1536]{2,1,0:T(8,128)(2,1)} %param.17) | copy-start | bytes 1179652
  483.1 367.9 %all-gather.2.cloned.1.call-start = ((), (), s32[]{:S(2)}) async-start(), calls=%async_computation.3 | async-start | bytes 2949120 | tf_op jit(solution)/shard_map/all_gather | solution.py:1841
  501.1 9.1 %copy-start.23 = (f32[1536]{0:T(1024)S(1)}, f32[1536]{0:T(1024)}, u32[]{:S(2)}) copy-start(f32[1536]{0:T(1024)} %get-tuple-element.102) | copy-start | bytes 18436
  828.6 4.5 copy-start.17
  835.4 4.0 copy-start.19
  840.5 15.1 %copy-start.14 = (f32[512,1536]{1,0:T(8,128)S(1)}, f32[512,1536]{1,0:T(8,128)}, u32[]{:S(2)}) copy-start(f32[512,1536]{1,0:T(8,128)} %get-tuple-element.78) | copy-start | bytes 9437188
  (15 other events, 35.6 us)
Sparse Core Ops, SparseCore 0:
  406.3 260.7 reduce-scatter.1
  825.9 25.0 all-gather.1
